TPU v7x, 256 devices: a whole 4x4x8 slice. The times are simulated.
256 devices in a mesh: row: 16 (over y_hi, x, core), col: 16 (over z, y_lo).
Axes of the slice: x: 4, y: 4 (y_hi: 2, y_lo: 2; y = y_hi * 2 + y_lo), z: 8, core: 2. Of those that a mesh axis runs over, the one named last changes fastest.
Arguments:
- slab: bfloat16 [2, 640, 640, 640], P(None, 'col', 'row'), may hold values from -6 to 6
- coef_virtual: bfloat16 [640, 576], replicated, may hold values from -0.25 to 0.25
- coef_occupied: bfloat16 [640, 64], replicated, may hold values from -0.25 to 0.25
- occ_level: int32 [64], replicated, may hold values from -160 to -16
- virt_level: int32 [576], replicated, may hold values from 16 to 192
- orbital_index: int32 [2], replicated, may hold values from 0 to 63
Outputs:
- back_slab: bfloat16 [2, 640, 640, 640], P(None, 'col', 'row')
All inputs are finite; a program needn't handle non-finite values.
Results may differ from a plain program's by a relative error of at most 0.008.
Values may be sent and summed in bfloat16 or wider, within the bound.
No kernel may reach another device: no remote copies, remote signals or barrier semaphores. Data moves between devices by JAX's collectives and lax.ppermute only.
A program may use at most 64 MiB of HBM per device.

v0:
```python
import jax
import jax.numpy as jnp
from jax import lax
from jax.experimental import pallas as pl
from jax.experimental.pallas import tpu as pltpu
from jax.sharding import Mesh, PartitionSpec as P


NB = 640
NO = 64
NV = 576
NROW = 16
NZ = 8
TILE = 8
JB = NO // NZ
LB = NB // 16
MB = NB // NROW
HALF = NV // 2
RW = NO * TILE
CL = LB * TILE
BF = jnp.bfloat16
F32 = jnp.float32
SWAP = [(0, 1), (1, 0)]
YT, ZT = 3, 2
YM, ZM = YT * TILE, ZT * TILE


def dot(a, b):
    return lax.dot_general(a, b, (((1,), (0,)), ((), ())), preferred_element_type=F32)


def call(body, grid, in_specs, out_specs, out_shape, args, scalars=None, aliases=None, flops=0):
    nbytes = sum(a.size * a.dtype.itemsize for a in args) // 2
    spec = pltpu.PrefetchScalarGridSpec(
        num_scalar_prefetch=0 if scalars is None else 1,
        grid=grid,
        in_specs=in_specs,
        out_specs=out_specs,
    )
    lead = () if scalars is None else (scalars,)
    return pl.pallas_call(
        body,
        grid_spec=spec,
        out_shape=out_shape,
        input_output_aliases=aliases or {},
        cost_estimate=pl.CostEstimate(flops=flops, bytes_accessed=nbytes, transcendentals=0),
        compiler_params=pltpu.CompilerParams(vmem_limit_bytes=24 * 1024 * 1024),
    )(*lead, *args)


def spread(coef_t, base, zi):
    lam = lax.broadcasted_iota(jnp.int32, (NB, CL), 0)
    col = lax.broadcasted_iota(jnp.int32, (NB, CL), 1)
    pick = (lam == base + col // TILE).astype(BF)
    wide = dot(coef_t, pick).astype(BF)
    row = lax.broadcasted_iota(jnp.int32, (RW, NO), 0)
    occ = lax.broadcasted_iota(jnp.int32, (RW, NO), 1)
    block = row // TILE
    want = ((zi + block // JB) % NZ) * JB + block % JB
    tall = dot((occ == want).astype(BF), wide)
    row = lax.broadcasted_iota(jnp.int32, (RW, CL), 0)
    col = lax.broadcasted_iota(jnp.int32, (RW, CL), 1)
    return jnp.where(row % TILE == col % TILE, tall, 0.0).astype(BF)


def fold(x):
    return x.astype(F32).reshape(x.shape[0] * x.shape[1], x.shape[2]).astype(BF)


def whole(shape):
    return pl.BlockSpec(shape, lambda *_: (0,) * len(shape))


def lift(slab, pick):
    step = 8

    def body(_, src, dst):
        dst[...] = src[0]

    return call(
        body,
        (LB // step,),
        [pl.BlockSpec((1, step, YM, NB), lambda i, s: (s[1], i, 0, 0))],
        pl.BlockSpec((step, YM, NB), lambda i, s: (i, 0, 0)),
        jax.ShapeDtypeStruct((LB, YM, NB), BF),
        (slab,),
        pick,
    )


def y_parts(slab, swapped, k_mine, k_other, pick, first, tiles):
    def body(_, here, came, km, ko, *outs):
        part = dot(km[...], fold(here[0])) + dot(ko[...], fold(came[...]))
        part = part.reshape(NZ, JB, TILE, NB)
        for k in range(NZ):
            outs[k][...] = part[k].astype(BF)

    return call(
        body,
        (tiles,),
        [
            pl.BlockSpec((1, LB, TILE, NB), lambda t, s: (s[0], 0, first + t, 0)),
            pl.BlockSpec((LB, TILE, NB), lambda t, s: (0, t, 0)),
            whole((RW, CL)),
            whole((RW, CL)),
        ],
        [pl.BlockSpec((JB, TILE, NB), lambda t, s: (0, t, 0))] * NZ,
        [jax.ShapeDtypeStruct((JB, tiles * TILE, NB), BF)] * NZ,
        (slab, swapped, k_mine, k_other),
        pick,
        flops=4 * tiles * RW * CL * NB,
    )


def z_parts(slab, k_mine, pick, first, tiles):
    def body(_, here, km, *outs):
        part = dot(km[...], fold(here[0])).reshape(NZ, JB, TILE, NB)
        for k in range(NZ):
            outs[k][0] = part[k].astype(BF)

    return call(
        body,
        (2, tiles),
        [
            pl.BlockSpec((1, LB, TILE, NB), lambda o, t, s: (s[o], 0, first + t, 0)),
            whole((RW, CL)),
        ],
        [pl.BlockSpec((1, JB, TILE, NB), lambda o, t, s: (o, 0, t, 0))] * NZ,
        [pltpu.HBM((2, JB, tiles * TILE, NB), BF)] * NZ,
        (slab, k_mine),
        pick,
        flops=4 * tiles * RW * CL * NB,
    )


def gathered(slots):
    return jnp.concatenate([fold(s) for s in slots], axis=0)


def y_expand(slots, kt_mine, kt_other, pick, first, tiles):
    def body(_, *refs):
        slot_refs, (km, ko, send, kept) = refs[:NZ], refs[NZ:]
        stack = gathered([s[...] for s in slot_refs])
        send[...] = dot(ko[...], stack).reshape(LB, TILE, NB).astype(BF)
        kept[0] = dot(km[...], stack).reshape(LB, TILE, NB).astype(BF)

    return call(
        body,
        (tiles,),
        [pl.BlockSpec((JB, TILE, NB), lambda t, s: (0, t, 0))] * NZ
        + [whole((CL, RW)), whole((CL, RW))],
        [
            pl.BlockSpec((LB, TILE, NB), lambda t, s: (0, t, 0)),
            pl.BlockSpec((1, LB, TILE, NB), lambda t, s: (s[0], 0, first + t, 0)),
        ],
        [
            jax.ShapeDtypeStruct((LB, tiles * TILE, NB), BF),
            jax.ShapeDtypeStruct((2, LB, MB, NB), BF),
        ],
        (*slots, kt_mine, kt_other),
        pick,
        flops=4 * tiles * RW * CL * NB,
    )


def z_expand(slots, kt_mine, out, pick, first, tiles):
    def body(_, *refs):
        slot_refs, km, kept = refs[:NZ], refs[NZ], refs[NZ + 2]
        stack = gathered([s[0] for s in slot_refs])
        kept[0] = dot(km[...], stack).reshape(LB, TILE, NB).astype(BF)

    return call(
        body,
        (2, tiles),
        [pl.BlockSpec((1, JB, TILE, NB), lambda o, t, s: (o, 0, t, 0))] * NZ
        + [whole((CL, RW)), pl.BlockSpec(memory_space=pl.ANY)],
        pl.BlockSpec((1, LB, TILE, NB), lambda o, t, s: (s[o], 0, first + t, 0)),
        jax.ShapeDtypeStruct((2, LB, MB, NB), BF),
        (*slots, kt_mine, out),
        pick,
        {NZ + 2: 0},
        flops=4 * tiles * RW * CL * NB,
    )


def put(got, out, pick, first, tiles):
    def body(_, src, __, dst):
        dst[0] = src[...]

    return call(
        body,
        (tiles,),
        [
            pl.BlockSpec((LB, TILE, NB), lambda t, s: (0, t, 0)),
            pl.BlockSpec(memory_space=pl.ANY),
        ],
        pl.BlockSpec((1, LB, TILE, NB), lambda t, s: (s[1], 0, first + t, 0)),
        jax.ShapeDtypeStruct((2, LB, MB, NB), BF),
        (got, out),
        pick,
        {2: 0},
    )


def to_virtual(summed, v_halves):
    def body(s, v, out):
        flat = s[...].astype(F32).reshape(JB * MB, NB).astype(BF)
        out[...] = dot(flat, v[0]).reshape(JB, MB, HALF).astype(BF)

    return call(
        body,
        (2,),
        [whole((JB, MB, NB)), pl.BlockSpec((1, NB, HALF), lambda h: (h, 0, 0))],
        pl.BlockSpec((JB, MB, HALF), lambda h: (h, 0, 0)),
        jax.ShapeDtypeStruct((NROW, MB, HALF), BF),
        (summed, v_halves),
        flops=2 * JB * MB * NB * NV,
    )


def divide(second, coef, coef_t, column, row):
    def body(x, v, vt, c, r, out):
        third = dot(vt[...], x[...])
        amplitude = (third / (c[...] + r[...])).astype(BF)
        out[...] = dot(v[...], amplitude).astype(BF)

    return call(
        body,
        (1,),
        [whole((NB, HALF)), whole((NB, NV)), whole((NV, NB)), whole((NV, 1)), whole((1, HALF))],
        whole((NB, HALF)),
        jax.ShapeDtypeStruct((NB, HALF), BF),
        (second, coef, coef_t, column, row),
        flops=4 * NB * HALF * NV,
    )


def to_basis(back, vt_halves, sizes):
    def body(x, v, *outs):
        flat = [
            x[h * JB : (h + 1) * JB].astype(F32).reshape(JB * MB, HALF).astype(BF) for h in range(2)
        ]
        wide = (dot(flat[0], v[0]) + dot(flat[1], v[1])).reshape(JB, MB, NB)
        lo = 0
        for out, size in zip(outs, sizes):
            out[...] = wide[:, lo : lo + size].astype(BF)
            lo += size

    return call(
        body,
        (1,),
        [whole((NROW, MB, HALF)), whole((2, HALF, NB))],
        [whole((JB, size, NB)) for size in sizes],
        [jax.ShapeDtypeStruct((JB, size, NB), BF) for size in sizes],
        (back, vt_halves),
        flops=2 * JB * MB * NB * NV,
    )


def add(*terms):
    total = terms[0].astype(F32)
    for term in terms[1:]:
        total = total + term.astype(F32)
    return total.astype(BF)


def move(x, step):
    return lax.ppermute(x, "z", [(i, (i + step) % NZ) for i in range(NZ)])


def swap(x):
    return lax.ppermute(x, "ylo", SWAP)


def reduce_z(parts, way):
    hop = [parts[3], parts[NZ - 3]]
    far = move(parts[4], 2 * way)
    for k in (2, 1, 0):
        hop = [move(hop[0], 1), move(hop[1], -1)]
        if k:
            terms = [[hop[0], parts[k]], [hop[1], parts[NZ - k]]]
            if k == 2:
                terms[0 if way > 0 else 1].append(far)
            hop = [add(*t) for t in terms]
    return add(parts[0], *hop)


def gather_z(own, way):
    slots = [own] + [None] * (NZ - 1)
    hop = [own, own]
    for k in (1, 2, 3):
        if k == 3:
            slots[4] = move(hop[0 if way > 0 else 1], 2 * way)
        hop = [move(hop[0], 1), move(hop[1], -1)]
        slots[NZ - k], slots[k] = hop
    return slots


def run(slab, coef_virtual, coef_occupied, occ_level, virt_level, orbital_index):
    zi = lax.axis_index("z")
    yi = lax.axis_index("ylo")
    ri = lax.axis_index("row")
    slab = pltpu.with_memory_space_constraint(slab, pltpu.HBM)
    pick = jnp.stack([yi, 1 - yi]).astype(jnp.int32)
    eo = occ_level.astype(F32) / 64.0
    ev = virt_level.astype(F32) / 64.0
    occs = jnp.arange(NO, dtype=jnp.int32)
    chosen = jnp.sum(jnp.where(jnp.arange(2) == yi, orbital_index, 0))
    energy_i = jnp.sum(jnp.where(occs == chosen, eo, 0.0))
    energy_j = jnp.sum(jnp.where(occs == zi * JB + ri % JB, eo, 0.0))
    row = (jnp.where(ri // JB == 0, ev[:HALF], ev[HALF:]) - energy_i - energy_j)[None, :]
    column = ev[:, None]
    coef_t = coef_virtual.T
    v_halves = jnp.stack([coef_virtual[:, :HALF], coef_virtual[:, HALF:]])
    vt_halves = coef_t.reshape(2, HALF, NB)

    k_mine = spread(coef_occupied.T, zi * 2 * LB + yi * LB, zi)
    k_other = spread(coef_occupied.T, zi * 2 * LB + (1 - yi) * LB, zi)

    raised, held = lax.optimization_barrier((lift(slab, pick), k_mine))
    swapped = swap(raised)
    both = reduce_z(z_parts(slab, held, pick, YT, ZT), -1)
    last = add(both[0], swap(both[1]))
    lead = reduce_z(y_parts(slab, swapped, k_mine, k_other, pick, 0, YT), 1)
    summed = jnp.concatenate([lead, last], axis=1)

    first = to_virtual(summed, v_halves)
    second = lax.all_to_all(first, "row", 0, 0, tiled=True).reshape(NB, HALF)
    back_one = divide(second, coef_virtual, coef_t, column, row)
    back = lax.all_to_all(back_one.reshape(NROW, MB, HALF), "row", 0, 0, tiled=True)
    wide_y, wide_z = to_basis(back, vt_halves, (YM, ZM))

    kt_mine, kt_other = k_mine.T, k_other.T
    slots = gather_z(wide_y, 1)
    send, out = y_expand(slots, kt_mine, kt_other, pick, 0, YT)
    got = swap(send)
    both = jnp.stack([wide_z, swap(wide_z)])
    out = z_expand(gather_z(both, -1), kt_mine, out, pick, YT, ZT)
    return put(got, out, pick, 0, YT)


def solution(mesh):
    fine = Mesh(mesh.devices.reshape(NROW, NZ, 2), ("row", "z", "ylo"))
    slab = P(None, ("z", "ylo"), "row", None)
    return jax.shard_map(
        run, mesh=fine, in_specs=(slab, P(), P(), P(), P(), P()), out_specs=slab, check_vma=False
    )
```

profile of v0, /device:TPU:2, one launch (start us, length us, event | category | flops | bytes accessed | tf_op | source)
XLA Modules:
  0.0 213.0 jit_solution(15097984455750097289)
XLA Ops:
  3.4 4.5 %shard_map.64 = bf16[40,24,640]{2,1,0:T(8,128)(2,1)} custom-call(s32[2]{0:T(128)S(1)} %pad_add_fusion._, bf16[2,40,40,640]{3,2,1,0:T(8,128)(2,1)} %here.3), custom_call_target="tpu_custom_call" | custom-call | bytes 2048000 | tf_op jit(solution)/shard_map/pallas_call | solution.py:41
  7.9 5.3 %shard_map.66 = (bf16[2,8,16,640]{3,2,1,0:T(8,128)(2,1)}, bf16[2,8,16,640]{3,2,1,0:T(8,128)(2,1)}, bf16[2,8,16,640]{3,2,1,0:T(8,128)(2,1)}, bf16[2,8,16,640]{3,2...) custom-call(s32[2]{0:T(128)S(1)} %pad_add_fusion._, ...), custom_call_target="tpu_custom_call" | custom-call | flops 838860800 | bytes 2211840 | tf_op jit(solution)/shard_map/pallas_call | solution.py:41
  15.2 4.0 %collective-permute-start.11 = (bf16[2,8,16,640]{3,2,1,0:T(8,128)(2,1)}, bf16[2,8,16,640]{3,2,1,0:T(8,128)(2,1)S(1)}, u32[]{:S(2)}, u32[]{:S(2)}) collective-permute-start(bf16[2,8,16,640]{3,2,1,0:T(8,128)(2,1)} %get-tuple-element.41), channel_id=1, source_target_pairs={{0,14},{2,0},{4,2},{6,4},{8,6},{10,8},{12,10},{14,12},{1,15},{3,1}... | collective-permute-start | bytes 983048 | tf_op jit(solution)/shard_map/ppermute | solution.py:268
  23.6 3.6 %collective-permute-done.8 = bf16[2,8,16,640]{3,2,1,0:T(8,128)(2,1)} collective-permute-done((bf16[2,8,16,640]{3,2,1,0:T(8,128)(2,1)}, bf16[2,8,16,640]{3,2,1,0:T(8,128)(2,1)}, u32[]{:S(2)}, u32[]{:S(2)}) %collective-permute-start.8) | collective-permute-done | bytes 327712 | tf_op jit(solution)/shard_map/ppermute | solution.py:268
  28.4 4.8 %collective-permute-done.11 = bf16[2,8,16,640]{3,2,1,0:T(8,128)(2,1)S(1)} collective-permute-done((bf16[2,8,16,640]{3,2,1,0:T(8,128)(2,1)}, bf16[2,8,16,640]{3,2,1,0:T(8,128)(2,1)S(1)}, u32[]{:S(2)}, u32[]{:S(2)}) %collective-permute-start.11) | collective-permute-done | bytes 327712 | tf_op jit(solution)/shard_map/ppermute | solution.py:268
  33.2 7.4 %collective-permute-done.12 = bf16[2,8,16,640]{3,2,1,0:T(8,128)(2,1)} collective-permute-done((bf16[2,8,16,640]{3,2,1,0:T(8,128)(2,1)}, bf16[2,8,16,640]{3,2,1,0:T(8,128)(2,1)}, u32[]{:S(2)}, u32[]{:S(2)}) %collective-permute-start.12) | collective-permute-done | bytes 327712 | tf_op jit(solution)/shard_map/ppermute | solution.py:268
  44.3 6.1 %collective-permute-done.13 = bf16[2,8,16,640]{3,2,1,0:T(8,128)(2,1)S(1)} collective-permute-done((bf16[2,8,16,640]{3,2,1,0:T(8,128)(2,1)S(1)}, bf16[2,8,16,640]{3,2,1,0:T(8,128)(2,1)S(1)}, u32[]{:S(2)}, u32[]{:S(2)}) %collective-permute-start.13) | collective-permute-done | bytes 327712 | tf_op jit(solution)/shard_map/ppermute | solution.py:268
  50.5 2.7 %collective-permute-start.14 = (bf16[2,8,16,640]{3,2,1,0:T(8,128)(2,1)S(1)}, bf16[2,8,16,640]{3,2,1,0:T(8,128)(2,1)S(1)}, u32[]{:S(2)}, u32[]{:S(2)}) collective-permute-start(bf16[2,8,16,640]{3,2,1,0:T(8,128)(2,1)S(1)} %add_convert_fusion.1), channel_id=1, source_target_pairs={{0,14},{2,0},{4,2},{6,4},{8,6},{10,8},{12,10},{14,12},{1,15},{3,1}... | collective-permute-start | bytes 983048 | tf_op jit(solution)/shard_map/ppermute | solution.py:268
  53.3 4.8 %shard_map.65 = (bf16[8,24,640]{2,1,0:T(8,128)(2,1)S(1)}, bf16[8,24,640]{2,1,0:T(8,128)(2,1)S(1)}, bf16[8,24,640]{2,1,0:T(8,128)(2,1)S(1)}, bf16[8,24,640]{2,1,0...) custom-call(s32[2]{0:T(128)S(1)} %pad_add_fusion._, ...), custom_call_target="tpu_custom_call" | custom-call | flops 1258291200 | bytes 2990080 | tf_op jit(solution)/shard_map/pallas_call | solution.py:41
  59.3 3.2 %collective-permute-start.2 = (bf16[8,24,640]{2,1,0:T(8,128)(2,1)S(1)}, bf16[8,24,640]{2,1,0:T(8,128)(2,1)S(1)}, u32[]{:S(2)}, u32[]{:S(2)}) collective-permute-start(bf16[8,24,640]{2,1,0:T(8,128)(2,1)S(1)} %get-tuple-element.31), channel_id=1, source_target_pairs={{0,4},{2,6},{4,8},{6,10},{8,12},{10,14},{12,0},{14,2},{1,5},{3,7},... | collective-permute-start | bytes 737288 | tf_op jit(solution)/shard_map/ppermute | solution.py:268
  64.2 6.2 %collective-permute-done.1 = bf16[8,24,640]{2,1,0:T(8,128)(2,1)S(1)} collective-permute-done((bf16[8,24,640]{2,1,0:T(8,128)(2,1)S(1)}, bf16[8,24,640]{2,1,0:T(8,128)(2,1)S(1)}, u32[]{:S(2)}, u32[]{:S(2)}) %collective-permute-start.1) | collective-permute-done | bytes 245792 | tf_op jit(solution)/shard_map/ppermute | solution.py:268
  70.4 3.9 %collective-permute-done.2 = bf16[8,24,640]{2,1,0:T(8,128)(2,1)S(1)} collective-permute-done((bf16[8,24,640]{2,1,0:T(8,128)(2,1)S(1)}, bf16[8,24,640]{2,1,0:T(8,128)(2,1)S(1)}, u32[]{:S(2)}, u32[]{:S(2)}) %collective-permute-start.2) | collective-permute-done | bytes 245792 | tf_op jit(solution)/shard_map/ppermute | solution.py:268
  74.3 4.4 %collective-permute-start.3 = (bf16[8,24,640]{2,1,0:T(8,128)(2,1)S(1)}, bf16[8,24,640]{2,1,0:T(8,128)(2,1)S(1)}, u32[]{:S(2)}, u32[]{:S(2)}) collective-permute-start(bf16[8,24,640]{2,1,0:T(8,128)(2,1)S(1)} %add_convert_fusion.9), channel_id=1, source_target_pairs={{0,2},{2,4},{4,6},{6,8},{8,10},{10,12},{12,14},{14,0},{1,3},{3,5},... | collective-permute-start | bytes 737288 | tf_op jit(solution)/shard_map/ppermute | solution.py:268
  81.1 3.7 %collective-permute-done.3 = bf16[8,24,640]{2,1,0:T(8,128)(2,1)S(1)} collective-permute-done((bf16[8,24,640]{2,1,0:T(8,128)(2,1)S(1)}, bf16[8,24,640]{2,1,0:T(8,128)(2,1)S(1)}, u32[]{:S(2)}, u32[]{:S(2)}) %collective-permute-start.3) | collective-permute-done | bytes 245792 | tf_op jit(solution)/shard_map/ppermute | solution.py:268
  89.0 3.5 %collective-permute-done.4 = bf16[8,24,640]{2,1,0:T(8,128)(2,1)S(1)} collective-permute-done((bf16[8,24,640]{2,1,0:T(8,128)(2,1)S(1)}, bf16[8,24,640]{2,1,0:T(8,128)(2,1)S(1)}, u32[]{:S(2)}, u32[]{:S(2)}) %collective-permute-start.4) | collective-permute-done | bytes 245792 | tf_op jit(solution)/shard_map/ppermute | solution.py:268
  94.7 7.5 %all-to-all-start = ((bf16[16,40,288]{2,1,0:T(8,128)(2,1)}), bf16[16,40,288]{2,1,0:T(8,128)(2,1)S(1)}, u32[]{:S(2)}, u32[]{:S(2)}) async-start(bf16[16,40,288]{2,1,0:T(8,128)(2,1)} %shard_map.67), calls=%async_computation | async-start | bytes 983040 | tf_op jit(solution)/shard_map/all_to_all | solution.py:328
  105.6 5.0 %all-to-all-done = bf16[16,40,288]{2,1,0:T(8,128)(2,1)S(1)} async-done(((bf16[16,40,288]{2,1,0:T(8,128)(2,1)}), bf16[16,40,288]{2,1,0:T(8,128)(2,1)S(1)}, u32[]{:S(2)}, u32[]{:S(2)}) %all-to-all-start) | async-done | bytes 368672 | tf_op jit(solution)/shard_map/all_to_all | solution.py:328
  111.8 14.6 %all_to_all.10.x = bf16[16,40,288]{2,1,0:T(8,128)(2,1)S(1)} all-to-all(bf16[16,40,288]{2,1,0:T(8,128)(2,1)S(1)} %bitcast.33), channel_id=1, replica_groups=mesh['row'=16,'z'=8,'ylo'=2] {'row'}, dimensions={0} | all-to-all | bytes 737280 | tf_op jit(solution)/shard_map/all_to_all | solution.py:330
  130.4 6.6 %collective-permute-done.19.refs_7_ = bf16[8,24,640]{2,1,0:T(8,128)(2,1)S(1)} collective-permute-done((bf16[8,24,640]{2,1,0:T(8,128)(2,1)S(1)}, bf16[8,24,640]{2,1,0:T(8,128)(2,1)S(1)}, u32[]{:S(2)}, u32[]{:S(2)}) %collective-permute-start.19) | collective-permute-done | bytes 245792 | tf_op jit(solution)/shard_map/ppermute | solution.py:268
  137.4 3.0 %collective-permute-start.17 = (bf16[8,24,640]{2,1,0:T(8,128)(2,1)S(1)}, bf16[8,24,640]{2,1,0:T(8,128)(2,1)S(1)}, u32[]{:S(2)}, u32[]{:S(2)}) collective-permute-start(bf16[8,24,640]{2,1,0:T(8,128)(2,1)S(1)} %collective-permute-done.16.refs_1_), channel_id=1, source_target_pairs={{0,14},{2,0},{4,2},{6,4},{8,6},{10,8},{12,10},{14,12},{1,15},{3,1}... | collective-permute-start | bytes 737288 | tf_op jit(solution)/shard_map/ppermute | solution.py:268
  140.4 5.7 %collective-permute-done.20.refs_6_ = bf16[8,24,640]{2,1,0:T(8,128)(2,1)S(1)} collective-permute-done((bf16[8,24,640]{2,1,0:T(8,128)(2,1)S(1)}, bf16[8,24,640]{2,1,0:T(8,128)(2,1)S(1)}, u32[]{:S(2)}, u32[]{:S(2)}) %collective-permute-start.20) | collective-permute-done | bytes 245792 | tf_op jit(solution)/shard_map/ppermute | solution.py:268
  146.1 2.7 %collective-permute-start.21 = (bf16[8,24,640]{2,1,0:T(8,128)(2,1)S(1)}, bf16[8,24,640]{2,1,0:T(8,128)(2,1)S(1)}, u32[]{:S(2)}, u32[]{:S(2)}) collective-permute-start(bf16[8,24,640]{2,1,0:T(8,128)(2,1)S(1)} %collective-permute-done.20.refs_6_), channel_id=1, source_target_pairs={{0,4},{2,6},{4,8},{6,10},{8,12},{10,14},{12,0},{14,2},{1,5},{3,7},... | collective-permute-start | bytes 737288 | tf_op jit(solution)/shard_map/ppermute | solution.py:268
  150.7 7.1 %collective-permute-done.22.refs_5_ = bf16[8,24,640]{2,1,0:T(8,128)(2,1)S(1)} collective-permute-done((bf16[8,24,640]{2,1,0:T(8,128)(2,1)S(1)}, bf16[8,24,640]{2,1,0:T(8,128)(2,1)S(1)}, u32[]{:S(2)}, u32[]{:S(2)}) %collective-permute-start.22) | collective-permute-done | bytes 245792 | tf_op jit(solution)/shard_map/ppermute | solution.py:268
  157.8 6.5 %collective-permute-done.21.refs_4_ = bf16[8,24,640]{2,1,0:T(8,128)(2,1)S(1)} collective-permute-done((bf16[8,24,640]{2,1,0:T(8,128)(2,1)S(1)}, bf16[8,24,640]{2,1,0:T(8,128)(2,1)S(1)}, u32[]{:S(2)}, u32[]{:S(2)}) %collective-permute-start.21) | collective-permute-done | bytes 245792 | tf_op jit(solution)/shard_map/ppermute | solution.py:268
  164.3 3.8 %shard_map.70 = (bf16[40,24,640]{2,1,0:T(8,128)(2,1)S(1)}, bf16[2,40,40,640]{3,2,1,0:T(8,128)(2,1)}) custom-call(s32[2]{0:T(128)S(1)} %pad_add_fusion._, bf16[8,24,640]{2,1,0:T(8,128)(2,1)S(1)} %get-tuple-element.45.refs_0_, bf16[8,24,640]{2,1,0:T(8,128)(2,1)S(1)} %collective-permute-done.16.refs_1_, ...), custom_call_target="tpu_custom_call" | custom-call | flops 1258291200 | bytes 1310720 | tf_op jit(solution)/shard_map/pallas_call | solution.py:41
  172.1 5.5 %collective-permute-done.29.refs_7_ = bf16[2,8,16,640]{3,2,1,0:T(8,128)(2,1)S(1)} collective-permute-done((bf16[2,8,16,640]{3,2,1,0:T(8,128)(2,1)S(1)}, bf16[2,8,16,640]{3,2,1,0:T(8,128)(2,1)S(1)}, u32[]{:S(2)}, u32[]{:S(2)}) %collective-permute-start.29) | collective-permute-done | bytes 327712 | tf_op jit(solution)/shard_map/ppermute | solution.py:268
  181.0 6.5 %collective-permute-done.30.refs_6_ = bf16[2,8,16,640]{3,2,1,0:T(8,128)(2,1)S(1)} collective-permute-done((bf16[2,8,16,640]{3,2,1,0:T(8,128)(2,1)S(1)}, bf16[2,8,16,640]{3,2,1,0:T(8,128)(2,1)S(1)}, u32[]{:S(2)}, u32[]{:S(2)}) %collective-permute-start.30) | collective-permute-done | bytes 327712 | tf_op jit(solution)/shard_map/ppermute | solution.py:268
  188.8 3.8 %collective-permute-start.27 = (bf16[2,8,16,640]{3,2,1,0:T(8,128)(2,1)S(1)}, bf16[2,8,16,640]{3,2,1,0:T(8,128)(2,1)S(1)}, u32[]{:S(2)}, u32[]{:S(2)}) collective-permute-start(bf16[2,8,16,640]{3,2,1,0:T(8,128)(2,1)S(1)} %collective-permute-done.26.refs_2_), channel_id=1, source_target_pairs={{0,14},{2,0},{4,2},{6,4},{8,6},{10,8},{12,10},{14,12},{1,15},{3,1}... | collective-permute-start | bytes 983048 | tf_op jit(solution)/shard_map/ppermute | solution.py:268
  192.6 3.2 %collective-permute-done.31.refs_5_ = bf16[2,8,16,640]{3,2,1,0:T(8,128)(2,1)S(1)} collective-permute-done((bf16[2,8,16,640]{3,2,1,0:T(8,128)(2,1)S(1)}, bf16[2,8,16,640]{3,2,1,0:T(8,128)(2,1)S(1)}, u32[]{:S(2)}, u32[]{:S(2)}) %collective-permute-start.31) | collective-permute-done | bytes 327712 | tf_op jit(solution)/shard_map/ppermute | solution.py:268
  195.8 5.0 %collective-permute-done.28.refs_4_ = bf16[2,8,16,640]{3,2,1,0:T(8,128)(2,1)S(1)} collective-permute-done((bf16[2,8,16,640]{3,2,1,0:T(8,128)(2,1)S(1)}, bf16[2,8,16,640]{3,2,1,0:T(8,128)(2,1)S(1)}, u32[]{:S(2)}, u32[]{:S(2)}) %collective-permute-start.28) | collective-permute-done | bytes 327712 | tf_op jit(solution)/shard_map/ppermute | solution.py:268
  200.7 6.4 %collective-permute-done.27.refs_3_ = bf16[2,8,16,640]{3,2,1,0:T(8,128)(2,1)S(1)} collective-permute-done((bf16[2,8,16,640]{3,2,1,0:T(8,128)(2,1)S(1)}, bf16[2,8,16,640]{3,2,1,0:T(8,128)(2,1)S(1)}, u32[]{:S(2)}, u32[]{:S(2)}) %collective-permute-start.27) | collective-permute-done | bytes 327712 | tf_op jit(solution)/shard_map/ppermute | solution.py:268
  207.1 3.7 %shard_map.71.__ = bf16[2,40,40,640]{3,2,1,0:T(8,128)(2,1)} custom-call(s32[2]{0:T(128)S(1)} %pad_add_fusion._, bf16[2,8,16,640]{3,2,1,0:T(8,128)(2,1)S(1)} %pad_maximum_fusion.2.refs_0_, bf16[2,8,16,640]{3,2,1,0:T(8,128)(2,1)S(1)} %collective-permute-done.25.refs_1_, ...), custom_call_target="tpu_custom_call", output_to_operand_aliasing={{}: (10, {})} | custom-call | flops 838860800 | bytes 3522560 | tf_op jit(solution)/shard_map/pallas_call | solution.py:41
  (95 shorter events, 48.3 us)
Async XLA Ops:
  13.2 14.0 %collective-permute-start.8 = (bf16[2,8,16,640]{3,2,1,0:T(8,128)(2,1)}, bf16[2,8,16,640]{3,2,1,0:T(8,128)(2,1)}, u32[]{:S(2)}, u32[]{:S(2)}) collective-permute-start(bf16[2,8,16,640]{3,2,1,0:T(8,128)(2,1)} %get-tuple-element.38), channel_id=1, source_target_pairs={{0,2},{2,4},{4,6},{6,8},{8,10},{10,12},{12,14},{14,0},{1,3},{3,5},... | collective-permute-start | bytes 983048 | tf_op jit(solution)/shard_map/ppermute | solution.py:268
  15.2 18.0 %collective-permute-start.11 = (bf16[2,8,16,640]{3,2,1,0:T(8,128)(2,1)}, bf16[2,8,16,640]{3,2,1,0:T(8,128)(2,1)S(1)}, u32[]{:S(2)}, u32[]{:S(2)}) collective-permute-start(bf16[2,8,16,640]{3,2,1,0:T(8,128)(2,1)} %get-tuple-element.41), channel_id=1, source_target_pairs={{0,14},{2,0},{4,2},{6,4},{8,6},{10,8},{12,10},{14,12},{1,15},{3,1}... | collective-permute-start | bytes 983048 | tf_op jit(solution)/shard_map/ppermute | solution.py:268
  19.2 21.3 %collective-permute-start.12 = (bf16[2,8,16,640]{3,2,1,0:T(8,128)(2,1)}, bf16[2,8,16,640]{3,2,1,0:T(8,128)(2,1)}, u32[]{:S(2)}, u32[]{:S(2)}) collective-permute-start(bf16[2,8,16,640]{3,2,1,0:T(8,128)(2,1)} %get-tuple-element.43), channel_id=1, source_target_pairs={{0,12},{2,14},{4,0},{6,2},{8,4},{10,6},{12,8},{14,10},{1,13},{3,15... | collective-permute-start | bytes 983048 | tf_op jit(solution)/shard_map/ppermute | solution.py:268
  21.6 31.7 %collective-permute-start = (bf16[40,24,640]{2,1,0:T(8,128)(2,1)}, bf16[40,24,640]{2,1,0:T(8,128)(2,1)}, u32[]{:S(2)}, u32[]{:S(2)}) collective-permute-start(bf16[40,24,640]{2,1,0:T(8,128)(2,1)} %shard_map.64), channel_id=1, source_target_pairs={{0,1},{1,0},{2,3},{3,2},{4,5},{5,4},{6,7},{7,6},{8,9},{9,8},{10,11... | collective-permute-start | bytes 3686408 | tf_op jit(solution)/shard_map/ppermute | solution.py:272
  28.3 13.8 %collective-permute-start.9 = (bf16[2,8,16,640]{3,2,1,0:T(8,128)(2,1)S(1)}, bf16[2,8,16,640]{3,2,1,0:T(8,128)(2,1)S(1)}, u32[]{:S(2)}, u32[]{:S(2)}) collective-permute-start(bf16[2,8,16,640]{3,2,1,0:T(8,128)(2,1)S(1)} %add_convert_fusion.4), channel_id=1, source_target_pairs={{0,2},{2,4},{4,6},{6,8},{8,10},{10,12},{12,14},{14,0},{1,3},{3,5},... | collective-permute-start | bytes 983048 | tf_op jit(solution)/shard_map/ppermute | solution.py:268
  41.8 8.7 %collective-permute-start.13 = (bf16[2,8,16,640]{3,2,1,0:T(8,128)(2,1)S(1)}, bf16[2,8,16,640]{3,2,1,0:T(8,128)(2,1)S(1)}, u32[]{:S(2)}, u32[]{:S(2)}) collective-permute-start(bf16[2,8,16,640]{3,2,1,0:T(8,128)(2,1)S(1)} %add_convert_fusion.2), channel_id=1, source_target_pairs={{0,14},{2,0},{4,2},{6,4},{8,6},{10,8},{12,10},{14,12},{1,15},{3,1}... | collective-permute-start | bytes 983048 | tf_op jit(solution)/shard_map/ppermute | solution.py:268
  42.2 20.3 %collective-permute-start.10 = (bf16[2,8,16,640]{3,2,1,0:T(8,128)(2,1)S(1)}, bf16[2,8,16,640]{3,2,1,0:T(8,128)(2,1)S(1)}, u32[]{:S(2)}, u32[]{:S(2)}) collective-permute-start(bf16[2,8,16,640]{3,2,1,0:T(8,128)(2,1)S(1)} %add_convert_fusion.3), channel_id=1, source_target_pairs={{0,2},{2,4},{4,6},{6,8},{8,10},{10,12},{12,14},{14,0},{1,3},{3,5},... | collective-permute-start | bytes 983048 | tf_op jit(solution)/shard_map/ppermute | solution.py:268
  50.5 12.0 %collective-permute-start.14 = (bf16[2,8,16,640]{3,2,1,0:T(8,128)(2,1)S(1)}, bf16[2,8,16,640]{3,2,1,0:T(8,128)(2,1)S(1)}, u32[]{:S(2)}, u32[]{:S(2)}) collective-permute-start(bf16[2,8,16,640]{3,2,1,0:T(8,128)(2,1)S(1)} %add_convert_fusion.1), channel_id=1, source_target_pairs={{0,14},{2,0},{4,2},{6,4},{8,6},{10,8},{12,10},{14,12},{1,15},{3,1}... | collective-permute-start | bytes 983048 | tf_op jit(solution)/shard_map/ppermute | solution.py:268
  58.1 12.2 %collective-permute-start.1 = (bf16[8,24,640]{2,1,0:T(8,128)(2,1)S(1)}, bf16[8,24,640]{2,1,0:T(8,128)(2,1)S(1)}, u32[]{:S(2)}, u32[]{:S(2)}) collective-permute-start(bf16[8,24,640]{2,1,0:T(8,128)(2,1)S(1)} %get-tuple-element.29), channel_id=1, source_target_pairs={{0,2},{2,4},{4,6},{6,8},{8,10},{10,12},{12,14},{14,0},{1,3},{3,5},... | collective-permute-start | bytes 737288 | tf_op jit(solution)/shard_map/ppermute | solution.py:268
  59.3 14.9 %collective-permute-start.2 = (bf16[8,24,640]{2,1,0:T(8,128)(2,1)S(1)}, bf16[8,24,640]{2,1,0:T(8,128)(2,1)S(1)}, u32[]{:S(2)}, u32[]{:S(2)}) collective-permute-start(bf16[8,24,640]{2,1,0:T(8,128)(2,1)S(1)} %get-tuple-element.31), channel_id=1, source_target_pairs={{0,4},{2,6},{4,8},{6,10},{8,12},{10,14},{12,0},{14,2},{1,5},{3,7},... | collective-permute-start | bytes 737288 | tf_op jit(solution)/shard_map/ppermute | solution.py:268
  62.6 16.1 %collective-permute-start.5 = (bf16[8,24,640]{2,1,0:T(8,128)(2,1)S(1)}, bf16[8,24,640]{2,1,0:T(8,128)(2,1)S(1)}, u32[]{:S(2)}, u32[]{:S(2)}) collective-permute-start(bf16[8,24,640]{2,1,0:T(8,128)(2,1)S(1)} %get-tuple-element.33), channel_id=1, source_target_pairs={{0,14},{2,0},{4,2},{6,4},{8,6},{10,8},{12,10},{14,12},{1,15},{3,1}... | collective-permute-start | bytes 737288 | tf_op jit(solution)/shard_map/ppermute | solution.py:268
  74.3 10.6 %collective-permute-start.3 = (bf16[8,24,640]{2,1,0:T(8,128)(2,1)S(1)}, bf16[8,24,640]{2,1,0:T(8,128)(2,1)S(1)}, u32[]{:S(2)}, u32[]{:S(2)}) collective-permute-start(bf16[8,24,640]{2,1,0:T(8,128)(2,1)S(1)} %add_convert_fusion.9), channel_id=1, source_target_pairs={{0,2},{2,4},{4,6},{6,8},{8,10},{10,12},{12,14},{14,0},{1,3},{3,5},... | collective-permute-start | bytes 737288 | tf_op jit(solution)/shard_map/ppermute | solution.py:268
  78.8 7.9 %collective-permute-start.6 = (bf16[8,24,640]{2,1,0:T(8,128)(2,1)S(1)}, bf16[8,24,640]{2,1,0:T(8,128)(2,1)S(1)}, u32[]{:S(2)}, u32[]{:S(2)}) collective-permute-start(bf16[8,24,640]{2,1,0:T(8,128)(2,1)S(1)} %add_convert_fusion.7), channel_id=1, source_target_pairs={{0,14},{2,0},{4,2},{6,4},{8,6},{10,8},{12,10},{14,12},{1,15},{3,1}... | collective-permute-start | bytes 737288 | tf_op jit(solution)/shard_map/ppermute | solution.py:268
  79.5 9.4 %collective-permute-start.15 = (bf16[8,16,640]{2,1,0:T(8,128)(2,1)S(1)}, bf16[8,16,640]{2,1,0:T(8,128)(2,1)S(1)}, u32[]{:S(2)}, u32[]{:S(2)}) collective-permute-start(bf16[8,16,640]{2,1,0:T(8,128)(2,1)S(1)} %slice_bitcast_fusion.2), channel_id=1, source_target_pairs={{0,1},{1,0},{2,3},{3,2},{4,5},{5,4},{6,7},{7,6},{8,9},{9,8},{10,11... | collective-permute-start | bytes 491528 | tf_op jit(solution)/shard_map/ppermute | solution.py:272
  85.0 7.5 %collective-permute-start.4 = (bf16[8,24,640]{2,1,0:T(8,128)(2,1)S(1)}, bf16[8,24,640]{2,1,0:T(8,128)(2,1)S(1)}, u32[]{:S(2)}, u32[]{:S(2)}) collective-permute-start(bf16[8,24,640]{2,1,0:T(8,128)(2,1)S(1)} %add_convert_fusion.8), channel_id=1, source_target_pairs={{0,2},{2,4},{4,6},{6,8},{8,10},{10,12},{12,14},{14,0},{1,3},{3,5},... | collective-permute-start | bytes 737288 | tf_op jit(solution)/shard_map/ppermute | solution.py:268
  94.7 15.9 %all-to-all-start = ((bf16[16,40,288]{2,1,0:T(8,128)(2,1)}), bf16[16,40,288]{2,1,0:T(8,128)(2,1)S(1)}, u32[]{:S(2)}, u32[]{:S(2)}) async-start(bf16[16,40,288]{2,1,0:T(8,128)(2,1)} %shard_map.67), calls=%async_computation | async-start | bytes 983040 | tf_op jit(solution)/shard_map/all_to_all | solution.py:328
  127.0 9.9 %collective-permute-start.19 = (bf16[8,24,640]{2,1,0:T(8,128)(2,1)S(1)}, bf16[8,24,640]{2,1,0:T(8,128)(2,1)S(1)}, u32[]{:S(2)}, u32[]{:S(2)}) collective-permute-start(bf16[8,24,640]{2,1,0:T(8,128)(2,1)S(1)} %get-tuple-element.45.refs_0_), channel_id=1, source_target_pairs={{0,2},{2,4},{4,6},{6,8},{8,10},{10,12},{12,14},{14,0},{1,3},{3,5},... | collective-permute-start | bytes 737288 | tf_op jit(solution)/shard_map/ppermute | solution.py:268
  128.6 8.8 %collective-permute-start.16 = (bf16[8,24,640]{2,1,0:T(8,128)(2,1)S(1)}, bf16[8,24,640]{2,1,0:T(8,128)(2,1)S(1)}, u32[]{:S(2)}, u32[]{:S(2)}) collective-permute-start(bf16[8,24,640]{2,1,0:T(8,128)(2,1)S(1)} %get-tuple-element.45.refs_0_), channel_id=1, source_target_pairs={{0,14},{2,0},{4,2},{6,4},{8,6},{10,8},{12,10},{14,12},{1,15},{3,1}... | collective-permute-start | bytes 737288 | tf_op jit(solution)/shard_map/ppermute | solution.py:268
  136.9 9.2 %collective-permute-start.20 = (bf16[8,24,640]{2,1,0:T(8,128)(2,1)S(1)}, bf16[8,24,640]{2,1,0:T(8,128)(2,1)S(1)}, u32[]{:S(2)}, u32[]{:S(2)}) collective-permute-start(bf16[8,24,640]{2,1,0:T(8,128)(2,1)S(1)} %collective-permute-done.19.refs_7_), channel_id=1, source_target_pairs={{0,2},{2,4},{4,6},{6,8},{8,10},{10,12},{12,14},{14,0},{1,3},{3,5},... | collective-permute-start | bytes 737288 | tf_op jit(solution)/shard_map/ppermute | solution.py:268
  137.4 11.4 %collective-permute-start.17 = (bf16[8,24,640]{2,1,0:T(8,128)(2,1)S(1)}, bf16[8,24,640]{2,1,0:T(8,128)(2,1)S(1)}, u32[]{:S(2)}, u32[]{:S(2)}) collective-permute-start(bf16[8,24,640]{2,1,0:T(8,128)(2,1)S(1)} %collective-permute-done.16.refs_1_), channel_id=1, source_target_pairs={{0,14},{2,0},{4,2},{6,4},{8,6},{10,8},{12,10},{14,12},{1,15},{3,1}... | collective-permute-start | bytes 737288 | tf_op jit(solution)/shard_map/ppermute | solution.py:268
  146.1 11.7 %collective-permute-start.22 = (bf16[8,24,640]{2,1,0:T(8,128)(2,1)S(1)}, bf16[8,24,640]{2,1,0:T(8,128)(2,1)S(1)}, u32[]{:S(2)}, u32[]{:S(2)}) collective-permute-start(bf16[8,24,640]{2,1,0:T(8,128)(2,1)S(1)} %collective-permute-done.20.refs_6_), channel_id=1, source_target_pairs={{0,2},{2,4},{4,6},{6,8},{8,10},{10,12},{12,14},{14,0},{1,3},{3,5},... | collective-permute-start | bytes 737288 | tf_op jit(solution)/shard_map/ppermute | solution.py:268
  146.1 18.2 %collective-permute-start.21 = (bf16[8,24,640]{2,1,0:T(8,128)(2,1)S(1)}, bf16[8,24,640]{2,1,0:T(8,128)(2,1)S(1)}, u32[]{:S(2)}, u32[]{:S(2)}) collective-permute-start(bf16[8,24,640]{2,1,0:T(8,128)(2,1)S(1)} %collective-permute-done.20.refs_6_), channel_id=1, source_target_pairs={{0,4},{2,6},{4,8},{6,10},{8,12},{10,14},{12,0},{14,2},{1,5},{3,7},... | collective-permute-start | bytes 737288 | tf_op jit(solution)/shard_map/ppermute | solution.py:268
  148.8 15.5 %collective-permute-start.18 = (bf16[8,24,640]{2,1,0:T(8,128)(2,1)S(1)}, bf16[8,24,640]{2,1,0:T(8,128)(2,1)S(1)}, u32[]{:S(2)}, u32[]{:S(2)}) collective-permute-start(bf16[8,24,640]{2,1,0:T(8,128)(2,1)S(1)} %collective-permute-done.17.refs_2_), channel_id=1, source_target_pairs={{0,14},{2,0},{4,2},{6,4},{8,6},{10,8},{12,10},{14,12},{1,15},{3,1}... | collective-permute-start | bytes 737288 | tf_op jit(solution)/shard_map/ppermute | solution.py:268
  150.1 18.7 %collective-permute-start.24 = (bf16[8,16,640]{2,1,0:T(8,128)(2,1)S(1)}, bf16[8,16,640]{2,1,0:T(8,128)(2,1)S(1)}, u32[]{:S(2)}, u32[]{:S(2)}) collective-permute-start(bf16[8,16,640]{2,1,0:T(8,128)(2,1)S(1)} %get-tuple-element.47), channel_id=1, source_target_pairs={{0,1},{1,0},{2,3},{3,2},{4,5},{5,4},{6,7},{7,6},{8,9},{9,8},{10,11... | collective-permute-start | bytes 491528 | tf_op jit(solution)/shard_map/ppermute | solution.py:272
  168.1 42.7 %collective-permute-start.23 = (bf16[40,24,640]{2,1,0:T(8,128)(2,1)S(1)}, bf16[40,24,640]{2,1,0:T(8,128)(2,1)S(1)}, u32[]{:S(2)}, u32[]{:S(2)}) collective-permute-start(bf16[40,24,640]{2,1,0:T(8,128)(2,1)S(1)} %get-tuple-element.46), channel_id=1, source_target_pairs={{0,1},{1,0},{2,3},{3,2},{4,5},{5,4},{6,7},{7,6},{8,9},{9,8},{10,11... | collective-permute-start | bytes 3686408 | tf_op jit(solution)/shard_map/ppermute | solution.py:272
  168.8 8.8 %collective-permute-start.29 = (bf16[2,8,16,640]{3,2,1,0:T(8,128)(2,1)S(1)}, bf16[2,8,16,640]{3,2,1,0:T(8,128)(2,1)S(1)}, u32[]{:S(2)}, u32[]{:S(2)}) collective-permute-start(bf16[2,8,16,640]{3,2,1,0:T(8,128)(2,1)S(1)} %pad_maximum_fusion.2.refs_0_), channel_id=1, source_target_pairs={{0,2},{2,4},{4,6},{6,8},{8,10},{10,12},{12,14},{14,0},{1,3},{3,5},... | collective-permute-start | bytes 983048 | tf_op jit(solution)/shard_map/ppermute | solution.py:268
  171.0 7.9 %collective-permute-start.25 = (bf16[2,8,16,640]{3,2,1,0:T(8,128)(2,1)S(1)}, bf16[2,8,16,640]{3,2,1,0:T(8,128)(2,1)S(1)}, u32[]{:S(2)}, u32[]{:S(2)}) collective-permute-start(bf16[2,8,16,640]{3,2,1,0:T(8,128)(2,1)S(1)} %pad_maximum_fusion.2.refs_0_), channel_id=1, source_target_pairs={{0,14},{2,0},{4,2},{6,4},{8,6},{10,8},{12,10},{14,12},{1,15},{3,1}... | collective-permute-start | bytes 983048 | tf_op jit(solution)/shard_map/ppermute | solution.py:268
  177.6 9.9 %collective-permute-start.30 = (bf16[2,8,16,640]{3,2,1,0:T(8,128)(2,1)S(1)}, bf16[2,8,16,640]{3,2,1,0:T(8,128)(2,1)S(1)}, u32[]{:S(2)}, u32[]{:S(2)}) collective-permute-start(bf16[2,8,16,640]{3,2,1,0:T(8,128)(2,1)S(1)} %collective-permute-done.29.refs_7_), channel_id=1, source_target_pairs={{0,2},{2,4},{4,6},{6,8},{8,10},{10,12},{12,14},{14,0},{1,3},{3,5},... | collective-permute-start | bytes 983048 | tf_op jit(solution)/shard_map/ppermute | solution.py:268
  178.9 9.9 %collective-permute-start.26 = (bf16[2,8,16,640]{3,2,1,0:T(8,128)(2,1)S(1)}, bf16[2,8,16,640]{3,2,1,0:T(8,128)(2,1)S(1)}, u32[]{:S(2)}, u32[]{:S(2)}) collective-permute-start(bf16[2,8,16,640]{3,2,1,0:T(8,128)(2,1)S(1)} %collective-permute-done.25.refs_1_), channel_id=1, source_target_pairs={{0,14},{2,0},{4,2},{6,4},{8,6},{10,8},{12,10},{14,12},{1,15},{3,1}... | collective-permute-start | bytes 983048 | tf_op jit(solution)/shard_map/ppermute | solution.py:268
  187.5 8.3 %collective-permute-start.31 = (bf16[2,8,16,640]{3,2,1,0:T(8,128)(2,1)S(1)}, bf16[2,8,16,640]{3,2,1,0:T(8,128)(2,1)S(1)}, u32[]{:S(2)}, u32[]{:S(2)}) collective-permute-start(bf16[2,8,16,640]{3,2,1,0:T(8,128)(2,1)S(1)} %collective-permute-done.30.refs_6_), channel_id=1, source_target_pairs={{0,2},{2,4},{4,6},{6,8},{8,10},{10,12},{12,14},{14,0},{1,3},{3,5},... | collective-permute-start | bytes 983048 | tf_op jit(solution)/shard_map/ppermute | solution.py:268
  188.8 11.9 %collective-permute-start.28 = (bf16[2,8,16,640]{3,2,1,0:T(8,128)(2,1)S(1)}, bf16[2,8,16,640]{3,2,1,0:T(8,128)(2,1)S(1)}, u32[]{:S(2)}, u32[]{:S(2)}) collective-permute-start(bf16[2,8,16,640]{3,2,1,0:T(8,128)(2,1)S(1)} %collective-permute-done.26.refs_2_), channel_id=1, source_target_pairs={{0,12},{2,14},{4,0},{6,2},{8,4},{10,6},{12,8},{14,10},{1,13},{3,15... | collective-permute-start | bytes 983048 | tf_op jit(solution)/shard_map/ppermute | solution.py:268
  188.8 18.3 %collective-permute-start.27 = (bf16[2,8,16,640]{3,2,1,0:T(8,128)(2,1)S(1)}, bf16[2,8,16,640]{3,2,1,0:T(8,128)(2,1)S(1)}, u32[]{:S(2)}, u32[]{:S(2)}) collective-permute-start(bf16[2,8,16,640]{3,2,1,0:T(8,128)(2,1)S(1)} %collective-permute-done.26.refs_2_), channel_id=1, source_target_pairs={{0,14},{2,0},{4,2},{6,4},{8,6},{10,8},{12,10},{14,12},{1,15},{3,1}... | collective-permute-start | bytes 983048 | tf_op jit(solution)/shard_map/ppermute | solution.py:268
  (9 other events, 166.4 us)
where the time goes:
time: 214 us; the launch traced here: 213 us
  waiting for transfers between devices  98.4 us (46%)
  starting transfers between devices  61.4 us (29%)
  Pallas kernels  27.6 us (13%)
  blocking collectives  14.6 us (7%)
  other arithmetic  6.92 us (3%)
    ppermute x28, waiting for transfers between devices, move(): return lax.ppermute(x, 'z', [(i, (i + step) % NZ) for i in range(NZ)])  93.3 us
    ppermute x28, starting transfers between devices, move(): return lax.ppermute(x, 'z', [(i, (i + step) % NZ) for i in range(NZ)])  49.3 us
    pallas_call x9, Pallas kernels, call(): pl.pallas_call(body, grid_spec=spec, out_shape=out_shape, input_output_al...  27.6 us
    all_to_all x1, blocking collectives, run(): lax.all_to_all(back_one.reshape(NROW, MB, HALF), 'row', 0, 0, tiled=True)  14.6 us
    all_to_all x1, starting transfers between devices, run(): second = lax.all_to_all(first, 'row', 0, 0, tiled=True).reshape(NB, HALF)  7.46 us
    all_to_all x1, waiting for transfers between devices, run(): second = lax.all_to_all(first, 'row', 0, 0, tiled=True).reshape(NB, HALF)  5.04 us
    ppermute x4, starting transfers between devices, swap(): return lax.ppermute(x, 'ylo', SWAP)  4.59 us
  transfers between devices with their start and end apart: 33, of which 20 were waited for; matrix products, arithmetic and copies ran while one was open for 3% of the time, Pallas kernels for 6%

commit v1 on v0

--- a/solution.py
+++ b/solution.py
@@ -23,6 +23,9 @@
 SWAP = [(0, 1), (1, 0)]
 YT, ZT = 3, 2
 YM, ZM = YT * TILE, ZT * TILE
+LEAD = 3
+FAR = NZ // 2
+JH = JB // 2
 
 
 def dot(a, b):
@@ -56,7 +59,7 @@
     row = lax.broadcasted_iota(jnp.int32, (RW, NO), 0)
     occ = lax.broadcasted_iota(jnp.int32, (RW, NO), 1)
     block = row // TILE
-    want = ((zi + block // JB) % NZ) * JB + block % JB
+    want = ((zi + block // JB + LEAD) % NZ) * JB + block % JB
     tall = dot((occ == want).astype(BF), wide)
     row = lax.broadcasted_iota(jnp.int32, (RW, CL), 0)
     col = lax.broadcasted_iota(jnp.int32, (RW, CL), 1)
@@ -72,7 +75,7 @@
 
 
 def lift(slab, pick):
-    step = 8
+    step = 20
 
     def body(_, src, dst):
         dst[...] = src[0]
@@ -88,12 +91,14 @@
     )
 
 
-def y_parts(slab, swapped, k_mine, k_other, pick, first, tiles):
+def y_parts(slab, swapped, k_mine, k_other, pick, first, tiles, lo, hi):
+    rows = slice(lo * JB * TILE, hi * JB * TILE)
+
     def body(_, here, came, km, ko, *outs):
-        part = dot(km[...], fold(here[0])) + dot(ko[...], fold(came[...]))
-        part = part.reshape(NZ, JB, TILE, NB)
-        for k in range(NZ):
-            outs[k][...] = part[k].astype(BF)
+        part = dot(km[rows], fold(here[0])) + dot(ko[rows], fold(came[...]))
+        part = part.reshape(hi - lo, JB, TILE, NB)
+        for k, out in enumerate(outs):
+            out[...] = part[k].astype(BF)
 
     return call(
         body,
@@ -104,19 +109,21 @@
             whole((RW, CL)),
             whole((RW, CL)),
         ],
-        [pl.BlockSpec((JB, TILE, NB), lambda t, s: (0, t, 0))] * NZ,
-        [jax.ShapeDtypeStruct((JB, tiles * TILE, NB), BF)] * NZ,
+        [pl.BlockSpec((JB, TILE, NB), lambda t, s: (0, t, 0))] * (hi - lo),
+        [jax.ShapeDtypeStruct((JB, tiles * TILE, NB), BF)] * (hi - lo),
         (slab, swapped, k_mine, k_other),
         pick,
-        flops=4 * tiles * RW * CL * NB,
-    )
-
-
-def z_parts(slab, k_mine, pick, first, tiles):
+        flops=4 * tiles * (hi - lo) * JB * TILE * CL * NB,
+    )
+
+
+def z_parts(slab, k_mine, pick, first, tiles, lo, hi):
+    rows = slice(lo * JB * TILE, hi * JB * TILE)
+
     def body(_, here, km, *outs):
-        part = dot(km[...], fold(here[0])).reshape(NZ, JB, TILE, NB)
-        for k in range(NZ):
-            outs[k][0] = part[k].astype(BF)
+        part = dot(km[rows], fold(here[0])).reshape(hi - lo, JB, TILE, NB)
+        for k, out in enumerate(outs):
+            out[0] = part[k].astype(BF)
 
     return call(
         body,
@@ -125,11 +132,11 @@
             pl.BlockSpec((1, LB, TILE, NB), lambda o, t, s: (s[o], 0, first + t, 0)),
             whole((RW, CL)),
         ],
-        [pl.BlockSpec((1, JB, TILE, NB), lambda o, t, s: (o, 0, t, 0))] * NZ,
-        [pltpu.HBM((2, JB, tiles * TILE, NB), BF)] * NZ,
+        [pl.BlockSpec((1, JB, TILE, NB), lambda o, t, s: (o, 0, t, 0))] * (hi - lo),
+        [pltpu.HBM((2, JB, tiles * TILE, NB), BF)] * (hi - lo),
         (slab, k_mine),
         pick,
-        flops=4 * tiles * RW * CL * NB,
+        flops=4 * tiles * (hi - lo) * JB * TILE * CL * NB,
     )
 
 
@@ -137,9 +144,13 @@
     return jnp.concatenate([fold(s) for s in slots], axis=0)
 
 
+def rolled(slots):
+    return [*slots[LEAD:], *slots[:LEAD]]
+
+
 def y_expand(slots, kt_mine, kt_other, pick, first, tiles):
     def body(_, *refs):
-        slot_refs, (km, ko, send, kept) = refs[:NZ], refs[NZ:]
+        slot_refs, (km, ko, send, kept) = refs[: len(slots)], refs[len(slots) :]
         stack = gathered([s[...] for s in slot_refs])
         send[...] = dot(ko[...], stack).reshape(LB, TILE, NB).astype(BF)
         kept[0] = dot(km[...], stack).reshape(LB, TILE, NB).astype(BF)
@@ -147,7 +158,7 @@
     return call(
         body,
         (tiles,),
-        [pl.BlockSpec((JB, TILE, NB), lambda t, s: (0, t, 0))] * NZ
+        [pl.BlockSpec((s.shape[0], TILE, NB), lambda t, s: (0, t, 0)) for s in slots]
         + [whole((CL, RW)), whole((CL, RW))],
         [
             pl.BlockSpec((LB, TILE, NB), lambda t, s: (0, t, 0)),
@@ -272,28 +283,54 @@
     return lax.ppermute(x, "ylo", SWAP)
 
 
-def reduce_z(parts, way):
-    hop = [parts[3], parts[NZ - 3]]
-    far = move(parts[4], 2 * way)
-    for k in (2, 1, 0):
-        hop = [move(hop[0], 1), move(hop[1], -1)]
-        if k:
-            terms = [[hop[0], parts[k]], [hop[1], parts[NZ - k]]]
-            if k == 2:
-                terms[0 if way > 0 else 1].append(far)
-            hop = [add(*t) for t in terms]
-    return add(parts[0], *hop)
-
-
-def gather_z(own, way):
+def unrolled(parts):
+    return [*parts[NZ - LEAD :], *parts[: NZ - LEAD]]
+
+
+def chain_sum(parts):
+    up, down = parts[3], parts[FAR]
+    for n in range(1, FAR + 1):
+        if n < FAR:
+            up = move(up, 1)
+            up = add(up, parts[3 - n]) if n < 3 else up
+        down = move(down, -1)
+        down = add(down, parts[FAR + n]) if n < FAR else down
+    return add(parts[0], up, down)
+
+
+def tree_sum(parts):
+    up = move(parts[3], 1)
+    down = move(parts[5], -1)
+    high = move(parts[FAR][:JH], 2)
+    low = move(parts[FAR][JH:], -2)
+    none = jnp.zeros_like(high)
+    up = add(up, parts[2], jnp.concatenate([high, none], axis=0))
+    down = add(down, parts[6], jnp.concatenate([none, low], axis=0))
+    up = add(move(up, 1), parts[1])
+    down = add(move(down, -1), parts[7])
+    return add(parts[0], move(up, 1), move(down, -1))
+
+
+def chain_gather(own):
     slots = [own] + [None] * (NZ - 1)
-    hop = [own, own]
-    for k in (1, 2, 3):
-        if k == 3:
-            slots[4] = move(hop[0 if way > 0 else 1], 2 * way)
-        hop = [move(hop[0], 1), move(hop[1], -1)]
-        slots[NZ - k], slots[k] = hop
-    return slots
+    up = down = own
+    for n in range(1, FAR + 1):
+        if n < FAR:
+            up = slots[NZ - n] = move(up, 1)
+        down = slots[n] = move(down, -1)
+    return rolled(slots)
+
+
+def tree_gather(own):
+    up1 = move(own, 1)
+    down1 = move(own, -1)
+    up2 = move(up1, 1)
+    down2 = move(down1, -1)
+    up3 = move(up2, 1)
+    down3 = move(down2, -1)
+    high = move(up2[:JH], 2)
+    low = move(down2[JH:], -2)
+    return [down3, high, low, up3, up2, up1, own, down1, down2]
 
 
 def run(slab, coef_virtual, coef_occupied, occ_level, virt_level, orbital_index):
@@ -319,9 +356,13 @@
 
     raised, held = lax.optimization_barrier((lift(slab, pick), k_mine))
     swapped = swap(raised)
-    both = reduce_z(z_parts(slab, held, pick, YT, ZT), -1)
+    head = z_parts(slab, held, pick, YT, ZT, 0, 2)
+    tail = z_parts(slab, held, pick, YT, ZT, 2, NZ)
+    both = chain_sum(unrolled([*head, *tail]))
     last = add(both[0], swap(both[1]))
-    lead = reduce_z(y_parts(slab, swapped, k_mine, k_other, pick, 0, YT), 1)
+    head = y_parts(slab, swapped, k_mine, k_other, pick, 0, YT, 0, 3)
+    tail = y_parts(slab, swapped, k_mine, k_other, pick, 0, YT, 3, NZ)
+    lead = tree_sum(unrolled([*head, *tail]))
     summed = jnp.concatenate([lead, last], axis=1)
 
     first = to_virtual(summed, v_halves)
@@ -331,11 +372,11 @@
     wide_y, wide_z = to_basis(back, vt_halves, (YM, ZM))
 
     kt_mine, kt_other = k_mine.T, k_other.T
-    slots = gather_z(wide_y, 1)
+    slots = tree_gather(wide_y)
     send, out = y_expand(slots, kt_mine, kt_other, pick, 0, YT)
     got = swap(send)
     both = jnp.stack([wide_z, swap(wide_z)])
-    out = z_expand(gather_z(both, -1), kt_mine, out, pick, YT, ZT)
+    out = z_expand(chain_gather(both), kt_mine, out, pick, YT, ZT)
     return put(got, out, pick, 0, YT)
 
 

time: 214 us -> 198 us (0.925)
  waiting for transfers between devices: 98.4 us -> 63.1 us
  starting transfers between devices: 61.4 us -> 71.1 us
  Pallas kernels: 27.6 us -> 32.7 us
    ppermute x28 -> x30, waiting for transfers between devices: 93.3 us -> 58.2 us  [move(): return lax.ppermute(x, 'z', [(i, (i + step) % NZ) for i in range(NZ)])]
    ppermute x28 -> x30, starting transfers between devices: 49.3 us -> 58.9 us  [move(): return lax.ppermute(x, 'z', [(i, (i + step) % NZ) for i in range(NZ)])]
    pallas_call x9 -> x11, Pallas kernels: 27.6 us -> 32.7 us  [call(): pl.pallas_call(body, grid_spec=spec, out_shape=out_shape, input_output_al...]
  transfers between devices with their start and end apart: 33 -> 35, of which waited for: 20 -> 16; matrix products, arithmetic and copies ran while one was open for 3% -> 4% of each run, Pallas kernels for 6% -> 10%
where the time goes in v1:
time: 198 us; the launch traced here: 196 us
  starting transfers between devices  71.1 us (36%)
  waiting for transfers between devices  63.1 us (32%)
  Pallas kernels  32.7 us (17%)
  blocking collectives  14.6 us (7%)
  other arithmetic  8.02 us (4%)
  local copies, waits for them, and re-layouts  3.05 us (2%)
  matrix products  2.53 us (1%)
    ppermute x30, starting transfers between devices, move(): return lax.ppermute(x, 'z', [(i, (i + step) % NZ) for i in range(NZ)])  58.9 us
    ppermute x30, waiting for transfers between devices, move(): return lax.ppermute(x, 'z', [(i, (i + step) % NZ) for i in range(NZ)])  58.2 us
    pallas_call x11, Pallas kernels, call(): pl.pallas_call(body, grid_spec=spec, out_shape=out_shape, input_output_al...  32.7 us
    all_to_all x1, blocking collectives, run(): lax.all_to_all(back_one.reshape(NROW, MB, HALF), 'row', 0, 0, tiled=True)  14.6 us
    all_to_all x1, starting transfers between devices, run(): second = lax.all_to_all(first, 'row', 0, 0, tiled=True).reshape(NB, HALF)  7.61 us
    all_to_all x1, waiting for transfers between devices, run(): second = lax.all_to_all(first, 'row', 0, 0, tiled=True).reshape(NB, HALF)  4.89 us
    ppermute x4, starting transfers between devices, swap(): return lax.ppermute(x, 'ylo', SWAP)  4.62 us
  transfers between devices with their start and end apart: 35, of which 16 were waited for; matrix products, arithmetic and copies ran while one was open for 4% of the time, Pallas kernels for 10%

profile of v1, /device:TPU:2, one launch (start us, length us, event | category | flops | bytes accessed | tf_op | source)
XLA Modules:
  0.0 195.5 jit_solution(11960060304326788208)
XLA Ops:
  7.7 4.4 %shard_map.68 = (bf16[2,8,16,640]{3,2,1,0:T(8,128)(2,1)}, bf16[2,8,16,640]{3,2,1,0:T(8,128)(2,1)}) custom-call(s32[2]{0:T(128)S(1)} %pad_add_fusion._, bf16[2,40,40,640]{3,2,1,0:T(8,128)(2,1)} %here.7, bf16[512,320]{1,0:T(8,128)(2,1)S(1)} %get-tuple-element.36.km), custom_call_target="tpu_custom_call" | custom-call | flops 209715200 | bytes 2211840 | tf_op jit(solution)/shard_map/pallas_call | solution.py:44
  12.1 5.9 %collective-permute-start.12 = (bf16[2,8,16,640]{3,2,1,0:T(8,128)(2,1)}, bf16[2,8,16,640]{3,2,1,0:T(8,128)(2,1)}, u32[]{:S(2)}, u32[]{:S(2)}) collective-permute-start(bf16[2,8,16,640]{3,2,1,0:T(8,128)(2,1)} %get-tuple-element.41), channel_id=1, source_target_pairs={{0,14},{2,0},{4,2},{6,4},{8,6},{10,8},{12,10},{14,12},{1,15},{3,1}... | collective-permute-start | bytes 983048 | tf_op jit(solution)/shard_map/ppermute | solution.py:279
  20.0 5.0 %shard_map.67 = (bf16[2,8,16,640]{3,2,1,0:T(8,128)(2,1)}, bf16[2,8,16,640]{3,2,1,0:T(8,128)(2,1)}, bf16[2,8,16,640]{3,2,1,0:T(8,128)(2,1)}, bf16[2,8,16,640]{3,2...) custom-call(s32[2]{0:T(128)S(1)} %pad_add_fusion._, bf16[2,40,40,640]{3,2,1,0:T(8,128)(2,1)} %here.7, ...), custom_call_target="tpu_custom_call" | custom-call | flops 629145600 | bytes 2211840 | tf_op jit(solution)/shard_map/pallas_call | solution.py:44
  26.6 3.6 %collective-permute-start.13 = (bf16[2,8,16,640]{3,2,1,0:T(8,128)(2,1)S(1)}, bf16[2,8,16,640]{3,2,1,0:T(8,128)(2,1)S(1)}, u32[]{:S(2)}, u32[]{:S(2)}) collective-permute-start(bf16[2,8,16,640]{3,2,1,0:T(8,128)(2,1)S(1)} %add_convert_fusion.3), channel_id=1, source_target_pairs={{0,14},{2,0},{4,2},{6,4},{8,6},{10,8},{12,10},{14,12},{1,15},{3,1}... | collective-permute-start | bytes 983048 | tf_op jit(solution)/shard_map/ppermute | solution.py:279
  31.7 4.6 %collective-permute-done.13 = bf16[2,8,16,640]{3,2,1,0:T(8,128)(2,1)S(1)} collective-permute-done((bf16[2,8,16,640]{3,2,1,0:T(8,128)(2,1)S(1)}, bf16[2,8,16,640]{3,2,1,0:T(8,128)(2,1)S(1)}, u32[]{:S(2)}, u32[]{:S(2)}) %collective-permute-start.13) | collective-permute-done | bytes 327712 | tf_op jit(solution)/shard_map/ppermute | solution.py:279
  36.4 3.8 %collective-permute-start.14 = (bf16[2,8,16,640]{3,2,1,0:T(8,128)(2,1)S(1)}, bf16[2,8,16,640]{3,2,1,0:T(8,128)(2,1)S(1)}, u32[]{:S(2)}, u32[]{:S(2)}) collective-permute-start(bf16[2,8,16,640]{3,2,1,0:T(8,128)(2,1)S(1)} %add_convert_fusion.2), channel_id=1, source_target_pairs={{0,14},{2,0},{4,2},{6,4},{8,6},{10,8},{12,10},{14,12},{1,15},{3,1}... | collective-permute-start | bytes 983048 | tf_op jit(solution)/shard_map/ppermute | solution.py:279
  41.4 4.0 %collective-permute-done.14 = bf16[2,8,16,640]{3,2,1,0:T(8,128)(2,1)S(1)} collective-permute-done((bf16[2,8,16,640]{3,2,1,0:T(8,128)(2,1)S(1)}, bf16[2,8,16,640]{3,2,1,0:T(8,128)(2,1)S(1)}, u32[]{:S(2)}, u32[]{:S(2)}) %collective-permute-start.14) | collective-permute-done | bytes 327712 | tf_op jit(solution)/shard_map/ppermute | solution.py:279
  45.5 3.8 %collective-permute-start.15 = (bf16[2,8,16,640]{3,2,1,0:T(8,128)(2,1)S(1)}, bf16[2,8,16,640]{3,2,1,0:T(8,128)(2,1)S(1)}, u32[]{:S(2)}, u32[]{:S(2)}) collective-permute-start(bf16[2,8,16,640]{3,2,1,0:T(8,128)(2,1)S(1)} %add_convert_fusion.1), channel_id=1, source_target_pairs={{0,14},{2,0},{4,2},{6,4},{8,6},{10,8},{12,10},{14,12},{1,15},{3,1}... | collective-permute-start | bytes 983048 | tf_op jit(solution)/shard_map/ppermute | solution.py:279
  49.3 3.5 %shard_map.66 = (bf16[8,24,640]{2,1,0:T(8,128)(2,1)S(1)}, bf16[8,24,640]{2,1,0:T(8,128)(2,1)S(1)}, bf16[8,24,640]{2,1,0:T(8,128)(2,1)S(1)}) custom-call(s32[2]{0:T(128)S(1)} %pad_add_fusion._, bf16[2,40,40,640]{3,2,1,0:T(8,128)(2,1)} %here.7, bf16[40,24,640]{2,1,0:T(8,128)(2,1)S(1)} %collective-permute-done.came, bf16[512,320]{1,0:T(8,128)(2,1)S(1)} %get-tuple-element.36.km, ...), custom_call_target="tpu_custom_call" | custom-call | flops 471859200 | bytes 2990080 | tf_op jit(solution)/shard_map/pallas_call | solution.py:44
  53.0 4.1 %collective-permute-start.6 = (bf16[4,24,640]{2,1,0:T(8,128)(2,1)S(1)}, bf16[4,24,640]{2,1,0:T(8,128)(2,1)S(1)}, u32[]{:S(2)}, u32[]{:S(2)}) collective-permute-start(bf16[4,24,640]{2,1,0:T(8,128)(2,1)S(1)} %get-tuple-element.54), channel_id=1, source_target_pairs={{0,12},{2,14},{4,0},{6,2},{8,4},{10,6},{12,8},{14,10},{1,13},{3,15... | collective-permute-start | bytes 368648 | tf_op jit(solution)/shard_map/ppermute | solution.py:279
  57.1 3.9 %shard_map.65 = (bf16[8,24,640]{2,1,0:T(8,128)(2,1)S(1)}, bf16[8,24,640]{2,1,0:T(8,128)(2,1)S(1)}, bf16[8,24,640]{2,1,0:T(8,128)(2,1)S(1)}, bf16[8,24,640]{2,1,0:T(8,128)(2,1)S(1)}, bf16[8,24,640]{2,1,0:T(8,128)(2,1)S(1)}) custom-call(s32[2]{0:T(128)S(1)} %pad_add_fusion._, bf16[2,40,40,640]{3,2,1,0:T(8,128)(2,1)} %here.7, ...), custom_call_target="tpu_custom_call" | custom-call | flops 786432000 | bytes 2990080 | tf_op jit(solution)/shard_map/pallas_call | solution.py:44
  64.8 4.3 %collective-permute-done.5 = bf16[8,24,640]{2,1,0:T(8,128)(2,1)S(1)} collective-permute-done((bf16[8,24,640]{2,1,0:T(8,128)(2,1)S(1)}, bf16[8,24,640]{2,1,0:T(8,128)(2,1)S(1)}, u32[]{:S(2)}, u32[]{:S(2)}) %collective-permute-start.5) | collective-permute-done | bytes 245792 | tf_op jit(solution)/shard_map/ppermute | solution.py:279
  69.2 3.8 %collective-permute-start.7 = (bf16[8,24,640]{2,1,0:T(8,128)(2,1)S(1)}, bf16[8,24,640]{2,1,0:T(8,128)(2,1)S(1)}, u32[]{:S(2)}, u32[]{:S(2)}) collective-permute-start(bf16[8,24,640]{2,1,0:T(8,128)(2,1)S(1)} %add_convert_fusion.8), channel_id=1, source_target_pairs={{0,14},{2,0},{4,2},{6,4},{8,6},{10,8},{12,10},{14,12},{1,15},{3,1}... | collective-permute-start | bytes 737288 | tf_op jit(solution)/shard_map/ppermute | solution.py:279
  74.8 4.0 %collective-permute-done.7 = bf16[8,24,640]{2,1,0:T(8,128)(2,1)S(1)} collective-permute-done((bf16[8,24,640]{2,1,0:T(8,128)(2,1)S(1)}, bf16[8,24,640]{2,1,0:T(8,128)(2,1)S(1)}, u32[]{:S(2)}, u32[]{:S(2)}) %collective-permute-start.7) | collective-permute-done | bytes 245792 | tf_op jit(solution)/shard_map/ppermute | solution.py:279
  78.9 3.8 %collective-permute-start.8 = (bf16[8,24,640]{2,1,0:T(8,128)(2,1)S(1)}, bf16[8,24,640]{2,1,0:T(8,128)(2,1)S(1)}, u32[]{:S(2)}, u32[]{:S(2)}) collective-permute-start(bf16[8,24,640]{2,1,0:T(8,128)(2,1)S(1)} %add_convert_fusion.7), channel_id=1, source_target_pairs={{0,14},{2,0},{4,2},{6,4},{8,6},{10,8},{12,10},{14,12},{1,15},{3,1}... | collective-permute-start | bytes 737288 | tf_op jit(solution)/shard_map/ppermute | solution.py:279
  83.0 3.4 %collective-permute-done.8 = bf16[8,24,640]{2,1,0:T(8,128)(2,1)S(1)} collective-permute-done((bf16[8,24,640]{2,1,0:T(8,128)(2,1)S(1)}, bf16[8,24,640]{2,1,0:T(8,128)(2,1)S(1)}, u32[]{:S(2)}, u32[]{:S(2)}) %collective-permute-start.8) | collective-permute-done | bytes 245792 | tf_op jit(solution)/shard_map/ppermute | solution.py:279
  88.1 7.6 %all-to-all-start = ((bf16[16,40,288]{2,1,0:T(8,128)(2,1)}), bf16[16,40,288]{2,1,0:T(8,128)(2,1)S(1)}, u32[]{:S(2)}, u32[]{:S(2)}) async-start(bf16[16,40,288]{2,1,0:T(8,128)(2,1)} %shard_map.69), calls=%async_computation | async-start | bytes 983040 | tf_op jit(solution)/shard_map/all_to_all | solution.py:369
  99.3 4.9 %all-to-all-done = bf16[16,40,288]{2,1,0:T(8,128)(2,1)S(1)} async-done(((bf16[16,40,288]{2,1,0:T(8,128)(2,1)}), bf16[16,40,288]{2,1,0:T(8,128)(2,1)S(1)}, u32[]{:S(2)}, u32[]{:S(2)}) %all-to-all-start) | async-done | bytes 368672 | tf_op jit(solution)/shard_map/all_to_all | solution.py:369
  105.3 14.6 %all_to_all.10.x = bf16[16,40,288]{2,1,0:T(8,128)(2,1)S(1)} all-to-all(bf16[16,40,288]{2,1,0:T(8,128)(2,1)S(1)} %bitcast.33), channel_id=1, replica_groups=mesh['row'=16,'z'=8,'ylo'=2] {'row'}, dimensions={0} | all-to-all | bytes 737280 | tf_op jit(solution)/shard_map/all_to_all | solution.py:371
  120.7 3.8 %collective-permute-start.17 = (bf16[8,24,640]{2,1,0:T(8,128)(2,1)S(1)}, bf16[8,24,640]{2,1,0:T(8,128)(2,1)S(1)}, u32[]{:S(2)}, u32[]{:S(2)}) collective-permute-start(bf16[8,24,640]{2,1,0:T(8,128)(2,1)S(1)} %get-tuple-element.45.refs_6_), channel_id=1, source_target_pairs={{0,14},{2,0},{4,2},{6,4},{8,6},{10,8},{12,10},{14,12},{1,15},{3,1}... | collective-permute-start | bytes 737288 | tf_op jit(solution)/shard_map/ppermute | solution.py:279
  124.4 6.4 %collective-permute-done.20.refs_5_ = bf16[8,24,640]{2,1,0:T(8,128)(2,1)S(1)} collective-permute-done((bf16[8,24,640]{2,1,0:T(8,128)(2,1)S(1)}, bf16[8,24,640]{2,1,0:T(8,128)(2,1)S(1)}, u32[]{:S(2)}, u32[]{:S(2)}) %collective-permute-start.20) | collective-permute-done | bytes 245792 | tf_op jit(solution)/shard_map/ppermute | solution.py:279
  130.8 3.6 %collective-permute-start.18 = (bf16[8,24,640]{2,1,0:T(8,128)(2,1)S(1)}, bf16[8,24,640]{2,1,0:T(8,128)(2,1)S(1)}, u32[]{:S(2)}, u32[]{:S(2)}) collective-permute-start(bf16[8,24,640]{2,1,0:T(8,128)(2,1)S(1)} %collective-permute-done.17.refs_7_), channel_id=1, source_target_pairs={{0,14},{2,0},{4,2},{6,4},{8,6},{10,8},{12,10},{14,12},{1,15},{3,1}... | collective-permute-start | bytes 737288 | tf_op jit(solution)/shard_map/ppermute | solution.py:279
  135.1 4.9 %collective-permute-done.21.refs_4_ = bf16[8,24,640]{2,1,0:T(8,128)(2,1)S(1)} collective-permute-done((bf16[8,24,640]{2,1,0:T(8,128)(2,1)S(1)}, bf16[8,24,640]{2,1,0:T(8,128)(2,1)S(1)}, u32[]{:S(2)}, u32[]{:S(2)}) %collective-permute-start.21) | collective-permute-done | bytes 245792 | tf_op jit(solution)/shard_map/ppermute | solution.py:279
  140.0 3.6 %collective-permute-start.19 = (bf16[8,24,640]{2,1,0:T(8,128)(2,1)S(1)}, bf16[8,24,640]{2,1,0:T(8,128)(2,1)S(1)}, u32[]{:S(2)}, u32[]{:S(2)}) collective-permute-start(bf16[8,24,640]{2,1,0:T(8,128)(2,1)S(1)} %collective-permute-done.18.refs_8_), channel_id=1, source_target_pairs={{0,14},{2,0},{4,2},{6,4},{8,6},{10,8},{12,10},{14,12},{1,15},{3,1}... | collective-permute-start | bytes 737288 | tf_op jit(solution)/shard_map/ppermute | solution.py:279
  143.7 4.2 %collective-permute-start.23 = (bf16[4,24,640]{2,1,0:T(8,128)(2,1)S(1)}, bf16[4,24,640]{2,1,0:T(8,128)(2,1)S(1)}, u32[]{:S(2)}, u32[]{:S(2)}) collective-permute-start(bf16[4,24,640]{2,1,0:T(8,128)(2,1)S(1)} %slice.45), channel_id=1, source_target_pairs={{0,12},{2,14},{4,0},{6,2},{8,4},{10,6},{12,8},{14,10},{1,13},{3,15... | collective-permute-start | bytes 368648 | tf_op jit(solution)/shard_map/ppermute | solution.py:279
  148.1 5.0 %collective-permute-done.22.refs_1_ = bf16[4,24,640]{2,1,0:T(8,128)(2,1)S(1)} collective-permute-done((bf16[4,24,640]{2,1,0:T(8,128)(2,1)S(1)}, bf16[4,24,640]{2,1,0:T(8,128)(2,1)S(1)}, u32[]{:S(2)}, u32[]{:S(2)}) %collective-permute-start.22) | collective-permute-done | bytes 122912 | tf_op jit(solution)/shard_map/ppermute | solution.py:279
  156.2 3.8 %shard_map.72 = (bf16[40,24,640]{2,1,0:T(8,128)(2,1)S(1)}, bf16[2,40,40,640]{3,2,1,0:T(8,128)(2,1)}) custom-call(s32[2]{0:T(128)S(1)} %pad_add_fusion._, bf16[8,24,640]{2,1,0:T(8,128)(2,1)S(1)} %collective-permute-done.19.refs_0_, bf16[4,24,640]{2,1,0:T(8,128)(2,1)S(1)} %collective-permute-done.22.refs_1_, ...), custom_call_target="tpu_custom_call" | custom-call | flops 1258291200 | bytes 1310720 | tf_op jit(solution)/shard_map/pallas_call | solution.py:44
  160.7 3.6 %collective-permute-start.28 = (bf16[2,8,16,640]{3,2,1,0:T(8,128)(2,1)S(1)}, bf16[2,8,16,640]{3,2,1,0:T(8,128)(2,1)S(1)}, u32[]{:S(2)}, u32[]{:S(2)}) collective-permute-start(bf16[2,8,16,640]{3,2,1,0:T(8,128)(2,1)S(1)} %collective-permute-done.27.refs_6_), channel_id=1, source_target_pairs={{0,14},{2,0},{4,2},{6,4},{8,6},{10,8},{12,10},{14,12},{1,15},{3,1}... | collective-permute-start | bytes 983048 | tf_op jit(solution)/shard_map/ppermute | solution.py:279
  164.2 5.1 %collective-permute-done.31.refs_4_ = bf16[2,8,16,640]{3,2,1,0:T(8,128)(2,1)S(1)} collective-permute-done((bf16[2,8,16,640]{3,2,1,0:T(8,128)(2,1)S(1)}, bf16[2,8,16,640]{3,2,1,0:T(8,128)(2,1)S(1)}, u32[]{:S(2)}, u32[]{:S(2)}) %collective-permute-start.31) | collective-permute-done | bytes 327712 | tf_op jit(solution)/shard_map/ppermute | solution.py:279
  173.7 7.7 %collective-permute-done.32.refs_3_ = bf16[2,8,16,640]{3,2,1,0:T(8,128)(2,1)S(1)} collective-permute-done((bf16[2,8,16,640]{3,2,1,0:T(8,128)(2,1)S(1)}, bf16[2,8,16,640]{3,2,1,0:T(8,128)(2,1)S(1)}, u32[]{:S(2)}, u32[]{:S(2)}) %collective-permute-start.32) | collective-permute-done | bytes 327712 | tf_op jit(solution)/shard_map/ppermute | solution.py:279
  184.6 5.0 %collective-permute-done.33.refs_2_ = bf16[2,8,16,640]{3,2,1,0:T(8,128)(2,1)S(1)} collective-permute-done((bf16[2,8,16,640]{3,2,1,0:T(8,128)(2,1)S(1)}, bf16[2,8,16,640]{3,2,1,0:T(8,128)(2,1)S(1)}, u32[]{:S(2)}, u32[]{:S(2)}) %collective-permute-start.33) | collective-permute-done | bytes 327712 | tf_op jit(solution)/shard_map/ppermute | solution.py:279
  189.6 3.7 %shard_map.73.__ = bf16[2,40,40,640]{3,2,1,0:T(8,128)(2,1)} custom-call(s32[2]{0:T(128)S(1)} %pad_add_fusion._, bf16[2,8,16,640]{3,2,1,0:T(8,128)(2,1)S(1)} %collective-permute-done.29.refs_0_, bf16[2,8,16,640]{3,2,1,0:T(8,128)(2,1)S(1)} %collective-permute-done.30.refs_1_, ...), custom_call_target="tpu_custom_call", output_to_operand_aliasing={{}: (10, {})} | custom-call | flops 838860800 | bytes 3522560 | tf_op jit(solution)/shard_map/pallas_call | solution.py:44
  (113 shorter events, 41.5 us)
Async XLA Ops:
  12.1 13.1 %collective-permute-start.12 = (bf16[2,8,16,640]{3,2,1,0:T(8,128)(2,1)}, bf16[2,8,16,640]{3,2,1,0:T(8,128)(2,1)}, u32[]{:S(2)}, u32[]{:S(2)}) collective-permute-start(bf16[2,8,16,640]{3,2,1,0:T(8,128)(2,1)} %get-tuple-element.41), channel_id=1, source_target_pairs={{0,14},{2,0},{4,2},{6,4},{8,6},{10,8},{12,10},{14,12},{1,15},{3,1}... | collective-permute-start | bytes 983048 | tf_op jit(solution)/shard_map/ppermute | solution.py:279
  18.0 12.5 %collective-permute-start.9 = (bf16[2,8,16,640]{3,2,1,0:T(8,128)(2,1)}, bf16[2,8,16,640]{3,2,1,0:T(8,128)(2,1)}, u32[]{:S(2)}, u32[]{:S(2)}) collective-permute-start(bf16[2,8,16,640]{3,2,1,0:T(8,128)(2,1)} %get-tuple-element.38), channel_id=1, source_target_pairs={{0,2},{2,4},{4,6},{6,8},{8,10},{10,12},{12,14},{14,0},{1,3},{3,5},... | collective-permute-start | bytes 983048 | tf_op jit(solution)/shard_map/ppermute | solution.py:279
  18.0 31.3 %collective-permute-start = (bf16[40,24,640]{2,1,0:T(8,128)(2,1)}, bf16[40,24,640]{2,1,0:T(8,128)(2,1)S(1)}, u32[]{:S(2)}, u32[]{:S(2)}) collective-permute-start(bf16[40,24,640]{2,1,0:T(8,128)(2,1)} %shard_map.64), channel_id=1, source_target_pairs={{0,1},{1,0},{2,3},{3,2},{4,5},{5,4},{6,7},{7,6},{8,9},{9,8},{10,11... | collective-permute-start | bytes 3686408 | tf_op jit(solution)/shard_map/ppermute | solution.py:283
  26.6 9.8 %collective-permute-start.13 = (bf16[2,8,16,640]{3,2,1,0:T(8,128)(2,1)S(1)}, bf16[2,8,16,640]{3,2,1,0:T(8,128)(2,1)S(1)}, u32[]{:S(2)}, u32[]{:S(2)}) collective-permute-start(bf16[2,8,16,640]{3,2,1,0:T(8,128)(2,1)S(1)} %add_convert_fusion.3), channel_id=1, source_target_pairs={{0,14},{2,0},{4,2},{6,4},{8,6},{10,8},{12,10},{14,12},{1,15},{3,1}... | collective-permute-start | bytes 983048 | tf_op jit(solution)/shard_map/ppermute | solution.py:279
  31.6 9.6 %collective-permute-start.10 = (bf16[2,8,16,640]{3,2,1,0:T(8,128)(2,1)S(1)}, bf16[2,8,16,640]{3,2,1,0:T(8,128)(2,1)S(1)}, u32[]{:S(2)}, u32[]{:S(2)}) collective-permute-start(bf16[2,8,16,640]{3,2,1,0:T(8,128)(2,1)S(1)} %add_convert_fusion.5), channel_id=1, source_target_pairs={{0,2},{2,4},{4,6},{6,8},{8,10},{10,12},{12,14},{14,0},{1,3},{3,5},... | collective-permute-start | bytes 983048 | tf_op jit(solution)/shard_map/ppermute | solution.py:279
  36.4 9.0 %collective-permute-start.14 = (bf16[2,8,16,640]{3,2,1,0:T(8,128)(2,1)S(1)}, bf16[2,8,16,640]{3,2,1,0:T(8,128)(2,1)S(1)}, u32[]{:S(2)}, u32[]{:S(2)}) collective-permute-start(bf16[2,8,16,640]{3,2,1,0:T(8,128)(2,1)S(1)} %add_convert_fusion.2), channel_id=1, source_target_pairs={{0,14},{2,0},{4,2},{6,4},{8,6},{10,8},{12,10},{14,12},{1,15},{3,1}... | collective-permute-start | bytes 983048 | tf_op jit(solution)/shard_map/ppermute | solution.py:279
  41.3 19.8 %collective-permute-start.11 = (bf16[2,8,16,640]{3,2,1,0:T(8,128)(2,1)S(1)}, bf16[2,8,16,640]{3,2,1,0:T(8,128)(2,1)S(1)}, u32[]{:S(2)}, u32[]{:S(2)}) collective-permute-start(bf16[2,8,16,640]{3,2,1,0:T(8,128)(2,1)S(1)} %add_convert_fusion.4), channel_id=1, source_target_pairs={{0,2},{2,4},{4,6},{6,8},{8,10},{10,12},{12,14},{14,0},{1,3},{3,5},... | collective-permute-start | bytes 983048 | tf_op jit(solution)/shard_map/ppermute | solution.py:279
  45.5 18.9 %collective-permute-start.15 = (bf16[2,8,16,640]{3,2,1,0:T(8,128)(2,1)S(1)}, bf16[2,8,16,640]{3,2,1,0:T(8,128)(2,1)S(1)}, u32[]{:S(2)}, u32[]{:S(2)}) collective-permute-start(bf16[2,8,16,640]{3,2,1,0:T(8,128)(2,1)S(1)} %add_convert_fusion.1), channel_id=1, source_target_pairs={{0,14},{2,0},{4,2},{6,4},{8,6},{10,8},{12,10},{14,12},{1,15},{3,1}... | collective-permute-start | bytes 983048 | tf_op jit(solution)/shard_map/ppermute | solution.py:279
  52.9 11.6 %collective-permute-start.2 = (bf16[4,24,640]{2,1,0:T(8,128)(2,1)S(1)}, bf16[4,24,640]{2,1,0:T(8,128)(2,1)S(1)}, u32[]{:S(2)}, u32[]{:S(2)}) collective-permute-start(bf16[4,24,640]{2,1,0:T(8,128)(2,1)S(1)} %get-tuple-element.53), channel_id=1, source_target_pairs={{0,4},{2,6},{4,8},{6,10},{8,12},{10,14},{12,0},{14,2},{1,5},{3,7},... | collective-permute-start | bytes 368648 | tf_op jit(solution)/shard_map/ppermute | solution.py:279
  53.0 11.8 %collective-permute-start.6 = (bf16[4,24,640]{2,1,0:T(8,128)(2,1)S(1)}, bf16[4,24,640]{2,1,0:T(8,128)(2,1)S(1)}, u32[]{:S(2)}, u32[]{:S(2)}) collective-permute-start(bf16[4,24,640]{2,1,0:T(8,128)(2,1)S(1)} %get-tuple-element.54), channel_id=1, source_target_pairs={{0,12},{2,14},{4,0},{6,2},{8,4},{10,6},{12,8},{14,10},{1,13},{3,15... | collective-permute-start | bytes 368648 | tf_op jit(solution)/shard_map/ppermute | solution.py:279
  61.1 8.0 %collective-permute-start.5 = (bf16[8,24,640]{2,1,0:T(8,128)(2,1)S(1)}, bf16[8,24,640]{2,1,0:T(8,128)(2,1)S(1)}, u32[]{:S(2)}, u32[]{:S(2)}) collective-permute-start(bf16[8,24,640]{2,1,0:T(8,128)(2,1)S(1)} %get-tuple-element.33), channel_id=1, source_target_pairs={{0,14},{2,0},{4,2},{6,4},{8,6},{10,8},{12,10},{14,12},{1,15},{3,1}... | collective-permute-start | bytes 737288 | tf_op jit(solution)/shard_map/ppermute | solution.py:279
  64.7 10.0 %collective-permute-start.3 = (bf16[8,24,640]{2,1,0:T(8,128)(2,1)S(1)}, bf16[8,24,640]{2,1,0:T(8,128)(2,1)S(1)}, u32[]{:S(2)}, u32[]{:S(2)}) collective-permute-start(bf16[8,24,640]{2,1,0:T(8,128)(2,1)S(1)} %add_convert_fusion.10), channel_id=1, source_target_pairs={{0,2},{2,4},{4,6},{6,8},{8,10},{10,12},{12,14},{14,0},{1,3},{3,5},... | collective-permute-start | bytes 737288 | tf_op jit(solution)/shard_map/ppermute | solution.py:279
  69.2 9.7 %collective-permute-start.7 = (bf16[8,24,640]{2,1,0:T(8,128)(2,1)S(1)}, bf16[8,24,640]{2,1,0:T(8,128)(2,1)S(1)}, u32[]{:S(2)}, u32[]{:S(2)}) collective-permute-start(bf16[8,24,640]{2,1,0:T(8,128)(2,1)S(1)} %add_convert_fusion.8), channel_id=1, source_target_pairs={{0,14},{2,0},{4,2},{6,4},{8,6},{10,8},{12,10},{14,12},{1,15},{3,1}... | collective-permute-start | bytes 737288 | tf_op jit(solution)/shard_map/ppermute | solution.py:279
  73.0 9.9 %collective-permute-start.16 = (bf16[8,16,640]{2,1,0:T(8,128)(2,1)S(1)}, bf16[8,16,640]{2,1,0:T(8,128)(2,1)S(1)}, u32[]{:S(2)}, u32[]{:S(2)}) collective-permute-start(bf16[8,16,640]{2,1,0:T(8,128)(2,1)S(1)} %slice_bitcast_fusion.2), channel_id=1, source_target_pairs={{0,1},{1,0},{2,3},{3,2},{4,5},{5,4},{6,7},{7,6},{8,9},{9,8},{10,11... | collective-permute-start | bytes 491528 | tf_op jit(solution)/shard_map/ppermute | solution.py:283
  74.7 8.2 %collective-permute-start.4 = (bf16[8,24,640]{2,1,0:T(8,128)(2,1)S(1)}, bf16[8,24,640]{2,1,0:T(8,128)(2,1)S(1)}, u32[]{:S(2)}, u32[]{:S(2)}) collective-permute-start(bf16[8,24,640]{2,1,0:T(8,128)(2,1)S(1)} %add_convert_fusion.9), channel_id=1, source_target_pairs={{0,2},{2,4},{4,6},{6,8},{8,10},{10,12},{12,14},{14,0},{1,3},{3,5},... | collective-permute-start | bytes 737288 | tf_op jit(solution)/shard_map/ppermute | solution.py:279
  88.1 16.0 %all-to-all-start = ((bf16[16,40,288]{2,1,0:T(8,128)(2,1)}), bf16[16,40,288]{2,1,0:T(8,128)(2,1)S(1)}, u32[]{:S(2)}, u32[]{:S(2)}) async-start(bf16[16,40,288]{2,1,0:T(8,128)(2,1)} %shard_map.69), calls=%async_computation | async-start | bytes 983040 | tf_op jit(solution)/shard_map/all_to_all | solution.py:369
  120.6 10.2 %collective-permute-start.20 = (bf16[8,24,640]{2,1,0:T(8,128)(2,1)S(1)}, bf16[8,24,640]{2,1,0:T(8,128)(2,1)S(1)}, u32[]{:S(2)}, u32[]{:S(2)}) collective-permute-start(bf16[8,24,640]{2,1,0:T(8,128)(2,1)S(1)} %get-tuple-element.45.refs_6_), channel_id=1, source_target_pairs={{0,2},{2,4},{4,6},{6,8},{8,10},{10,12},{12,14},{14,0},{1,3},{3,5},... | collective-permute-start | bytes 737288 | tf_op jit(solution)/shard_map/ppermute | solution.py:279
  120.7 10.2 %collective-permute-start.17 = (bf16[8,24,640]{2,1,0:T(8,128)(2,1)S(1)}, bf16[8,24,640]{2,1,0:T(8,128)(2,1)S(1)}, u32[]{:S(2)}, u32[]{:S(2)}) collective-permute-start(bf16[8,24,640]{2,1,0:T(8,128)(2,1)S(1)} %get-tuple-element.45.refs_6_), channel_id=1, source_target_pairs={{0,14},{2,0},{4,2},{6,4},{8,6},{10,8},{12,10},{14,12},{1,15},{3,1}... | collective-permute-start | bytes 737288 | tf_op jit(solution)/shard_map/ppermute | solution.py:279
  130.8 9.2 %collective-permute-start.21 = (bf16[8,24,640]{2,1,0:T(8,128)(2,1)S(1)}, bf16[8,24,640]{2,1,0:T(8,128)(2,1)S(1)}, u32[]{:S(2)}, u32[]{:S(2)}) collective-permute-start(bf16[8,24,640]{2,1,0:T(8,128)(2,1)S(1)} %collective-permute-done.20.refs_5_), channel_id=1, source_target_pairs={{0,2},{2,4},{4,6},{6,8},{8,10},{10,12},{12,14},{14,0},{1,3},{3,5},... | collective-permute-start | bytes 737288 | tf_op jit(solution)/shard_map/ppermute | solution.py:279
  130.8 9.2 %collective-permute-start.18 = (bf16[8,24,640]{2,1,0:T(8,128)(2,1)S(1)}, bf16[8,24,640]{2,1,0:T(8,128)(2,1)S(1)}, u32[]{:S(2)}, u32[]{:S(2)}) collective-permute-start(bf16[8,24,640]{2,1,0:T(8,128)(2,1)S(1)} %collective-permute-done.17.refs_7_), channel_id=1, source_target_pairs={{0,14},{2,0},{4,2},{6,4},{8,6},{10,8},{12,10},{14,12},{1,15},{3,1}... | collective-permute-start | bytes 737288 | tf_op jit(solution)/shard_map/ppermute | solution.py:279
  134.4 13.5 %collective-permute-start.26 = (bf16[8,16,640]{2,1,0:T(8,128)(2,1)S(1)}, bf16[8,16,640]{2,1,0:T(8,128)(2,1)S(1)}, u32[]{:S(2)}, u32[]{:S(2)}) collective-permute-start(bf16[8,16,640]{2,1,0:T(8,128)(2,1)S(1)} %get-tuple-element.47), channel_id=1, source_target_pairs={{0,1},{1,0},{2,3},{3,2},{4,5},{5,4},{6,7},{7,6},{8,9},{9,8},{10,11... | collective-permute-start | bytes 491528 | tf_op jit(solution)/shard_map/ppermute | solution.py:283
  140.0 15.2 %collective-permute-start.24 = (bf16[8,24,640]{2,1,0:T(8,128)(2,1)S(1)}, bf16[8,24,640]{2,1,0:T(8,128)(2,1)S(1)}, u32[]{:S(2)}, u32[]{:S(2)}) collective-permute-start(bf16[8,24,640]{2,1,0:T(8,128)(2,1)S(1)} %collective-permute-done.21.refs_4_), channel_id=1, source_target_pairs={{0,2},{2,4},{4,6},{6,8},{8,10},{10,12},{12,14},{14,0},{1,3},{3,5},... | collective-permute-start | bytes 737288 | tf_op jit(solution)/shard_map/ppermute | solution.py:279
  140.0 15.2 %collective-permute-start.19 = (bf16[8,24,640]{2,1,0:T(8,128)(2,1)S(1)}, bf16[8,24,640]{2,1,0:T(8,128)(2,1)S(1)}, u32[]{:S(2)}, u32[]{:S(2)}) collective-permute-start(bf16[8,24,640]{2,1,0:T(8,128)(2,1)S(1)} %collective-permute-done.18.refs_8_), channel_id=1, source_target_pairs={{0,14},{2,0},{4,2},{6,4},{8,6},{10,8},{12,10},{14,12},{1,15},{3,1}... | collective-permute-start | bytes 737288 | tf_op jit(solution)/shard_map/ppermute | solution.py:279
  143.6 9.5 %collective-permute-start.22 = (bf16[4,24,640]{2,1,0:T(8,128)(2,1)S(1)}, bf16[4,24,640]{2,1,0:T(8,128)(2,1)S(1)}, u32[]{:S(2)}, u32[]{:S(2)}) collective-permute-start(bf16[4,24,640]{2,1,0:T(8,128)(2,1)S(1)} %slice.44), channel_id=1, source_target_pairs={{0,4},{2,6},{4,8},{6,10},{8,12},{10,14},{12,0},{14,2},{1,5},{3,7},... | collective-permute-start | bytes 368648 | tf_op jit(solution)/shard_map/ppermute | solution.py:279
  143.7 11.5 %collective-permute-start.23 = (bf16[4,24,640]{2,1,0:T(8,128)(2,1)S(1)}, bf16[4,24,640]{2,1,0:T(8,128)(2,1)S(1)}, u32[]{:S(2)}, u32[]{:S(2)}) collective-permute-start(bf16[4,24,640]{2,1,0:T(8,128)(2,1)S(1)} %slice.45), channel_id=1, source_target_pairs={{0,12},{2,14},{4,0},{6,2},{8,4},{10,6},{12,8},{14,10},{1,13},{3,15... | collective-permute-start | bytes 368648 | tf_op jit(solution)/shard_map/ppermute | solution.py:279
  148.0 12.7 %collective-permute-start.27 = (bf16[2,8,16,640]{3,2,1,0:T(8,128)(2,1)S(1)}, bf16[2,8,16,640]{3,2,1,0:T(8,128)(2,1)S(1)}, u32[]{:S(2)}, u32[]{:S(2)}) collective-permute-start(bf16[2,8,16,640]{3,2,1,0:T(8,128)(2,1)S(1)} %pad_maximum_fusion.2.refs_5_), channel_id=1, source_target_pairs={{0,14},{2,0},{4,2},{6,4},{8,6},{10,8},{12,10},{14,12},{1,15},{3,1}... | collective-permute-start | bytes 983048 | tf_op jit(solution)/shard_map/ppermute | solution.py:279
  160.0 33.3 %collective-permute-start.25 = (bf16[40,24,640]{2,1,0:T(8,128)(2,1)S(1)}, bf16[40,24,640]{2,1,0:T(8,128)(2,1)S(1)}, u32[]{:S(2)}, u32[]{:S(2)}) collective-permute-start(bf16[40,24,640]{2,1,0:T(8,128)(2,1)S(1)} %get-tuple-element.46), channel_id=1, source_target_pairs={{0,1},{1,0},{2,3},{3,2},{4,5},{5,4},{6,7},{7,6},{8,9},{9,8},{10,11... | collective-permute-start | bytes 3686408 | tf_op jit(solution)/shard_map/ppermute | solution.py:283
  160.7 8.7 %collective-permute-start.31 = (bf16[2,8,16,640]{3,2,1,0:T(8,128)(2,1)S(1)}, bf16[2,8,16,640]{3,2,1,0:T(8,128)(2,1)S(1)}, u32[]{:S(2)}, u32[]{:S(2)}) collective-permute-start(bf16[2,8,16,640]{3,2,1,0:T(8,128)(2,1)S(1)} %pad_maximum_fusion.2.refs_5_), channel_id=1, source_target_pairs={{0,2},{2,4},{4,6},{6,8},{8,10},{10,12},{12,14},{14,0},{1,3},{3,5},... | collective-permute-start | bytes 983048 | tf_op jit(solution)/shard_map/ppermute | solution.py:279
  160.7 10.9 %collective-permute-start.28 = (bf16[2,8,16,640]{3,2,1,0:T(8,128)(2,1)S(1)}, bf16[2,8,16,640]{3,2,1,0:T(8,128)(2,1)S(1)}, u32[]{:S(2)}, u32[]{:S(2)}) collective-permute-start(bf16[2,8,16,640]{3,2,1,0:T(8,128)(2,1)S(1)} %collective-permute-done.27.refs_6_), channel_id=1, source_target_pairs={{0,14},{2,0},{4,2},{6,4},{8,6},{10,8},{12,10},{14,12},{1,15},{3,1}... | collective-permute-start | bytes 983048 | tf_op jit(solution)/shard_map/ppermute | solution.py:279
  169.4 12.0 %collective-permute-start.32 = (bf16[2,8,16,640]{3,2,1,0:T(8,128)(2,1)S(1)}, bf16[2,8,16,640]{3,2,1,0:T(8,128)(2,1)S(1)}, u32[]{:S(2)}, u32[]{:S(2)}) collective-permute-start(bf16[2,8,16,640]{3,2,1,0:T(8,128)(2,1)S(1)} %collective-permute-done.31.refs_4_), channel_id=1, source_target_pairs={{0,2},{2,4},{4,6},{6,8},{8,10},{10,12},{12,14},{14,0},{1,3},{3,5},... | collective-permute-start | bytes 983048 | tf_op jit(solution)/shard_map/ppermute | solution.py:279
  171.5 10.5 %collective-permute-start.29 = (bf16[2,8,16,640]{3,2,1,0:T(8,128)(2,1)S(1)}, bf16[2,8,16,640]{3,2,1,0:T(8,128)(2,1)S(1)}, u32[]{:S(2)}, u32[]{:S(2)}) collective-permute-start(bf16[2,8,16,640]{3,2,1,0:T(8,128)(2,1)S(1)} %collective-permute-done.28.refs_7_), channel_id=1, source_target_pairs={{0,14},{2,0},{4,2},{6,4},{8,6},{10,8},{12,10},{14,12},{1,15},{3,1}... | collective-permute-start | bytes 983048 | tf_op jit(solution)/shard_map/ppermute | solution.py:279
  181.3 8.3 %collective-permute-start.33 = (bf16[2,8,16,640]{3,2,1,0:T(8,128)(2,1)S(1)}, bf16[2,8,16,640]{3,2,1,0:T(8,128)(2,1)S(1)}, u32[]{:S(2)}, u32[]{:S(2)}) collective-permute-start(bf16[2,8,16,640]{3,2,1,0:T(8,128)(2,1)S(1)} %collective-permute-done.32.refs_3_), channel_id=1, source_target_pairs={{0,2},{2,4},{4,6},{6,8},{8,10},{10,12},{12,14},{14,0},{1,3},{3,5},... | collective-permute-start | bytes 983048 | tf_op jit(solution)/shard_map/ppermute | solution.py:279
  (15 other events, 248.8 us)

commit v2 on v1

--- a/solution.py
+++ b/solution.py
@@ -75,20 +75,21 @@
 
 
 def lift(slab, pick):
-    step = 20
-
-    def body(_, src, dst):
-        dst[...] = src[0]
-
-    return call(
-        body,
-        (LB // step,),
-        [pl.BlockSpec((1, step, YM, NB), lambda i, s: (s[1], i, 0, 0))],
-        pl.BlockSpec((step, YM, NB), lambda i, s: (i, 0, 0)),
-        jax.ShapeDtypeStruct((LB, YM, NB), BF),
-        (slab,),
-        pick,
-    )
+    def body(which, src, dst, sem):
+        copy = pltpu.make_async_copy(src.at[which[1], :, pl.ds(0, YM), :], dst, sem)
+        copy.start()
+        copy.wait()
+
+    return pl.pallas_call(
+        body,
+        in_specs=[pl.BlockSpec(memory_space=pltpu.SMEM), pl.BlockSpec(memory_space=pltpu.HBM)],
+        out_specs=pl.BlockSpec(memory_space=pltpu.VMEM),
+        out_shape=pltpu.VMEM((LB, YM, NB), BF),
+        scratch_shapes=[pltpu.SemaphoreType.DMA],
+        name="lift",
+        cost_estimate=pl.CostEstimate(flops=0, bytes_accessed=4 * LB * YM * NB, transcendentals=0),
+        compiler_params=pltpu.CompilerParams(vmem_limit_bytes=24 * 1024 * 1024),
+    )(pick, slab)
 
 
 def y_parts(slab, swapped, k_mine, k_other, pick, first, tiles, lo, hi):
@@ -133,7 +134,7 @@
             whole((RW, CL)),
         ],
         [pl.BlockSpec((1, JB, TILE, NB), lambda o, t, s: (o, 0, t, 0))] * (hi - lo),
-        [pltpu.HBM((2, JB, tiles * TILE, NB), BF)] * (hi - lo),
+        [jax.ShapeDtypeStruct((2, JB, tiles * TILE, NB), BF)] * (hi - lo),
         (slab, k_mine),
         pick,
         flops=4 * tiles * (hi - lo) * JB * TILE * CL * NB,
@@ -194,23 +195,27 @@
     )
 
 
-def put(got, out, pick, first, tiles):
-    def body(_, src, __, dst):
-        dst[0] = src[...]
-
-    return call(
-        body,
-        (tiles,),
-        [
-            pl.BlockSpec((LB, TILE, NB), lambda t, s: (0, t, 0)),
-            pl.BlockSpec(memory_space=pl.ANY),
-        ],
-        pl.BlockSpec((1, LB, TILE, NB), lambda t, s: (s[1], 0, first + t, 0)),
-        jax.ShapeDtypeStruct((2, LB, MB, NB), BF),
-        (got, out),
-        pick,
-        {2: 0},
-    )
+def put(got, out, pick):
+    def body(which, src, _, dst, sem):
+        copy = pltpu.make_async_copy(src, dst.at[which[1], :, pl.ds(0, YM), :], sem)
+        copy.start()
+        copy.wait()
+
+    return pl.pallas_call(
+        body,
+        in_specs=[
+            pl.BlockSpec(memory_space=pltpu.SMEM),
+            pl.BlockSpec(memory_space=pltpu.VMEM),
+            pl.BlockSpec(memory_space=pltpu.HBM),
+        ],
+        out_specs=pl.BlockSpec(memory_space=pltpu.HBM),
+        out_shape=jax.ShapeDtypeStruct((2, LB, MB, NB), BF),
+        scratch_shapes=[pltpu.SemaphoreType.DMA],
+        input_output_aliases={2: 0},
+        name="put",
+        cost_estimate=pl.CostEstimate(flops=0, bytes_accessed=4 * LB * YM * NB, transcendentals=0),
+        compiler_params=pltpu.CompilerParams(vmem_limit_bytes=24 * 1024 * 1024),
+    )(pick, got, out)
 
 
 def to_virtual(summed, v_halves):
@@ -351,13 +356,12 @@
     v_halves = jnp.stack([coef_virtual[:, :HALF], coef_virtual[:, HALF:]])
     vt_halves = coef_t.reshape(2, HALF, NB)
 
-    k_mine = spread(coef_occupied.T, zi * 2 * LB + yi * LB, zi)
-    k_other = spread(coef_occupied.T, zi * 2 * LB + (1 - yi) * LB, zi)
-
-    raised, held = lax.optimization_barrier((lift(slab, pick), k_mine))
+    raised, coef_o = lax.optimization_barrier((lift(slab, pick), coef_occupied.T))
     swapped = swap(raised)
-    head = z_parts(slab, held, pick, YT, ZT, 0, 2)
-    tail = z_parts(slab, held, pick, YT, ZT, 2, NZ)
+    k_mine = spread(coef_o, zi * 2 * LB + yi * LB, zi)
+    k_other = spread(coef_o, zi * 2 * LB + (1 - yi) * LB, zi)
+    head = z_parts(slab, k_mine, pick, YT, ZT, 0, 2)
+    tail = z_parts(slab, k_mine, pick, YT, ZT, 2, NZ)
     both = chain_sum(unrolled([*head, *tail]))
     last = add(both[0], swap(both[1]))
     head = y_parts(slab, swapped, k_mine, k_other, pick, 0, YT, 0, 3)
@@ -377,7 +381,7 @@
     got = swap(send)
     both = jnp.stack([wide_z, swap(wide_z)])
     out = z_expand(chain_gather(both), kt_mine, out, pick, YT, ZT)
-    return put(got, out, pick, 0, YT)
+    return put(got, out, pick)
 
 
 def solution(mesh):

time: 198 us -> 196 us (0.990)
  Pallas kernels: 32.7 us -> 30.3 us
    pallas_call x11 -> x9, Pallas kernels: 32.7 us -> 26.9 us  [call(): pl.pallas_call(body, grid_spec=spec, out_shape=out_shape, input_output_al...]
    pallas_call x0 -> x2, Pallas kernels: none -> 3.42 us  [the longest x1 1.84 us: lift(): pl.pallas_call(body, in_specs=[pl.BlockSpec(memory_space=pltpu.SMEM), pl....]
  transfers between devices with their start and end apart: 35 -> 35, of which waited for: 16 -> 17; matrix products, arithmetic and copies ran while one was open for 4% -> 4% of each run, Pallas kernels for 10% -> 10%
where the time goes in v2:
time: 196 us; the launch traced here: 194 us
  starting transfers between devices  72.1 us (37%)
  waiting for transfers between devices  63.6 us (32%)
  Pallas kernels  30.3 us (15%)
  blocking collectives  14.6 us (7%)
  other arithmetic  7.52 us (4%)
  matrix products  2.61 us (1%)
  local copies, waits for them, and re-layouts  2.29 us (1%)
    ppermute x30, starting transfers between devices, move(): return lax.ppermute(x, 'z', [(i, (i + step) % NZ) for i in range(NZ)])  59.9 us
    ppermute x30, waiting for transfers between devices, move(): return lax.ppermute(x, 'z', [(i, (i + step) % NZ) for i in range(NZ)])  58.5 us
    pallas_call x9, Pallas kernels, call(): pl.pallas_call(body, grid_spec=spec, out_shape=out_shape, input_output_al...  26.9 us
    all_to_all x1, blocking collectives, run(): lax.all_to_all(back_one.reshape(NROW, MB, HALF), 'row', 0, 0, tiled=True)  14.6 us
    all_to_all x1, starting transfers between devices, run(): second = lax.all_to_all(first, 'row', 0, 0, tiled=True).reshape(NB, HALF)  7.61 us
    all_to_all x1, waiting for transfers between devices, run(): second = lax.all_to_all(first, 'row', 0, 0, tiled=True).reshape(NB, HALF)  5.05 us
    ppermute x4, starting transfers between devices, swap(): return lax.ppermute(x, 'ylo', SWAP)  4.55 us
  transfers between devices with their start and end apart: 35, of which 17 were waited for; matrix products, arithmetic and copies ran while one was open for 4% of the time, Pallas kernels for 10%

profile of v2, /device:TPU:2, one launch (start us, length us, event | category | flops | bytes accessed | tf_op | source)
XLA Modules:
  0.0 193.6 jit_solution(5131684348814676288)
XLA Ops:
  7.1 4.4 %shard_map.67 = (bf16[2,8,16,640]{3,2,1,0:T(8,128)(2,1)}, bf16[2,8,16,640]{3,2,1,0:T(8,128)(2,1)}) custom-call(s32[2]{0:T(128)S(1)} %pad_add_fusion.which._, bf16[2,40,40,640]{3,2,1,0:T(8,128)(2,1)} %here.7, bf16[512,320]{1,0:T(8,128)(2,1)S(1)} %get-tuple-element.58.km), custom_call_target="tpu_custom_call" | custom-call | flops 209715200 | bytes 2211840 | tf_op jit(solution)/shard_map/pallas_call | solution.py:44
  11.6 5.9 %collective-permute-start.12 = (bf16[2,8,16,640]{3,2,1,0:T(8,128)(2,1)}, bf16[2,8,16,640]{3,2,1,0:T(8,128)(2,1)}, u32[]{:S(2)}, u32[]{:S(2)}) collective-permute-start(bf16[2,8,16,640]{3,2,1,0:T(8,128)(2,1)} %get-tuple-element.41), channel_id=1, source_target_pairs={{0,14},{2,0},{4,2},{6,4},{8,6},{10,8},{12,10},{14,12},{1,15},{3,1}... | collective-permute-start | bytes 983048 | tf_op jit(solution)/shard_map/ppermute | solution.py:284
  19.4 4.1 %shard_map.66 = (bf16[2,8,16,640]{3,2,1,0:T(8,128)(2,1)S(1)}, bf16[2,8,16,640]{3,2,1,0:T(8,128)(2,1)S(1)}, bf16[2,8,16,640]{3,2,1,0:T(8,128)(2,1)S(1)}, bf16[2,8...) custom-call(s32[2]{0:T(128)S(1)} %pad_add_fusion.which._, ...), custom_call_target="tpu_custom_call" | custom-call | flops 629145600 | bytes 2211840 | tf_op jit(solution)/shard_map/pallas_call | solution.py:44
  25.8 3.8 %collective-permute-start.13 = (bf16[2,8,16,640]{3,2,1,0:T(8,128)(2,1)S(1)}, bf16[2,8,16,640]{3,2,1,0:T(8,128)(2,1)S(1)}, u32[]{:S(2)}, u32[]{:S(2)}) collective-permute-start(bf16[2,8,16,640]{3,2,1,0:T(8,128)(2,1)S(1)} %add_convert_fusion.3), channel_id=1, source_target_pairs={{0,14},{2,0},{4,2},{6,4},{8,6},{10,8},{12,10},{14,12},{1,15},{3,1}... | collective-permute-start | bytes 983048 | tf_op jit(solution)/shard_map/ppermute | solution.py:284
  31.0 4.7 %collective-permute-done.13 = bf16[2,8,16,640]{3,2,1,0:T(8,128)(2,1)S(1)} collective-permute-done((bf16[2,8,16,640]{3,2,1,0:T(8,128)(2,1)S(1)}, bf16[2,8,16,640]{3,2,1,0:T(8,128)(2,1)S(1)}, u32[]{:S(2)}, u32[]{:S(2)}) %collective-permute-start.13) | collective-permute-done | bytes 327712 | tf_op jit(solution)/shard_map/ppermute | solution.py:284
  35.8 3.8 %collective-permute-start.14 = (bf16[2,8,16,640]{3,2,1,0:T(8,128)(2,1)S(1)}, bf16[2,8,16,640]{3,2,1,0:T(8,128)(2,1)S(1)}, u32[]{:S(2)}, u32[]{:S(2)}) collective-permute-start(bf16[2,8,16,640]{3,2,1,0:T(8,128)(2,1)S(1)} %add_convert_fusion.2), channel_id=1, source_target_pairs={{0,14},{2,0},{4,2},{6,4},{8,6},{10,8},{12,10},{14,12},{1,15},{3,1}... | collective-permute-start | bytes 983048 | tf_op jit(solution)/shard_map/ppermute | solution.py:284
  40.6 4.1 %collective-permute-done.14 = bf16[2,8,16,640]{3,2,1,0:T(8,128)(2,1)S(1)} collective-permute-done((bf16[2,8,16,640]{3,2,1,0:T(8,128)(2,1)S(1)}, bf16[2,8,16,640]{3,2,1,0:T(8,128)(2,1)S(1)}, u32[]{:S(2)}, u32[]{:S(2)}) %collective-permute-start.14) | collective-permute-done | bytes 327712 | tf_op jit(solution)/shard_map/ppermute | solution.py:284
  44.9 3.8 %collective-permute-start.15 = (bf16[2,8,16,640]{3,2,1,0:T(8,128)(2,1)S(1)}, bf16[2,8,16,640]{3,2,1,0:T(8,128)(2,1)S(1)}, u32[]{:S(2)}, u32[]{:S(2)}) collective-permute-start(bf16[2,8,16,640]{3,2,1,0:T(8,128)(2,1)S(1)} %add_convert_fusion.1), channel_id=1, source_target_pairs={{0,14},{2,0},{4,2},{6,4},{8,6},{10,8},{12,10},{14,12},{1,15},{3,1}... | collective-permute-start | bytes 983048 | tf_op jit(solution)/shard_map/ppermute | solution.py:284
  48.6 3.5 %shard_map.65 = (bf16[8,24,640]{2,1,0:T(8,128)(2,1)S(1)}, bf16[8,24,640]{2,1,0:T(8,128)(2,1)S(1)}, bf16[8,24,640]{2,1,0:T(8,128)(2,1)S(1)}) custom-call(s32[2]{0:T(128)S(1)} %pad_add_fusion.which._, bf16[2,40,40,640]{3,2,1,0:T(8,128)(2,1)} %here.7, bf16[40,24,640]{2,1,0:T(8,128)(2,1)S(1)} %collective-permute-done.came, ...), custom_call_target="tpu_custom_call" | custom-call | flops 471859200 | bytes 2990080 | tf_op jit(solution)/shard_map/pallas_call | solution.py:44
  52.3 4.1 %collective-permute-start.6 = (bf16[4,24,640]{2,1,0:T(8,128)(2,1)S(1)}, bf16[4,24,640]{2,1,0:T(8,128)(2,1)S(1)}, u32[]{:S(2)}, u32[]{:S(2)}) collective-permute-start(bf16[4,24,640]{2,1,0:T(8,128)(2,1)S(1)} %get-tuple-element.54), channel_id=1, source_target_pairs={{0,12},{2,14},{4,0},{6,2},{8,4},{10,6},{12,8},{14,10},{1,13},{3,15... | collective-permute-start | bytes 368648 | tf_op jit(solution)/shard_map/ppermute | solution.py:284
  56.4 3.9 %shard_map.64 = (bf16[8,24,640]{2,1,0:T(8,128)(2,1)S(1)}, bf16[8,24,640]{2,1,0:T(8,128)(2,1)S(1)}, bf16[8,24,640]{2,1,0:T(8,128)(2,1)S(1)}, bf16[8,24,640]{2,1,0:T(8,128)(2,1)S(1)}, bf16[8,24,640]{2,1,0:T(8,128)(2,1)S(1)}) custom-call(s32[2]{0:T(128)S(1)} %pad_add_fusion.which._, bf16[2,40,40,640]{3,2,1,0:T(8,128)(2,1)} %here.7, ...), custom_call_target="tpu_custom_call" | custom-call | flops 786432000 | bytes 2990080 | tf_op jit(solution)/shard_map/pallas_call | solution.py:44
  64.1 4.3 %collective-permute-done.5 = bf16[8,24,640]{2,1,0:T(8,128)(2,1)S(1)} collective-permute-done((bf16[8,24,640]{2,1,0:T(8,128)(2,1)S(1)}, bf16[8,24,640]{2,1,0:T(8,128)(2,1)S(1)}, u32[]{:S(2)}, u32[]{:S(2)}) %collective-permute-start.5) | collective-permute-done | bytes 245792 | tf_op jit(solution)/shard_map/ppermute | solution.py:284
  68.6 3.8 %collective-permute-start.7 = (bf16[8,24,640]{2,1,0:T(8,128)(2,1)S(1)}, bf16[8,24,640]{2,1,0:T(8,128)(2,1)S(1)}, u32[]{:S(2)}, u32[]{:S(2)}) collective-permute-start(bf16[8,24,640]{2,1,0:T(8,128)(2,1)S(1)} %add_convert_fusion.8), channel_id=1, source_target_pairs={{0,14},{2,0},{4,2},{6,4},{8,6},{10,8},{12,10},{14,12},{1,15},{3,1}... | collective-permute-start | bytes 737288 | tf_op jit(solution)/shard_map/ppermute | solution.py:284
  74.1 4.1 %collective-permute-done.7 = bf16[8,24,640]{2,1,0:T(8,128)(2,1)S(1)} collective-permute-done((bf16[8,24,640]{2,1,0:T(8,128)(2,1)S(1)}, bf16[8,24,640]{2,1,0:T(8,128)(2,1)S(1)}, u32[]{:S(2)}, u32[]{:S(2)}) %collective-permute-start.7) | collective-permute-done | bytes 245792 | tf_op jit(solution)/shard_map/ppermute | solution.py:284
  78.3 3.8 %collective-permute-start.8 = (bf16[8,24,640]{2,1,0:T(8,128)(2,1)S(1)}, bf16[8,24,640]{2,1,0:T(8,128)(2,1)S(1)}, u32[]{:S(2)}, u32[]{:S(2)}) collective-permute-start(bf16[8,24,640]{2,1,0:T(8,128)(2,1)S(1)} %add_convert_fusion.7), channel_id=1, source_target_pairs={{0,14},{2,0},{4,2},{6,4},{8,6},{10,8},{12,10},{14,12},{1,15},{3,1}... | collective-permute-start | bytes 737288 | tf_op jit(solution)/shard_map/ppermute | solution.py:284
  82.4 3.5 %collective-permute-done.8 = bf16[8,24,640]{2,1,0:T(8,128)(2,1)S(1)} collective-permute-done((bf16[8,24,640]{2,1,0:T(8,128)(2,1)S(1)}, bf16[8,24,640]{2,1,0:T(8,128)(2,1)S(1)}, u32[]{:S(2)}, u32[]{:S(2)}) %collective-permute-start.8) | collective-permute-done | bytes 245792 | tf_op jit(solution)/shard_map/ppermute | solution.py:284
  87.5 7.6 %all-to-all-start = ((bf16[16,40,288]{2,1,0:T(8,128)(2,1)}), bf16[16,40,288]{2,1,0:T(8,128)(2,1)S(1)}, u32[]{:S(2)}, u32[]{:S(2)}) async-start(bf16[16,40,288]{2,1,0:T(8,128)(2,1)} %shard_map.68), calls=%async_computation | async-start | bytes 983040 | tf_op jit(solution)/shard_map/all_to_all | solution.py:373
  98.5 5.1 %all-to-all-done = bf16[16,40,288]{2,1,0:T(8,128)(2,1)S(1)} async-done(((bf16[16,40,288]{2,1,0:T(8,128)(2,1)}), bf16[16,40,288]{2,1,0:T(8,128)(2,1)S(1)}, u32[]{:S(2)}, u32[]{:S(2)}) %all-to-all-start) | async-done | bytes 368672 | tf_op jit(solution)/shard_map/all_to_all | solution.py:373
  104.7 14.6 %all_to_all.10.x = bf16[16,40,288]{2,1,0:T(8,128)(2,1)S(1)} all-to-all(bf16[16,40,288]{2,1,0:T(8,128)(2,1)S(1)} %bitcast.36), channel_id=1, replica_groups=mesh['row'=16,'z'=8,'ylo'=2] {'row'}, dimensions={0} | all-to-all | bytes 737280 | tf_op jit(solution)/shard_map/all_to_all | solution.py:375
  120.1 3.8 %collective-permute-start.17 = (bf16[8,24,640]{2,1,0:T(8,128)(2,1)S(1)}, bf16[8,24,640]{2,1,0:T(8,128)(2,1)S(1)}, u32[]{:S(2)}, u32[]{:S(2)}) collective-permute-start(bf16[8,24,640]{2,1,0:T(8,128)(2,1)S(1)} %get-tuple-element.45.refs_6_), channel_id=1, source_target_pairs={{0,14},{2,0},{4,2},{6,4},{8,6},{10,8},{12,10},{14,12},{1,15},{3,1}... | collective-permute-start | bytes 737288 | tf_op jit(solution)/shard_map/ppermute | solution.py:284
  123.8 6.4 %collective-permute-done.20.refs_5_ = bf16[8,24,640]{2,1,0:T(8,128)(2,1)S(1)} collective-permute-done((bf16[8,24,640]{2,1,0:T(8,128)(2,1)S(1)}, bf16[8,24,640]{2,1,0:T(8,128)(2,1)S(1)}, u32[]{:S(2)}, u32[]{:S(2)}) %collective-permute-start.20) | collective-permute-done | bytes 245792 | tf_op jit(solution)/shard_map/ppermute | solution.py:284
  130.2 3.6 %collective-permute-start.18 = (bf16[8,24,640]{2,1,0:T(8,128)(2,1)S(1)}, bf16[8,24,640]{2,1,0:T(8,128)(2,1)S(1)}, u32[]{:S(2)}, u32[]{:S(2)}) collective-permute-start(bf16[8,24,640]{2,1,0:T(8,128)(2,1)S(1)} %collective-permute-done.17.refs_7_), channel_id=1, source_target_pairs={{0,14},{2,0},{4,2},{6,4},{8,6},{10,8},{12,10},{14,12},{1,15},{3,1}... | collective-permute-start | bytes 737288 | tf_op jit(solution)/shard_map/ppermute | solution.py:284
  134.5 4.9 %collective-permute-done.21.refs_4_ = bf16[8,24,640]{2,1,0:T(8,128)(2,1)S(1)} collective-permute-done((bf16[8,24,640]{2,1,0:T(8,128)(2,1)S(1)}, bf16[8,24,640]{2,1,0:T(8,128)(2,1)S(1)}, u32[]{:S(2)}, u32[]{:S(2)}) %collective-permute-start.21) | collective-permute-done | bytes 245792 | tf_op jit(solution)/shard_map/ppermute | solution.py:284
  139.4 3.6 %collective-permute-start.19 = (bf16[8,24,640]{2,1,0:T(8,128)(2,1)S(1)}, bf16[8,24,640]{2,1,0:T(8,128)(2,1)S(1)}, u32[]{:S(2)}, u32[]{:S(2)}) collective-permute-start(bf16[8,24,640]{2,1,0:T(8,128)(2,1)S(1)} %collective-permute-done.18.refs_8_), channel_id=1, source_target_pairs={{0,14},{2,0},{4,2},{6,4},{8,6},{10,8},{12,10},{14,12},{1,15},{3,1}... | collective-permute-start | bytes 737288 | tf_op jit(solution)/shard_map/ppermute | solution.py:284
  143.1 4.2 %collective-permute-start.23 = (bf16[4,24,640]{2,1,0:T(8,128)(2,1)S(1)}, bf16[4,24,640]{2,1,0:T(8,128)(2,1)S(1)}, u32[]{:S(2)}, u32[]{:S(2)}) collective-permute-start(bf16[4,24,640]{2,1,0:T(8,128)(2,1)S(1)} %slice.45), channel_id=1, source_target_pairs={{0,12},{2,14},{4,0},{6,2},{8,4},{10,6},{12,8},{14,10},{1,13},{3,15... | collective-permute-start | bytes 368648 | tf_op jit(solution)/shard_map/ppermute | solution.py:284
  147.5 5.0 %collective-permute-done.22.refs_1_ = bf16[4,24,640]{2,1,0:T(8,128)(2,1)S(1)} collective-permute-done((bf16[4,24,640]{2,1,0:T(8,128)(2,1)S(1)}, bf16[4,24,640]{2,1,0:T(8,128)(2,1)S(1)}, u32[]{:S(2)}, u32[]{:S(2)}) %collective-permute-start.22) | collective-permute-done | bytes 122912 | tf_op jit(solution)/shard_map/ppermute | solution.py:284
  154.6 3.8 %shard_map.71 = (bf16[40,24,640]{2,1,0:T(8,128)(2,1)S(1)}, bf16[2,40,40,640]{3,2,1,0:T(8,128)(2,1)}) custom-call(s32[2]{0:T(128)S(1)} %pad_add_fusion.which._, bf16[8,24,640]{2,1,0:T(8,128)(2,1)S(1)} %collective-permute-done.19.refs_0_, bf16[4,24,640]{2,1,0:T(8,128)(2,1)S(1)} %collective-permute-done.22.refs_1_, ...), custom_call_target="tpu_custom_call" | custom-call | flops 1258291200 | bytes 1310720 | tf_op jit(solution)/shard_map/pallas_call | solution.py:44
  159.9 3.7 %collective-permute-start.28 = (bf16[2,8,16,640]{3,2,1,0:T(8,128)(2,1)S(1)}, bf16[2,8,16,640]{3,2,1,0:T(8,128)(2,1)S(1)}, u32[]{:S(2)}, u32[]{:S(2)}) collective-permute-start(bf16[2,8,16,640]{3,2,1,0:T(8,128)(2,1)S(1)} %collective-permute-done.27.refs_6_), channel_id=1, source_target_pairs={{0,14},{2,0},{4,2},{6,4},{8,6},{10,8},{12,10},{14,12},{1,15},{3,1}... | collective-permute-start | bytes 983048 | tf_op jit(solution)/shard_map/ppermute | solution.py:284
  163.6 4.2 %collective-permute-done.31.refs_4_ = bf16[2,8,16,640]{3,2,1,0:T(8,128)(2,1)S(1)} collective-permute-done((bf16[2,8,16,640]{3,2,1,0:T(8,128)(2,1)S(1)}, bf16[2,8,16,640]{3,2,1,0:T(8,128)(2,1)S(1)}, u32[]{:S(2)}, u32[]{:S(2)}) %collective-permute-start.31) | collective-permute-done | bytes 327712 | tf_op jit(solution)/shard_map/ppermute | solution.py:284
  172.9 7.0 %collective-permute-done.32.refs_3_ = bf16[2,8,16,640]{3,2,1,0:T(8,128)(2,1)S(1)} collective-permute-done((bf16[2,8,16,640]{3,2,1,0:T(8,128)(2,1)S(1)}, bf16[2,8,16,640]{3,2,1,0:T(8,128)(2,1)S(1)}, u32[]{:S(2)}, u32[]{:S(2)}) %collective-permute-start.32) | collective-permute-done | bytes 327712 | tf_op jit(solution)/shard_map/ppermute | solution.py:284
  183.1 5.0 %collective-permute-done.33.refs_2_ = bf16[2,8,16,640]{3,2,1,0:T(8,128)(2,1)S(1)} collective-permute-done((bf16[2,8,16,640]{3,2,1,0:T(8,128)(2,1)S(1)}, bf16[2,8,16,640]{3,2,1,0:T(8,128)(2,1)S(1)}, u32[]{:S(2)}, u32[]{:S(2)}) %collective-permute-start.33) | collective-permute-done | bytes 327712 | tf_op jit(solution)/shard_map/ppermute | solution.py:284
  188.1 3.7 %shard_map.72._ = bf16[2,40,40,640]{3,2,1,0:T(8,128)(2,1)} custom-call(s32[2]{0:T(128)S(1)} %pad_add_fusion.which._, bf16[2,8,16,640]{3,2,1,0:T(8,128)(2,1)S(1)} %collective-permute-done.29.refs_0_, bf16[2,8,16,640]{3,2,1,0:T(8,128)(2,1)S(1)} %collective-permute-done.30.refs_1_, ...), custom_call_target="tpu_custom_call", output_to_operand_aliasing={{}: (10, {})} | custom-call | flops 838860800 | bytes 3522560 | tf_op jit(solution)/shard_map/pallas_call | solution.py:44
  (107 shorter events, 41.2 us)
Async XLA Ops:
  11.6 13.1 %collective-permute-start.12 = (bf16[2,8,16,640]{3,2,1,0:T(8,128)(2,1)}, bf16[2,8,16,640]{3,2,1,0:T(8,128)(2,1)}, u32[]{:S(2)}, u32[]{:S(2)}) collective-permute-start(bf16[2,8,16,640]{3,2,1,0:T(8,128)(2,1)} %get-tuple-element.41), channel_id=1, source_target_pairs={{0,14},{2,0},{4,2},{6,4},{8,6},{10,8},{12,10},{14,12},{1,15},{3,1}... | collective-permute-start | bytes 983048 | tf_op jit(solution)/shard_map/ppermute | solution.py:284
  17.4 12.4 %collective-permute-start.9 = (bf16[2,8,16,640]{3,2,1,0:T(8,128)(2,1)}, bf16[2,8,16,640]{3,2,1,0:T(8,128)(2,1)}, u32[]{:S(2)}, u32[]{:S(2)}) collective-permute-start(bf16[2,8,16,640]{3,2,1,0:T(8,128)(2,1)} %get-tuple-element.38), channel_id=1, source_target_pairs={{0,2},{2,4},{4,6},{6,8},{8,10},{10,12},{12,14},{14,0},{1,3},{3,5},... | collective-permute-start | bytes 983048 | tf_op jit(solution)/shard_map/ppermute | solution.py:284
  17.4 31.2 %collective-permute-start = (bf16[40,24,640]{2,1,0:T(8,128)(2,1)}, bf16[40,24,640]{2,1,0:T(8,128)(2,1)S(1)}, u32[]{:S(2)}, u32[]{:S(2)}) collective-permute-start(bf16[40,24,640]{2,1,0:T(8,128)(2,1)} %copy-done.3), channel_id=1, source_target_pairs={{0,1},{1,0},{2,3},{3,2},{4,5},{5,4},{6,7},{7,6},{8,9},{9,8},{10,11... | collective-permute-start | bytes 3686408 | tf_op jit(solution)/shard_map/ppermute | solution.py:288
  25.8 9.9 %collective-permute-start.13 = (bf16[2,8,16,640]{3,2,1,0:T(8,128)(2,1)S(1)}, bf16[2,8,16,640]{3,2,1,0:T(8,128)(2,1)S(1)}, u32[]{:S(2)}, u32[]{:S(2)}) collective-permute-start(bf16[2,8,16,640]{3,2,1,0:T(8,128)(2,1)S(1)} %add_convert_fusion.3), channel_id=1, source_target_pairs={{0,14},{2,0},{4,2},{6,4},{8,6},{10,8},{12,10},{14,12},{1,15},{3,1}... | collective-permute-start | bytes 983048 | tf_op jit(solution)/shard_map/ppermute | solution.py:284
  30.9 9.6 %collective-permute-start.10 = (bf16[2,8,16,640]{3,2,1,0:T(8,128)(2,1)S(1)}, bf16[2,8,16,640]{3,2,1,0:T(8,128)(2,1)S(1)}, u32[]{:S(2)}, u32[]{:S(2)}) collective-permute-start(bf16[2,8,16,640]{3,2,1,0:T(8,128)(2,1)S(1)} %add_convert_fusion.5), channel_id=1, source_target_pairs={{0,2},{2,4},{4,6},{6,8},{8,10},{10,12},{12,14},{14,0},{1,3},{3,5},... | collective-permute-start | bytes 983048 | tf_op jit(solution)/shard_map/ppermute | solution.py:284
  35.8 9.0 %collective-permute-start.14 = (bf16[2,8,16,640]{3,2,1,0:T(8,128)(2,1)S(1)}, bf16[2,8,16,640]{3,2,1,0:T(8,128)(2,1)S(1)}, u32[]{:S(2)}, u32[]{:S(2)}) collective-permute-start(bf16[2,8,16,640]{3,2,1,0:T(8,128)(2,1)S(1)} %add_convert_fusion.2), channel_id=1, source_target_pairs={{0,14},{2,0},{4,2},{6,4},{8,6},{10,8},{12,10},{14,12},{1,15},{3,1}... | collective-permute-start | bytes 983048 | tf_op jit(solution)/shard_map/ppermute | solution.py:284
  40.5 19.8 %collective-permute-start.11 = (bf16[2,8,16,640]{3,2,1,0:T(8,128)(2,1)S(1)}, bf16[2,8,16,640]{3,2,1,0:T(8,128)(2,1)S(1)}, u32[]{:S(2)}, u32[]{:S(2)}) collective-permute-start(bf16[2,8,16,640]{3,2,1,0:T(8,128)(2,1)S(1)} %add_convert_fusion.4), channel_id=1, source_target_pairs={{0,2},{2,4},{4,6},{6,8},{8,10},{10,12},{12,14},{14,0},{1,3},{3,5},... | collective-permute-start | bytes 983048 | tf_op jit(solution)/shard_map/ppermute | solution.py:284
  44.9 18.8 %collective-permute-start.15 = (bf16[2,8,16,640]{3,2,1,0:T(8,128)(2,1)S(1)}, bf16[2,8,16,640]{3,2,1,0:T(8,128)(2,1)S(1)}, u32[]{:S(2)}, u32[]{:S(2)}) collective-permute-start(bf16[2,8,16,640]{3,2,1,0:T(8,128)(2,1)S(1)} %add_convert_fusion.1), channel_id=1, source_target_pairs={{0,14},{2,0},{4,2},{6,4},{8,6},{10,8},{12,10},{14,12},{1,15},{3,1}... | collective-permute-start | bytes 983048 | tf_op jit(solution)/shard_map/ppermute | solution.py:284
  52.2 11.6 %collective-permute-start.2 = (bf16[4,24,640]{2,1,0:T(8,128)(2,1)S(1)}, bf16[4,24,640]{2,1,0:T(8,128)(2,1)S(1)}, u32[]{:S(2)}, u32[]{:S(2)}) collective-permute-start(bf16[4,24,640]{2,1,0:T(8,128)(2,1)S(1)} %get-tuple-element.53), channel_id=1, source_target_pairs={{0,4},{2,6},{4,8},{6,10},{8,12},{10,14},{12,0},{14,2},{1,5},{3,7},... | collective-permute-start | bytes 368648 | tf_op jit(solution)/shard_map/ppermute | solution.py:284
  52.3 11.8 %collective-permute-start.6 = (bf16[4,24,640]{2,1,0:T(8,128)(2,1)S(1)}, bf16[4,24,640]{2,1,0:T(8,128)(2,1)S(1)}, u32[]{:S(2)}, u32[]{:S(2)}) collective-permute-start(bf16[4,24,640]{2,1,0:T(8,128)(2,1)S(1)} %get-tuple-element.54), channel_id=1, source_target_pairs={{0,12},{2,14},{4,0},{6,2},{8,4},{10,6},{12,8},{14,10},{1,13},{3,15... | collective-permute-start | bytes 368648 | tf_op jit(solution)/shard_map/ppermute | solution.py:284
  60.4 8.1 %collective-permute-start.5 = (bf16[8,24,640]{2,1,0:T(8,128)(2,1)S(1)}, bf16[8,24,640]{2,1,0:T(8,128)(2,1)S(1)}, u32[]{:S(2)}, u32[]{:S(2)}) collective-permute-start(bf16[8,24,640]{2,1,0:T(8,128)(2,1)S(1)} %get-tuple-element.34), channel_id=1, source_target_pairs={{0,14},{2,0},{4,2},{6,4},{8,6},{10,8},{12,10},{14,12},{1,15},{3,1}... | collective-permute-start | bytes 737288 | tf_op jit(solution)/shard_map/ppermute | solution.py:284
  64.0 9.9 %collective-permute-start.3 = (bf16[8,24,640]{2,1,0:T(8,128)(2,1)S(1)}, bf16[8,24,640]{2,1,0:T(8,128)(2,1)S(1)}, u32[]{:S(2)}, u32[]{:S(2)}) collective-permute-start(bf16[8,24,640]{2,1,0:T(8,128)(2,1)S(1)} %add_convert_fusion.10), channel_id=1, source_target_pairs={{0,2},{2,4},{4,6},{6,8},{8,10},{10,12},{12,14},{14,0},{1,3},{3,5},... | collective-permute-start | bytes 737288 | tf_op jit(solution)/shard_map/ppermute | solution.py:284
  68.6 9.7 %collective-permute-start.7 = (bf16[8,24,640]{2,1,0:T(8,128)(2,1)S(1)}, bf16[8,24,640]{2,1,0:T(8,128)(2,1)S(1)}, u32[]{:S(2)}, u32[]{:S(2)}) collective-permute-start(bf16[8,24,640]{2,1,0:T(8,128)(2,1)S(1)} %add_convert_fusion.8), channel_id=1, source_target_pairs={{0,14},{2,0},{4,2},{6,4},{8,6},{10,8},{12,10},{14,12},{1,15},{3,1}... | collective-permute-start | bytes 737288 | tf_op jit(solution)/shard_map/ppermute | solution.py:284
  72.3 9.9 %collective-permute-start.16 = (bf16[8,16,640]{2,1,0:T(8,128)(2,1)S(1)}, bf16[8,16,640]{2,1,0:T(8,128)(2,1)S(1)}, u32[]{:S(2)}, u32[]{:S(2)}) collective-permute-start(bf16[8,16,640]{2,1,0:T(8,128)(2,1)S(1)} %slice_bitcast_fusion.2), channel_id=1, source_target_pairs={{0,1},{1,0},{2,3},{3,2},{4,5},{5,4},{6,7},{7,6},{8,9},{9,8},{10,11... | collective-permute-start | bytes 491528 | tf_op jit(solution)/shard_map/ppermute | solution.py:288
  74.0 8.3 %collective-permute-start.4 = (bf16[8,24,640]{2,1,0:T(8,128)(2,1)S(1)}, bf16[8,24,640]{2,1,0:T(8,128)(2,1)S(1)}, u32[]{:S(2)}, u32[]{:S(2)}) collective-permute-start(bf16[8,24,640]{2,1,0:T(8,128)(2,1)S(1)} %add_convert_fusion.9), channel_id=1, source_target_pairs={{0,2},{2,4},{4,6},{6,8},{8,10},{10,12},{12,14},{14,0},{1,3},{3,5},... | collective-permute-start | bytes 737288 | tf_op jit(solution)/shard_map/ppermute | solution.py:284
  87.5 16.0 %all-to-all-start = ((bf16[16,40,288]{2,1,0:T(8,128)(2,1)}), bf16[16,40,288]{2,1,0:T(8,128)(2,1)S(1)}, u32[]{:S(2)}, u32[]{:S(2)}) async-start(bf16[16,40,288]{2,1,0:T(8,128)(2,1)} %shard_map.68), calls=%async_computation | async-start | bytes 983040 | tf_op jit(solution)/shard_map/all_to_all | solution.py:373
  120.0 10.2 %collective-permute-start.20 = (bf16[8,24,640]{2,1,0:T(8,128)(2,1)S(1)}, bf16[8,24,640]{2,1,0:T(8,128)(2,1)S(1)}, u32[]{:S(2)}, u32[]{:S(2)}) collective-permute-start(bf16[8,24,640]{2,1,0:T(8,128)(2,1)S(1)} %get-tuple-element.45.refs_6_), channel_id=1, source_target_pairs={{0,2},{2,4},{4,6},{6,8},{8,10},{10,12},{12,14},{14,0},{1,3},{3,5},... | collective-permute-start | bytes 737288 | tf_op jit(solution)/shard_map/ppermute | solution.py:284
  120.1 10.2 %collective-permute-start.17 = (bf16[8,24,640]{2,1,0:T(8,128)(2,1)S(1)}, bf16[8,24,640]{2,1,0:T(8,128)(2,1)S(1)}, u32[]{:S(2)}, u32[]{:S(2)}) collective-permute-start(bf16[8,24,640]{2,1,0:T(8,128)(2,1)S(1)} %get-tuple-element.45.refs_6_), channel_id=1, source_target_pairs={{0,14},{2,0},{4,2},{6,4},{8,6},{10,8},{12,10},{14,12},{1,15},{3,1}... | collective-permute-start | bytes 737288 | tf_op jit(solution)/shard_map/ppermute | solution.py:284
  130.2 9.2 %collective-permute-start.21 = (bf16[8,24,640]{2,1,0:T(8,128)(2,1)S(1)}, bf16[8,24,640]{2,1,0:T(8,128)(2,1)S(1)}, u32[]{:S(2)}, u32[]{:S(2)}) collective-permute-start(bf16[8,24,640]{2,1,0:T(8,128)(2,1)S(1)} %collective-permute-done.20.refs_5_), channel_id=1, source_target_pairs={{0,2},{2,4},{4,6},{6,8},{8,10},{10,12},{12,14},{14,0},{1,3},{3,5},... | collective-permute-start | bytes 737288 | tf_op jit(solution)/shard_map/ppermute | solution.py:284
  130.2 9.2 %collective-permute-start.18 = (bf16[8,24,640]{2,1,0:T(8,128)(2,1)S(1)}, bf16[8,24,640]{2,1,0:T(8,128)(2,1)S(1)}, u32[]{:S(2)}, u32[]{:S(2)}) collective-permute-start(bf16[8,24,640]{2,1,0:T(8,128)(2,1)S(1)} %collective-permute-done.17.refs_7_), channel_id=1, source_target_pairs={{0,14},{2,0},{4,2},{6,4},{8,6},{10,8},{12,10},{14,12},{1,15},{3,1}... | collective-permute-start | bytes 737288 | tf_op jit(solution)/shard_map/ppermute | solution.py:284
  133.8 13.5 %collective-permute-start.26 = (bf16[8,16,640]{2,1,0:T(8,128)(2,1)S(1)}, bf16[8,16,640]{2,1,0:T(8,128)(2,1)S(1)}, u32[]{:S(2)}, u32[]{:S(2)}) collective-permute-start(bf16[8,16,640]{2,1,0:T(8,128)(2,1)S(1)} %get-tuple-element.47), channel_id=1, source_target_pairs={{0,1},{1,0},{2,3},{3,2},{4,5},{5,4},{6,7},{7,6},{8,9},{9,8},{10,11... | collective-permute-start | bytes 491528 | tf_op jit(solution)/shard_map/ppermute | solution.py:288
  139.4 15.2 %collective-permute-start.24 = (bf16[8,24,640]{2,1,0:T(8,128)(2,1)S(1)}, bf16[8,24,640]{2,1,0:T(8,128)(2,1)S(1)}, u32[]{:S(2)}, u32[]{:S(2)}) collective-permute-start(bf16[8,24,640]{2,1,0:T(8,128)(2,1)S(1)} %collective-permute-done.21.refs_4_), channel_id=1, source_target_pairs={{0,2},{2,4},{4,6},{6,8},{8,10},{10,12},{12,14},{14,0},{1,3},{3,5},... | collective-permute-start | bytes 737288 | tf_op jit(solution)/shard_map/ppermute | solution.py:284
  139.4 15.2 %collective-permute-start.19 = (bf16[8,24,640]{2,1,0:T(8,128)(2,1)S(1)}, bf16[8,24,640]{2,1,0:T(8,128)(2,1)S(1)}, u32[]{:S(2)}, u32[]{:S(2)}) collective-permute-start(bf16[8,24,640]{2,1,0:T(8,128)(2,1)S(1)} %collective-permute-done.18.refs_8_), channel_id=1, source_target_pairs={{0,14},{2,0},{4,2},{6,4},{8,6},{10,8},{12,10},{14,12},{1,15},{3,1}... | collective-permute-start | bytes 737288 | tf_op jit(solution)/shard_map/ppermute | solution.py:284
  143.0 9.5 %collective-permute-start.22 = (bf16[4,24,640]{2,1,0:T(8,128)(2,1)S(1)}, bf16[4,24,640]{2,1,0:T(8,128)(2,1)S(1)}, u32[]{:S(2)}, u32[]{:S(2)}) collective-permute-start(bf16[4,24,640]{2,1,0:T(8,128)(2,1)S(1)} %slice.44), channel_id=1, source_target_pairs={{0,4},{2,6},{4,8},{6,10},{8,12},{10,14},{12,0},{14,2},{1,5},{3,7},... | collective-permute-start | bytes 368648 | tf_op jit(solution)/shard_map/ppermute | solution.py:284
  143.1 11.5 %collective-permute-start.23 = (bf16[4,24,640]{2,1,0:T(8,128)(2,1)S(1)}, bf16[4,24,640]{2,1,0:T(8,128)(2,1)S(1)}, u32[]{:S(2)}, u32[]{:S(2)}) collective-permute-start(bf16[4,24,640]{2,1,0:T(8,128)(2,1)S(1)} %slice.45), channel_id=1, source_target_pairs={{0,12},{2,14},{4,0},{6,2},{8,4},{10,6},{12,8},{14,10},{1,13},{3,15... | collective-permute-start | bytes 368648 | tf_op jit(solution)/shard_map/ppermute | solution.py:284
  147.4 12.6 %collective-permute-start.27 = (bf16[2,8,16,640]{3,2,1,0:T(8,128)(2,1)S(1)}, bf16[2,8,16,640]{3,2,1,0:T(8,128)(2,1)S(1)}, u32[]{:S(2)}, u32[]{:S(2)}) collective-permute-start(bf16[2,8,16,640]{3,2,1,0:T(8,128)(2,1)S(1)} %pad_maximum_fusion.2.refs_5_), channel_id=1, source_target_pairs={{0,14},{2,0},{4,2},{6,4},{8,6},{10,8},{12,10},{14,12},{1,15},{3,1}... | collective-permute-start | bytes 983048 | tf_op jit(solution)/shard_map/ppermute | solution.py:284
  158.4 33.4 %collective-permute-start.25 = (bf16[40,24,640]{2,1,0:T(8,128)(2,1)S(1)}, bf16[40,24,640]{2,1,0:T(8,128)(2,1)S(1)}, u32[]{:S(2)}, u32[]{:S(2)}) collective-permute-start(bf16[40,24,640]{2,1,0:T(8,128)(2,1)S(1)} %get-tuple-element.46), channel_id=1, source_target_pairs={{0,1},{1,0},{2,3},{3,2},{4,5},{5,4},{6,7},{7,6},{8,9},{9,8},{10,11... | collective-permute-start | bytes 3686408 | tf_op jit(solution)/shard_map/ppermute | solution.py:288
  159.1 8.7 %collective-permute-start.31 = (bf16[2,8,16,640]{3,2,1,0:T(8,128)(2,1)S(1)}, bf16[2,8,16,640]{3,2,1,0:T(8,128)(2,1)S(1)}, u32[]{:S(2)}, u32[]{:S(2)}) collective-permute-start(bf16[2,8,16,640]{3,2,1,0:T(8,128)(2,1)S(1)} %pad_maximum_fusion.2.refs_5_), channel_id=1, source_target_pairs={{0,2},{2,4},{4,6},{6,8},{8,10},{10,12},{12,14},{14,0},{1,3},{3,5},... | collective-permute-start | bytes 983048 | tf_op jit(solution)/shard_map/ppermute | solution.py:284
  159.9 10.0 %collective-permute-start.28 = (bf16[2,8,16,640]{3,2,1,0:T(8,128)(2,1)S(1)}, bf16[2,8,16,640]{3,2,1,0:T(8,128)(2,1)S(1)}, u32[]{:S(2)}, u32[]{:S(2)}) collective-permute-start(bf16[2,8,16,640]{3,2,1,0:T(8,128)(2,1)S(1)} %collective-permute-done.27.refs_6_), channel_id=1, source_target_pairs={{0,14},{2,0},{4,2},{6,4},{8,6},{10,8},{12,10},{14,12},{1,15},{3,1}... | collective-permute-start | bytes 983048 | tf_op jit(solution)/shard_map/ppermute | solution.py:284
  167.8 12.0 %collective-permute-start.32 = (bf16[2,8,16,640]{3,2,1,0:T(8,128)(2,1)S(1)}, bf16[2,8,16,640]{3,2,1,0:T(8,128)(2,1)S(1)}, u32[]{:S(2)}, u32[]{:S(2)}) collective-permute-start(bf16[2,8,16,640]{3,2,1,0:T(8,128)(2,1)S(1)} %collective-permute-done.31.refs_4_), channel_id=1, source_target_pairs={{0,2},{2,4},{4,6},{6,8},{8,10},{10,12},{12,14},{14,0},{1,3},{3,5},... | collective-permute-start | bytes 983048 | tf_op jit(solution)/shard_map/ppermute | solution.py:284
  170.0 10.5 %collective-permute-start.29 = (bf16[2,8,16,640]{3,2,1,0:T(8,128)(2,1)S(1)}, bf16[2,8,16,640]{3,2,1,0:T(8,128)(2,1)S(1)}, u32[]{:S(2)}, u32[]{:S(2)}) collective-permute-start(bf16[2,8,16,640]{3,2,1,0:T(8,128)(2,1)S(1)} %collective-permute-done.28.refs_7_), channel_id=1, source_target_pairs={{0,14},{2,0},{4,2},{6,4},{8,6},{10,8},{12,10},{14,12},{1,15},{3,1}... | collective-permute-start | bytes 983048 | tf_op jit(solution)/shard_map/ppermute | solution.py:284
  179.8 8.3 %collective-permute-start.33 = (bf16[2,8,16,640]{3,2,1,0:T(8,128)(2,1)S(1)}, bf16[2,8,16,640]{3,2,1,0:T(8,128)(2,1)S(1)}, u32[]{:S(2)}, u32[]{:S(2)}) collective-permute-start(bf16[2,8,16,640]{3,2,1,0:T(8,128)(2,1)S(1)} %collective-permute-done.32.refs_3_), channel_id=1, source_target_pairs={{0,2},{2,4},{4,6},{6,8},{8,10},{10,12},{12,14},{14,0},{1,3},{3,5},... | collective-permute-start | bytes 983048 | tf_op jit(solution)/shard_map/ppermute | solution.py:284
  (12 other events, 258.0 us)

commit v3 on v2

--- a/solution.py
+++ b/solution.py
@@ -74,18 +74,43 @@
     return pl.BlockSpec(shape, lambda *_: (0,) * len(shape))
 
 
+CUTS = 5
+CUT = LB // CUTS
+
+
 def lift(slab, pick):
-    def body(which, src, dst, sem):
-        copy = pltpu.make_async_copy(src.at[which[1], :, pl.ds(0, YM), :], dst, sem)
-        copy.start()
-        copy.wait()
+    def body(which, src, dst, hold, came, went):
+        def spot(i):
+            return pl.ds(i * CUT, CUT)
+
+        takes = [
+            pltpu.make_async_copy(
+                src.at[which[1], spot(i), pl.ds(0, YM), :], hold.at[spot(i)], came.at[i]
+            )
+            for i in range(CUTS)
+        ]
+        gives = [
+            pltpu.make_async_copy(hold.at[spot(i)], dst.at[spot(i)], went.at[i])
+            for i in range(CUTS)
+        ]
+        for take in takes:
+            take.start()
+        for take, give in zip(takes, gives):
+            take.wait()
+            give.start()
+        for give in gives:
+            give.wait()
 
     return pl.pallas_call(
         body,
         in_specs=[pl.BlockSpec(memory_space=pltpu.SMEM), pl.BlockSpec(memory_space=pltpu.HBM)],
-        out_specs=pl.BlockSpec(memory_space=pltpu.VMEM),
-        out_shape=pltpu.VMEM((LB, YM, NB), BF),
-        scratch_shapes=[pltpu.SemaphoreType.DMA],
+        out_specs=pl.BlockSpec(memory_space=pltpu.HBM),
+        out_shape=jax.ShapeDtypeStruct((LB, YM, NB), BF),
+        scratch_shapes=[
+            pltpu.VMEM((LB, YM, NB), BF),
+            pltpu.SemaphoreType.DMA((CUTS,)),
+            pltpu.SemaphoreType.DMA((CUTS,)),
+        ],
         name="lift",
         cost_estimate=pl.CostEstimate(flops=0, bytes_accessed=4 * LB * YM * NB, transcendentals=0),
         compiler_params=pltpu.CompilerParams(vmem_limit_bytes=24 * 1024 * 1024),
@@ -149,29 +174,40 @@
     return [*slots[LEAD:], *slots[:LEAD]]
 
 
-def y_expand(slots, kt_mine, kt_other, pick, first, tiles):
-    def body(_, *refs):
-        slot_refs, (km, ko, send, kept) = refs[: len(slots)], refs[len(slots) :]
+def y_send(slots, kt_other, tiles):
+    def body(*refs):
+        slot_refs, (ko, send) = refs[: len(slots)], refs[len(slots) :]
         stack = gathered([s[...] for s in slot_refs])
         send[...] = dot(ko[...], stack).reshape(LB, TILE, NB).astype(BF)
+
+    return call(
+        body,
+        (tiles,),
+        [pl.BlockSpec((s.shape[0], TILE, NB), lambda t: (0, t, 0)) for s in slots]
+        + [whole((CL, RW))],
+        pl.BlockSpec((LB, TILE, NB), lambda t: (0, t, 0)),
+        jax.ShapeDtypeStruct((LB, tiles * TILE, NB), BF),
+        (*slots, kt_other),
+        flops=2 * tiles * RW * CL * NB,
+    )
+
+
+def y_keep(slots, kt_mine, pick, first, tiles):
+    def body(_, *refs):
+        slot_refs, (km, kept) = refs[: len(slots)], refs[len(slots) :]
+        stack = gathered([s[...] for s in slot_refs])
         kept[0] = dot(km[...], stack).reshape(LB, TILE, NB).astype(BF)
 
     return call(
         body,
         (tiles,),
         [pl.BlockSpec((s.shape[0], TILE, NB), lambda t, s: (0, t, 0)) for s in slots]
-        + [whole((CL, RW)), whole((CL, RW))],
-        [
-            pl.BlockSpec((LB, TILE, NB), lambda t, s: (0, t, 0)),
-            pl.BlockSpec((1, LB, TILE, NB), lambda t, s: (s[0], 0, first + t, 0)),
-        ],
-        [
-            jax.ShapeDtypeStruct((LB, tiles * TILE, NB), BF),
-            jax.ShapeDtypeStruct((2, LB, MB, NB), BF),
-        ],
-        (*slots, kt_mine, kt_other),
+        + [whole((CL, RW))],
+        pl.BlockSpec((1, LB, TILE, NB), lambda t, s: (s[0], 0, first + t, 0)),
+        jax.ShapeDtypeStruct((2, LB, MB, NB), BF),
+        (*slots, kt_mine),
         pick,
-        flops=4 * tiles * RW * CL * NB,
+        flops=2 * tiles * RW * CL * NB,
     )
 
 
@@ -197,9 +233,18 @@
 
 def put(got, out, pick):
     def body(which, src, _, dst, sem):
-        copy = pltpu.make_async_copy(src, dst.at[which[1], :, pl.ds(0, YM), :], sem)
-        copy.start()
-        copy.wait()
+        copies = [
+            pltpu.make_async_copy(
+                src.at[pl.ds(i * CUT, CUT)],
+                dst.at[which[1], pl.ds(i * CUT, CUT), pl.ds(0, YM), :],
+                sem.at[i],
+            )
+            for i in range(CUTS)
+        ]
+        for copy in copies:
+            copy.start()
+        for copy in copies:
+            copy.wait()
 
     return pl.pallas_call(
         body,
@@ -210,7 +255,7 @@
         ],
         out_specs=pl.BlockSpec(memory_space=pltpu.HBM),
         out_shape=jax.ShapeDtypeStruct((2, LB, MB, NB), BF),
-        scratch_shapes=[pltpu.SemaphoreType.DMA],
+        scratch_shapes=[pltpu.SemaphoreType.DMA((CUTS,))],
         input_output_aliases={2: 0},
         name="put",
         cost_estimate=pl.CostEstimate(flops=0, bytes_accessed=4 * LB * YM * NB, transcendentals=0),
@@ -306,11 +351,9 @@
 def tree_sum(parts):
     up = move(parts[3], 1)
     down = move(parts[5], -1)
-    high = move(parts[FAR][:JH], 2)
-    low = move(parts[FAR][JH:], -2)
-    none = jnp.zeros_like(high)
-    up = add(up, parts[2], jnp.concatenate([high, none], axis=0))
-    down = add(down, parts[6], jnp.concatenate([none, low], axis=0))
+    far = move(parts[FAR], 2)
+    up = add(up, parts[2], far)
+    down = add(down, parts[6])
     up = add(move(up, 1), parts[1])
     down = add(move(down, -1), parts[7])
     return add(parts[0], move(up, 1), move(down, -1))
@@ -377,8 +420,8 @@
 
     kt_mine, kt_other = k_mine.T, k_other.T
     slots = tree_gather(wide_y)
-    send, out = y_expand(slots, kt_mine, kt_other, pick, 0, YT)
-    got = swap(send)
+    got = swap(y_send(slots, kt_other, YT))
+    out = y_keep(slots, kt_mine, pick, 0, YT)
     both = jnp.stack([wide_z, swap(wide_z)])
     out = z_expand(chain_gather(both), kt_mine, out, pick, YT, ZT)
     return put(got, out, pick)

time: 196 us -> 202 us (1.031)
  waiting for transfers between devices: 63.6 us -> 69.8 us
  starting transfers between devices: 72.1 us -> 69.7 us
    ppermute x4, waiting for transfers between devices: 0.01 us -> 7.47 us  [swap(): return lax.ppermute(x, 'ylo', SWAP)]
    ppermute x30 -> x29, starting transfers between devices: 59.9 us -> 57.3 us  [move(): return lax.ppermute(x, 'z', [(i, (i + step) % NZ) for i in range(NZ)])]
    ppermute x30 -> x29, waiting for transfers between devices: 58.5 us -> 57.5 us  [move(): return lax.ppermute(x, 'z', [(i, (i + step) % NZ) for i in range(NZ)])]
    pallas_call x9 -> x10, Pallas kernels: 26.9 us -> 27.7 us  [call(): pl.pallas_call(body, grid_spec=spec, out_shape=out_shape, input_output_al...]
  transfers between devices with their start and end apart: 35 -> 34, of which waited for: 17 -> 20; matrix products, arithmetic and copies ran while one was open for 4% -> 4% of each run, Pallas kernels for 10% -> 10%
where the time goes in v3:
time: 202 us; the launch traced here: 201 us
  waiting for transfers between devices  69.8 us (35%)
  starting transfers between devices  69.7 us (35%)
  Pallas kernels  32 us (16%)
  blocking collectives  14.7 us (7%)
  other arithmetic  8.67 us (4%)
  local copies, waits for them, and re-layouts  2.7 us (1%)
  matrix products  2.63 us (1%)
    ppermute x29, waiting for transfers between devices, move(): return lax.ppermute(x, 'z', [(i, (i + step) % NZ) for i in range(NZ)])  57.5 us
    ppermute x29, starting transfers between devices, move(): return lax.ppermute(x, 'z', [(i, (i + step) % NZ) for i in range(NZ)])  57.3 us
    pallas_call x10, Pallas kernels, call(): pl.pallas_call(body, grid_spec=spec, out_shape=out_shape, input_output_al...  27.7 us
    all_to_all x1, blocking collectives, run(): lax.all_to_all(back_one.reshape(NROW, MB, HALF), 'row', 0, 0, tiled=True)  14.7 us
    all_to_all x1, starting transfers between devices, run(): second = lax.all_to_all(first, 'row', 0, 0, tiled=True).reshape(NB, HALF)  7.61 us
    ppermute x4, waiting for transfers between devices, swap(): return lax.ppermute(x, 'ylo', SWAP)  7.47 us
    all_to_all x1, waiting for transfers between devices, run(): second = lax.all_to_all(first, 'row', 0, 0, tiled=True).reshape(NB, HALF)  4.89 us
    ppermute x4, starting transfers between devices, swap(): return lax.ppermute(x, 'ylo', SWAP)  4.83 us
  transfers between devices with their start and end apart: 34, of which 20 were waited for; matrix products, arithmetic and copies ran while one was open for 4% of the time, Pallas kernels for 10%

profile of v3, /device:TPU:2, one launch (start us, length us, event | category | flops | bytes accessed | tf_op | source)
XLA Modules:
  0.0 200.9 jit_solution(299837532294120663)
XLA Ops:
  7.0 4.4 %shard_map.67 = (bf16[2,8,16,640]{3,2,1,0:T(8,128)(2,1)}, bf16[2,8,16,640]{3,2,1,0:T(8,128)(2,1)S(1)}) custom-call(s32[2]{0:T(128)S(1)} %pad_add_fusion.which._, bf16[2,40,40,640]{3,2,1,0:T(8,128)(2,1)} %here.7, bf16[512,320]{1,0:T(8,128)(2,1)S(1)} %get-tuple-element.52.km), custom_call_target="tpu_custom_call" | custom-call | flops 209715200 | bytes 2211840 | tf_op jit(solution)/shard_map/pallas_call | solution.py:44
  11.4 5.8 %collective-permute-start.11 = (bf16[2,8,16,640]{3,2,1,0:T(8,128)(2,1)S(1)}, bf16[2,8,16,640]{3,2,1,0:T(8,128)(2,1)S(1)}, u32[]{:S(2)}, u32[]{:S(2)}) collective-permute-start(bf16[2,8,16,640]{3,2,1,0:T(8,128)(2,1)S(1)} %get-tuple-element.39), channel_id=1, source_target_pairs={{0,14},{2,0},{4,2},{6,4},{8,6},{10,8},{12,10},{14,12},{1,15},{3,1}... | collective-permute-start | bytes 983048 | tf_op jit(solution)/shard_map/ppermute | solution.py:329
  17.2 4.1 %shard_map.66 = (bf16[2,8,16,640]{3,2,1,0:T(8,128)(2,1)S(1)}, bf16[2,8,16,640]{3,2,1,0:T(8,128)(2,1)S(1)}, bf16[2,8,16,640]{3,2,1,0:T(8,128)(2,1)S(1)}, bf16[2,8...) custom-call(s32[2]{0:T(128)S(1)} %pad_add_fusion.which._, ...), custom_call_target="tpu_custom_call" | custom-call | flops 629145600 | bytes 2211840 | tf_op jit(solution)/shard_map/pallas_call | solution.py:44
  25.0 3.7 %collective-permute-start.12 = (bf16[2,8,16,640]{3,2,1,0:T(8,128)(2,1)}, bf16[2,8,16,640]{3,2,1,0:T(8,128)(2,1)}, u32[]{:S(2)}, u32[]{:S(2)}) collective-permute-start(bf16[2,8,16,640]{3,2,1,0:T(8,128)(2,1)} %add_convert_fusion.3), channel_id=1, source_target_pairs={{0,14},{2,0},{4,2},{6,4},{8,6},{10,8},{12,10},{14,12},{1,15},{3,1}... | collective-permute-start | bytes 983048 | tf_op jit(solution)/shard_map/ppermute | solution.py:329
  32.1 3.0 %collective-permute-done.12 = bf16[2,8,16,640]{3,2,1,0:T(8,128)(2,1)} collective-permute-done((bf16[2,8,16,640]{3,2,1,0:T(8,128)(2,1)}, bf16[2,8,16,640]{3,2,1,0:T(8,128)(2,1)}, u32[]{:S(2)}, u32[]{:S(2)}) %collective-permute-start.12) | collective-permute-done | bytes 327712 | tf_op jit(solution)/shard_map/ppermute | solution.py:329
  36.2 3.8 %collective-permute-start.13 = (bf16[2,8,16,640]{3,2,1,0:T(8,128)(2,1)S(1)}, bf16[2,8,16,640]{3,2,1,0:T(8,128)(2,1)S(1)}, u32[]{:S(2)}, u32[]{:S(2)}) collective-permute-start(bf16[2,8,16,640]{3,2,1,0:T(8,128)(2,1)S(1)} %add_convert_fusion.2), channel_id=1, source_target_pairs={{0,14},{2,0},{4,2},{6,4},{8,6},{10,8},{12,10},{14,12},{1,15},{3,1}... | collective-permute-start | bytes 983048 | tf_op jit(solution)/shard_map/ppermute | solution.py:329
  41.5 3.8 %collective-permute-done.13 = bf16[2,8,16,640]{3,2,1,0:T(8,128)(2,1)S(1)} collective-permute-done((bf16[2,8,16,640]{3,2,1,0:T(8,128)(2,1)S(1)}, bf16[2,8,16,640]{3,2,1,0:T(8,128)(2,1)S(1)}, u32[]{:S(2)}, u32[]{:S(2)}) %collective-permute-start.13) | collective-permute-done | bytes 327712 | tf_op jit(solution)/shard_map/ppermute | solution.py:329
  45.4 3.8 %collective-permute-start.14 = (bf16[2,8,16,640]{3,2,1,0:T(8,128)(2,1)S(1)}, bf16[2,8,16,640]{3,2,1,0:T(8,128)(2,1)S(1)}, u32[]{:S(2)}, u32[]{:S(2)}) collective-permute-start(bf16[2,8,16,640]{3,2,1,0:T(8,128)(2,1)S(1)} %add_convert_fusion.1), channel_id=1, source_target_pairs={{0,14},{2,0},{4,2},{6,4},{8,6},{10,8},{12,10},{14,12},{1,15},{3,1}... | collective-permute-start | bytes 983048 | tf_op jit(solution)/shard_map/ppermute | solution.py:329
  49.1 7.5 %collective-permute-done.came = bf16[40,24,640]{2,1,0:T(8,128)(2,1)S(1)} collective-permute-done((bf16[40,24,640]{2,1,0:T(8,128)(2,1)}, bf16[40,24,640]{2,1,0:T(8,128)(2,1)S(1)}, u32[]{:S(2)}, u32[]{:S(2)}) %collective-permute-start) | collective-permute-done | bytes 1228832 | tf_op jit(solution)/shard_map/ppermute | solution.py:333
  56.6 3.5 %shard_map.65 = (bf16[8,24,640]{2,1,0:T(8,128)(2,1)S(1)}, bf16[8,24,640]{2,1,0:T(8,128)(2,1)S(1)}, bf16[8,24,640]{2,1,0:T(8,128)(2,1)S(1)}) custom-call(s32[2]{0:T(128)S(1)} %pad_add_fusion.which._, bf16[2,40,40,640]{3,2,1,0:T(8,128)(2,1)} %here.7, bf16[40,24,640]{2,1,0:T(8,128)(2,1)S(1)} %collective-permute-done.came, ...), custom_call_target="tpu_custom_call" | custom-call | flops 471859200 | bytes 2990080 | tf_op jit(solution)/shard_map/pallas_call | solution.py:44
  60.3 3.1 %collective-permute-start.5 = (bf16[8,24,640]{2,1,0:T(8,128)(2,1)S(1)}, bf16[8,24,640]{2,1,0:T(8,128)(2,1)S(1)}, u32[]{:S(2)}, u32[]{:S(2)}) collective-permute-start(bf16[8,24,640]{2,1,0:T(8,128)(2,1)S(1)} %get-tuple-element.32), channel_id=1, source_target_pairs={{0,14},{2,0},{4,2},{6,4},{8,6},{10,8},{12,10},{14,12},{1,15},{3,1}... | collective-permute-start | bytes 737288 | tf_op jit(solution)/shard_map/ppermute | solution.py:329
  63.5 3.9 %shard_map.64 = (bf16[8,24,640]{2,1,0:T(8,128)(2,1)S(1)}, bf16[8,24,640]{2,1,0:T(8,128)(2,1)S(1)}, bf16[8,24,640]{2,1,0:T(8,128)(2,1)S(1)}, bf16[8,24,640]{2,1,0:T(8,128)(2,1)S(1)}, bf16[8,24,640]{2,1,0:T(8,128)(2,1)S(1)}) custom-call(s32[2]{0:T(128)S(1)} %pad_add_fusion.which._, bf16[2,40,40,640]{3,2,1,0:T(8,128)(2,1)} %here.7, ...), custom_call_target="tpu_custom_call" | custom-call | flops 786432000 | bytes 2990080 | tf_op jit(solution)/shard_map/pallas_call | solution.py:44
  67.6 7.1 %collective-permute-done.1 = bf16[8,24,640]{2,1,0:T(8,128)(2,1)S(1)} collective-permute-done((bf16[8,24,640]{2,1,0:T(8,128)(2,1)S(1)}, bf16[8,24,640]{2,1,0:T(8,128)(2,1)S(1)}, u32[]{:S(2)}, u32[]{:S(2)}) %collective-permute-start.1) | collective-permute-done | bytes 245792 | tf_op jit(solution)/shard_map/ppermute | solution.py:329
  74.8 6.1 %collective-permute-start.3 = (bf16[8,24,640]{2,1,0:T(8,128)(2,1)S(1)}, bf16[8,24,640]{2,1,0:T(8,128)(2,1)S(1)}, u32[]{:S(2)}, u32[]{:S(2)}) collective-permute-start(bf16[8,24,640]{2,1,0:T(8,128)(2,1)S(1)} %add_convert_fusion.10), channel_id=1, source_target_pairs={{0,2},{2,4},{4,6},{6,8},{8,10},{10,12},{12,14},{14,0},{1,3},{3,5},... | collective-permute-start | bytes 737288 | tf_op jit(solution)/shard_map/ppermute | solution.py:329
  82.8 3.5 %collective-permute-done.3 = bf16[8,24,640]{2,1,0:T(8,128)(2,1)S(1)} collective-permute-done((bf16[8,24,640]{2,1,0:T(8,128)(2,1)S(1)}, bf16[8,24,640]{2,1,0:T(8,128)(2,1)S(1)}, u32[]{:S(2)}, u32[]{:S(2)}) %collective-permute-start.3) | collective-permute-done | bytes 245792 | tf_op jit(solution)/shard_map/ppermute | solution.py:329
  90.1 3.8 %collective-permute-done.4 = bf16[8,24,640]{2,1,0:T(8,128)(2,1)S(1)} collective-permute-done((bf16[8,24,640]{2,1,0:T(8,128)(2,1)S(1)}, bf16[8,24,640]{2,1,0:T(8,128)(2,1)S(1)}, u32[]{:S(2)}, u32[]{:S(2)}) %collective-permute-start.4) | collective-permute-done | bytes 245792 | tf_op jit(solution)/shard_map/ppermute | solution.py:329
  97.2 7.6 %all-to-all-start = ((bf16[16,40,288]{2,1,0:T(8,128)(2,1)}), bf16[16,40,288]{2,1,0:T(8,128)(2,1)S(1)}, u32[]{:S(2)}, u32[]{:S(2)}) async-start(bf16[16,40,288]{2,1,0:T(8,128)(2,1)} %shard_map.68), calls=%async_computation | async-start | bytes 983040 | tf_op jit(solution)/shard_map/all_to_all | solution.py:416
  108.4 4.9 %all-to-all-done = bf16[16,40,288]{2,1,0:T(8,128)(2,1)S(1)} async-done(((bf16[16,40,288]{2,1,0:T(8,128)(2,1)}), bf16[16,40,288]{2,1,0:T(8,128)(2,1)S(1)}, u32[]{:S(2)}, u32[]{:S(2)}) %all-to-all-start) | async-done | bytes 368672 | tf_op jit(solution)/shard_map/all_to_all | solution.py:416
  114.5 14.7 %all_to_all.10.x = bf16[16,40,288]{2,1,0:T(8,128)(2,1)S(1)} all-to-all(bf16[16,40,288]{2,1,0:T(8,128)(2,1)S(1)} %bitcast.36), channel_id=1, replica_groups=mesh['row'=16,'z'=8,'ylo'=2] {'row'}, dimensions={0} | all-to-all | bytes 737280 | tf_op jit(solution)/shard_map/all_to_all | solution.py:418
  129.9 3.2 %collective-permute-start.16 = (bf16[8,24,640]{2,1,0:T(8,128)(2,1)S(1)}, bf16[8,24,640]{2,1,0:T(8,128)(2,1)S(1)}, u32[]{:S(2)}, u32[]{:S(2)}) collective-permute-start(bf16[8,24,640]{2,1,0:T(8,128)(2,1)S(1)} %get-tuple-element.43.refs_6_), channel_id=1, source_target_pairs={{0,14},{2,0},{4,2},{6,4},{8,6},{10,8},{12,10},{14,12},{1,15},{3,1}... | collective-permute-start | bytes 737288 | tf_op jit(solution)/shard_map/ppermute | solution.py:329
  133.1 6.8 %collective-permute-done.19.refs_5_ = bf16[8,24,640]{2,1,0:T(8,128)(2,1)S(1)} collective-permute-done((bf16[8,24,640]{2,1,0:T(8,128)(2,1)S(1)}, bf16[8,24,640]{2,1,0:T(8,128)(2,1)S(1)}, u32[]{:S(2)}, u32[]{:S(2)}) %collective-permute-start.19) | collective-permute-done | bytes 245792 | tf_op jit(solution)/shard_map/ppermute | solution.py:329
  139.9 3.2 %collective-permute-start.17 = (bf16[8,24,640]{2,1,0:T(8,128)(2,1)S(1)}, bf16[8,24,640]{2,1,0:T(8,128)(2,1)S(1)}, u32[]{:S(2)}, u32[]{:S(2)}) collective-permute-start(bf16[8,24,640]{2,1,0:T(8,128)(2,1)S(1)} %collective-permute-done.16.refs_7_), channel_id=1, source_target_pairs={{0,14},{2,0},{4,2},{6,4},{8,6},{10,8},{12,10},{14,12},{1,15},{3,1}... | collective-permute-start | bytes 737288 | tf_op jit(solution)/shard_map/ppermute | solution.py:329
  143.8 5.2 %collective-permute-done.20.refs_4_ = bf16[8,24,640]{2,1,0:T(8,128)(2,1)S(1)} collective-permute-done((bf16[8,24,640]{2,1,0:T(8,128)(2,1)S(1)}, bf16[8,24,640]{2,1,0:T(8,128)(2,1)S(1)}, u32[]{:S(2)}, u32[]{:S(2)}) %collective-permute-start.20) | collective-permute-done | bytes 245792 | tf_op jit(solution)/shard_map/ppermute | solution.py:329
  149.1 3.2 %collective-permute-start.18 = (bf16[8,24,640]{2,1,0:T(8,128)(2,1)S(1)}, bf16[8,24,640]{2,1,0:T(8,128)(2,1)S(1)}, u32[]{:S(2)}, u32[]{:S(2)}) collective-permute-start(bf16[8,24,640]{2,1,0:T(8,128)(2,1)S(1)} %collective-permute-done.17.refs_8_), channel_id=1, source_target_pairs={{0,14},{2,0},{4,2},{6,4},{8,6},{10,8},{12,10},{14,12},{1,15},{3,1}... | collective-permute-start | bytes 737288 | tf_op jit(solution)/shard_map/ppermute | solution.py:329
  152.5 4.2 %collective-permute-start.22 = (bf16[4,24,640]{2,1,0:T(8,128)(2,1)S(1)}, bf16[4,24,640]{2,1,0:T(8,128)(2,1)S(1)}, u32[]{:S(2)}, u32[]{:S(2)}) collective-permute-start(bf16[4,24,640]{2,1,0:T(8,128)(2,1)S(1)} %slice.37), channel_id=1, source_target_pairs={{0,12},{2,14},{4,0},{6,2},{8,4},{10,6},{12,8},{14,10},{1,13},{3,15... | collective-permute-start | bytes 368648 | tf_op jit(solution)/shard_map/ppermute | solution.py:329
  156.8 3.7 %collective-permute-done.21.refs_1_ = bf16[4,24,640]{2,1,0:T(8,128)(2,1)S(1)} collective-permute-done((bf16[4,24,640]{2,1,0:T(8,128)(2,1)S(1)}, bf16[4,24,640]{2,1,0:T(8,128)(2,1)S(1)}, u32[]{:S(2)}, u32[]{:S(2)}) %collective-permute-start.21) | collective-permute-done | bytes 122912 | tf_op jit(solution)/shard_map/ppermute | solution.py:329
  160.5 3.5 %collective-permute-done.22.refs_2_ = bf16[4,24,640]{2,1,0:T(8,128)(2,1)S(1)} collective-permute-done((bf16[4,24,640]{2,1,0:T(8,128)(2,1)S(1)}, bf16[4,24,640]{2,1,0:T(8,128)(2,1)S(1)}, u32[]{:S(2)}, u32[]{:S(2)}) %collective-permute-start.22) | collective-permute-done | bytes 122912 | tf_op jit(solution)/shard_map/ppermute | solution.py:329
  169.0 3.7 %collective-permute-start.27 = (bf16[2,8,16,640]{3,2,1,0:T(8,128)(2,1)S(1)}, bf16[2,8,16,640]{3,2,1,0:T(8,128)(2,1)S(1)}, u32[]{:S(2)}, u32[]{:S(2)}) collective-permute-start(bf16[2,8,16,640]{3,2,1,0:T(8,128)(2,1)S(1)} %collective-permute-done.26.refs_6_), channel_id=1, source_target_pairs={{0,14},{2,0},{4,2},{6,4},{8,6},{10,8},{12,10},{14,12},{1,15},{3,1}... | collective-permute-start | bytes 983048 | tf_op jit(solution)/shard_map/ppermute | solution.py:329
  177.9 3.7 %collective-permute-start.28 = (bf16[2,8,16,640]{3,2,1,0:T(8,128)(2,1)S(1)}, bf16[2,8,16,640]{3,2,1,0:T(8,128)(2,1)S(1)}, u32[]{:S(2)}, u32[]{:S(2)}) collective-permute-start(bf16[2,8,16,640]{3,2,1,0:T(8,128)(2,1)S(1)} %collective-permute-done.27.refs_7_), channel_id=1, source_target_pairs={{0,14},{2,0},{4,2},{6,4},{8,6},{10,8},{12,10},{14,12},{1,15},{3,1}... | collective-permute-start | bytes 983048 | tf_op jit(solution)/shard_map/ppermute | solution.py:329
  181.6 5.6 %collective-permute-done.31.refs_3_ = bf16[2,8,16,640]{3,2,1,0:T(8,128)(2,1)S(1)} collective-permute-done((bf16[2,8,16,640]{3,2,1,0:T(8,128)(2,1)S(1)}, bf16[2,8,16,640]{3,2,1,0:T(8,128)(2,1)S(1)}, u32[]{:S(2)}, u32[]{:S(2)}) %collective-permute-start.31) | collective-permute-done | bytes 327712 | tf_op jit(solution)/shard_map/ppermute | solution.py:329
  190.4 3.1 %shard_map.72.refs_9_ = bf16[2,40,40,640]{3,2,1,0:T(8,128)(2,1)} custom-call(s32[2]{0:T(128)S(1)} %pad_add_fusion.which._, bf16[8,24,640]{2,1,0:T(8,128)(2,1)S(1)} %collective-permute-done.18.refs_0_, bf16[4,24,640]{2,1,0:T(8,128)(2,1)S(1)} %collective-permute-done.21.refs_1_, bf16[4,24,640]{2,1,0:T(8,128)(2,1)S(1)} %collective-permute-done.22.refs_2_, ...), custom_call_target="tpu_custom_call" | custom-call | flops 629145600 | bytes 1146880 | tf_op jit(solution)/shard_map/pallas_call | solution.py:44
  195.5 3.7 %shard_map.73._ = bf16[2,40,40,640]{3,2,1,0:T(8,128)(2,1)} custom-call(s32[2]{0:T(128)S(1)} %pad_add_fusion.which._, bf16[2,8,16,640]{3,2,1,0:T(8,128)(2,1)S(1)} %collective-permute-done.28.refs_0_, bf16[2,8,16,640]{3,2,1,0:T(8,128)(2,1)S(1)} %collective-permute-done.29.refs_1_, ...), custom_call_target="tpu_custom_call", output_to_operand_aliasing={{}: (10, {})} | custom-call | flops 838860800 | bytes 3522560 | tf_op jit(solution)/shard_map/pallas_call | solution.py:44
  (119 shorter events, 49.5 us)
Async XLA Ops:
  11.4 12.8 %collective-permute-start.11 = (bf16[2,8,16,640]{3,2,1,0:T(8,128)(2,1)S(1)}, bf16[2,8,16,640]{3,2,1,0:T(8,128)(2,1)S(1)}, u32[]{:S(2)}, u32[]{:S(2)}) collective-permute-start(bf16[2,8,16,640]{3,2,1,0:T(8,128)(2,1)S(1)} %get-tuple-element.39), channel_id=1, source_target_pairs={{0,14},{2,0},{4,2},{6,4},{8,6},{10,8},{12,10},{14,12},{1,15},{3,1}... | collective-permute-start | bytes 983048 | tf_op jit(solution)/shard_map/ppermute | solution.py:329
  17.2 13.6 %collective-permute-start.8 = (bf16[2,8,16,640]{3,2,1,0:T(8,128)(2,1)}, bf16[2,8,16,640]{3,2,1,0:T(8,128)(2,1)}, u32[]{:S(2)}, u32[]{:S(2)}) collective-permute-start(bf16[2,8,16,640]{3,2,1,0:T(8,128)(2,1)} %get-tuple-element.36), channel_id=1, source_target_pairs={{0,2},{2,4},{4,6},{6,8},{8,10},{10,12},{12,14},{14,0},{1,3},{3,5},... | collective-permute-start | bytes 983048 | tf_op jit(solution)/shard_map/ppermute | solution.py:329
  25.0 10.1 %collective-permute-start.12 = (bf16[2,8,16,640]{3,2,1,0:T(8,128)(2,1)}, bf16[2,8,16,640]{3,2,1,0:T(8,128)(2,1)}, u32[]{:S(2)}, u32[]{:S(2)}) collective-permute-start(bf16[2,8,16,640]{3,2,1,0:T(8,128)(2,1)} %add_convert_fusion.3), channel_id=1, source_target_pairs={{0,14},{2,0},{4,2},{6,4},{8,6},{10,8},{12,10},{14,12},{1,15},{3,1}... | collective-permute-start | bytes 983048 | tf_op jit(solution)/shard_map/ppermute | solution.py:329
  28.7 27.9 %collective-permute-start = (bf16[40,24,640]{2,1,0:T(8,128)(2,1)}, bf16[40,24,640]{2,1,0:T(8,128)(2,1)S(1)}, u32[]{:S(2)}, u32[]{:S(2)}) collective-permute-start(bf16[40,24,640]{2,1,0:T(8,128)(2,1)} %lift.1), channel_id=1, source_target_pairs={{0,1},{1,0},{2,3},{3,2},{4,5},{5,4},{6,7},{7,6},{8,9},{9,8},{10,11... | collective-permute-start | bytes 3686408 | tf_op jit(solution)/shard_map/ppermute | solution.py:333
  32.0 9.3 %collective-permute-start.9 = (bf16[2,8,16,640]{3,2,1,0:T(8,128)(2,1)S(1)}, bf16[2,8,16,640]{3,2,1,0:T(8,128)(2,1)S(1)}, u32[]{:S(2)}, u32[]{:S(2)}) collective-permute-start(bf16[2,8,16,640]{3,2,1,0:T(8,128)(2,1)S(1)} %add_convert_fusion.5), channel_id=1, source_target_pairs={{0,2},{2,4},{4,6},{6,8},{8,10},{10,12},{12,14},{14,0},{1,3},{3,5},... | collective-permute-start | bytes 983048 | tf_op jit(solution)/shard_map/ppermute | solution.py:329
  36.2 9.0 %collective-permute-start.13 = (bf16[2,8,16,640]{3,2,1,0:T(8,128)(2,1)S(1)}, bf16[2,8,16,640]{3,2,1,0:T(8,128)(2,1)S(1)}, u32[]{:S(2)}, u32[]{:S(2)}) collective-permute-start(bf16[2,8,16,640]{3,2,1,0:T(8,128)(2,1)S(1)} %add_convert_fusion.2), channel_id=1, source_target_pairs={{0,14},{2,0},{4,2},{6,4},{8,6},{10,8},{12,10},{14,12},{1,15},{3,1}... | collective-permute-start | bytes 983048 | tf_op jit(solution)/shard_map/ppermute | solution.py:329
  41.4 26.0 %collective-permute-start.10 = (bf16[2,8,16,640]{3,2,1,0:T(8,128)(2,1)S(1)}, bf16[2,8,16,640]{3,2,1,0:T(8,128)(2,1)S(1)}, u32[]{:S(2)}, u32[]{:S(2)}) collective-permute-start(bf16[2,8,16,640]{3,2,1,0:T(8,128)(2,1)S(1)} %add_convert_fusion.4), channel_id=1, source_target_pairs={{0,2},{2,4},{4,6},{6,8},{8,10},{10,12},{12,14},{14,0},{1,3},{3,5},... | collective-permute-start | bytes 983048 | tf_op jit(solution)/shard_map/ppermute | solution.py:329
  45.4 22.1 %collective-permute-start.14 = (bf16[2,8,16,640]{3,2,1,0:T(8,128)(2,1)S(1)}, bf16[2,8,16,640]{3,2,1,0:T(8,128)(2,1)S(1)}, u32[]{:S(2)}, u32[]{:S(2)}) collective-permute-start(bf16[2,8,16,640]{3,2,1,0:T(8,128)(2,1)S(1)} %add_convert_fusion.1), channel_id=1, source_target_pairs={{0,14},{2,0},{4,2},{6,4},{8,6},{10,8},{12,10},{14,12},{1,15},{3,1}... | collective-permute-start | bytes 983048 | tf_op jit(solution)/shard_map/ppermute | solution.py:329
  60.1 14.5 %collective-permute-start.1 = (bf16[8,24,640]{2,1,0:T(8,128)(2,1)S(1)}, bf16[8,24,640]{2,1,0:T(8,128)(2,1)S(1)}, u32[]{:S(2)}, u32[]{:S(2)}) collective-permute-start(bf16[8,24,640]{2,1,0:T(8,128)(2,1)S(1)} %get-tuple-element.28), channel_id=1, source_target_pairs={{0,2},{2,4},{4,6},{6,8},{8,10},{10,12},{12,14},{14,0},{1,3},{3,5},... | collective-permute-start | bytes 737288 | tf_op jit(solution)/shard_map/ppermute | solution.py:329
  60.2 14.4 %collective-permute-start.2 = (bf16[8,24,640]{2,1,0:T(8,128)(2,1)S(1)}, bf16[8,24,640]{2,1,0:T(8,128)(2,1)S(1)}, u32[]{:S(2)}, u32[]{:S(2)}) collective-permute-start(bf16[8,24,640]{2,1,0:T(8,128)(2,1)S(1)} %get-tuple-element.30), channel_id=1, source_target_pairs={{0,4},{2,6},{4,8},{6,10},{8,12},{10,14},{12,0},{14,2},{1,5},{3,7},... | collective-permute-start | bytes 737288 | tf_op jit(solution)/shard_map/ppermute | solution.py:329
  60.3 20.6 %collective-permute-start.5 = (bf16[8,24,640]{2,1,0:T(8,128)(2,1)S(1)}, bf16[8,24,640]{2,1,0:T(8,128)(2,1)S(1)}, u32[]{:S(2)}, u32[]{:S(2)}) collective-permute-start(bf16[8,24,640]{2,1,0:T(8,128)(2,1)S(1)} %get-tuple-element.32), channel_id=1, source_target_pairs={{0,14},{2,0},{4,2},{6,4},{8,6},{10,8},{12,10},{14,12},{1,15},{3,1}... | collective-permute-start | bytes 737288 | tf_op jit(solution)/shard_map/ppermute | solution.py:329
  74.8 11.5 %collective-permute-start.3 = (bf16[8,24,640]{2,1,0:T(8,128)(2,1)S(1)}, bf16[8,24,640]{2,1,0:T(8,128)(2,1)S(1)}, u32[]{:S(2)}, u32[]{:S(2)}) collective-permute-start(bf16[8,24,640]{2,1,0:T(8,128)(2,1)S(1)} %add_convert_fusion.10), channel_id=1, source_target_pairs={{0,2},{2,4},{4,6},{6,8},{8,10},{10,12},{12,14},{14,0},{1,3},{3,5},... | collective-permute-start | bytes 737288 | tf_op jit(solution)/shard_map/ppermute | solution.py:329
  81.0 8.2 %collective-permute-start.6 = (bf16[8,24,640]{2,1,0:T(8,128)(2,1)S(1)}, bf16[8,24,640]{2,1,0:T(8,128)(2,1)S(1)}, u32[]{:S(2)}, u32[]{:S(2)}) collective-permute-start(bf16[8,24,640]{2,1,0:T(8,128)(2,1)S(1)} %add_convert_fusion.8), channel_id=1, source_target_pairs={{0,14},{2,0},{4,2},{6,4},{8,6},{10,8},{12,10},{14,12},{1,15},{3,1}... | collective-permute-start | bytes 737288 | tf_op jit(solution)/shard_map/ppermute | solution.py:329
  81.1 8.9 %collective-permute-start.15 = (bf16[8,16,640]{2,1,0:T(8,128)(2,1)S(1)}, bf16[8,16,640]{2,1,0:T(8,128)(2,1)S(1)}, u32[]{:S(2)}, u32[]{:S(2)}) collective-permute-start(bf16[8,16,640]{2,1,0:T(8,128)(2,1)S(1)} %slice_bitcast_fusion.2), channel_id=1, source_target_pairs={{0,1},{1,0},{2,3},{3,2},{4,5},{5,4},{6,7},{7,6},{8,9},{9,8},{10,11... | collective-permute-start | bytes 491528 | tf_op jit(solution)/shard_map/ppermute | solution.py:333
  97.2 16.0 %all-to-all-start = ((bf16[16,40,288]{2,1,0:T(8,128)(2,1)}), bf16[16,40,288]{2,1,0:T(8,128)(2,1)S(1)}, u32[]{:S(2)}, u32[]{:S(2)}) async-start(bf16[16,40,288]{2,1,0:T(8,128)(2,1)} %shard_map.68), calls=%async_computation | async-start | bytes 983040 | tf_op jit(solution)/shard_map/all_to_all | solution.py:416
  129.8 10.1 %collective-permute-start.19 = (bf16[8,24,640]{2,1,0:T(8,128)(2,1)S(1)}, bf16[8,24,640]{2,1,0:T(8,128)(2,1)S(1)}, u32[]{:S(2)}, u32[]{:S(2)}) collective-permute-start(bf16[8,24,640]{2,1,0:T(8,128)(2,1)S(1)} %get-tuple-element.43.refs_6_), channel_id=1, source_target_pairs={{0,2},{2,4},{4,6},{6,8},{8,10},{10,12},{12,14},{14,0},{1,3},{3,5},... | collective-permute-start | bytes 737288 | tf_op jit(solution)/shard_map/ppermute | solution.py:329
  129.9 10.0 %collective-permute-start.16 = (bf16[8,24,640]{2,1,0:T(8,128)(2,1)S(1)}, bf16[8,24,640]{2,1,0:T(8,128)(2,1)S(1)}, u32[]{:S(2)}, u32[]{:S(2)}) collective-permute-start(bf16[8,24,640]{2,1,0:T(8,128)(2,1)S(1)} %get-tuple-element.43.refs_6_), channel_id=1, source_target_pairs={{0,14},{2,0},{4,2},{6,4},{8,6},{10,8},{12,10},{14,12},{1,15},{3,1}... | collective-permute-start | bytes 737288 | tf_op jit(solution)/shard_map/ppermute | solution.py:329
  139.9 9.2 %collective-permute-start.20 = (bf16[8,24,640]{2,1,0:T(8,128)(2,1)S(1)}, bf16[8,24,640]{2,1,0:T(8,128)(2,1)S(1)}, u32[]{:S(2)}, u32[]{:S(2)}) collective-permute-start(bf16[8,24,640]{2,1,0:T(8,128)(2,1)S(1)} %collective-permute-done.19.refs_5_), channel_id=1, source_target_pairs={{0,2},{2,4},{4,6},{6,8},{8,10},{10,12},{12,14},{14,0},{1,3},{3,5},... | collective-permute-start | bytes 737288 | tf_op jit(solution)/shard_map/ppermute | solution.py:329
  139.9 9.2 %collective-permute-start.17 = (bf16[8,24,640]{2,1,0:T(8,128)(2,1)S(1)}, bf16[8,24,640]{2,1,0:T(8,128)(2,1)S(1)}, u32[]{:S(2)}, u32[]{:S(2)}) collective-permute-start(bf16[8,24,640]{2,1,0:T(8,128)(2,1)S(1)} %collective-permute-done.16.refs_7_), channel_id=1, source_target_pairs={{0,14},{2,0},{4,2},{6,4},{8,6},{10,8},{12,10},{14,12},{1,15},{3,1}... | collective-permute-start | bytes 737288 | tf_op jit(solution)/shard_map/ppermute | solution.py:329
  143.1 13.5 %collective-permute-start.25 = (bf16[8,16,640]{2,1,0:T(8,128)(2,1)S(1)}, bf16[8,16,640]{2,1,0:T(8,128)(2,1)S(1)}, u32[]{:S(2)}, u32[]{:S(2)}) collective-permute-start(bf16[8,16,640]{2,1,0:T(8,128)(2,1)S(1)} %get-tuple-element.44), channel_id=1, source_target_pairs={{0,1},{1,0},{2,3},{3,2},{4,5},{5,4},{6,7},{7,6},{8,9},{9,8},{10,11... | collective-permute-start | bytes 491528 | tf_op jit(solution)/shard_map/ppermute | solution.py:333
  149.1 14.8 %collective-permute-start.23 = (bf16[8,24,640]{2,1,0:T(8,128)(2,1)S(1)}, bf16[8,24,640]{2,1,0:T(8,128)(2,1)S(1)}, u32[]{:S(2)}, u32[]{:S(2)}) collective-permute-start(bf16[8,24,640]{2,1,0:T(8,128)(2,1)S(1)} %collective-permute-done.20.refs_4_), channel_id=1, source_target_pairs={{0,2},{2,4},{4,6},{6,8},{8,10},{10,12},{12,14},{14,0},{1,3},{3,5},... | collective-permute-start | bytes 737288 | tf_op jit(solution)/shard_map/ppermute | solution.py:329
  149.1 14.8 %collective-permute-start.18 = (bf16[8,24,640]{2,1,0:T(8,128)(2,1)S(1)}, bf16[8,24,640]{2,1,0:T(8,128)(2,1)S(1)}, u32[]{:S(2)}, u32[]{:S(2)}) collective-permute-start(bf16[8,24,640]{2,1,0:T(8,128)(2,1)S(1)} %collective-permute-done.17.refs_8_), channel_id=1, source_target_pairs={{0,14},{2,0},{4,2},{6,4},{8,6},{10,8},{12,10},{14,12},{1,15},{3,1}... | collective-permute-start | bytes 737288 | tf_op jit(solution)/shard_map/ppermute | solution.py:329
  152.3 8.1 %collective-permute-start.21 = (bf16[4,24,640]{2,1,0:T(8,128)(2,1)S(1)}, bf16[4,24,640]{2,1,0:T(8,128)(2,1)S(1)}, u32[]{:S(2)}, u32[]{:S(2)}) collective-permute-start(bf16[4,24,640]{2,1,0:T(8,128)(2,1)S(1)} %slice.36), channel_id=1, source_target_pairs={{0,4},{2,6},{4,8},{6,10},{8,12},{10,14},{12,0},{14,2},{1,5},{3,7},... | collective-permute-start | bytes 368648 | tf_op jit(solution)/shard_map/ppermute | solution.py:329
  152.5 11.5 %collective-permute-start.22 = (bf16[4,24,640]{2,1,0:T(8,128)(2,1)S(1)}, bf16[4,24,640]{2,1,0:T(8,128)(2,1)S(1)}, u32[]{:S(2)}, u32[]{:S(2)}) collective-permute-start(bf16[4,24,640]{2,1,0:T(8,128)(2,1)S(1)} %slice.37), channel_id=1, source_target_pairs={{0,12},{2,14},{4,0},{6,2},{8,4},{10,6},{12,8},{14,10},{1,13},{3,15... | collective-permute-start | bytes 368648 | tf_op jit(solution)/shard_map/ppermute | solution.py:329
  156.7 12.3 %collective-permute-start.26 = (bf16[2,8,16,640]{3,2,1,0:T(8,128)(2,1)S(1)}, bf16[2,8,16,640]{3,2,1,0:T(8,128)(2,1)S(1)}, u32[]{:S(2)}, u32[]{:S(2)}) collective-permute-start(bf16[2,8,16,640]{3,2,1,0:T(8,128)(2,1)S(1)} %pad_maximum_fusion.2.refs_5_), channel_id=1, source_target_pairs={{0,14},{2,0},{4,2},{6,4},{8,6},{10,8},{12,10},{14,12},{1,15},{3,1}... | collective-permute-start | bytes 983048 | tf_op jit(solution)/shard_map/ppermute | solution.py:329
  165.6 33.6 %collective-permute-start.24 = (bf16[40,24,640]{2,1,0:T(8,128)(2,1)S(1)}, bf16[40,24,640]{2,1,0:T(8,128)(2,1)S(1)}, u32[]{:S(2)}, u32[]{:S(2)}) collective-permute-start(bf16[40,24,640]{2,1,0:T(8,128)(2,1)S(1)} %shard_map.71), channel_id=1, source_target_pairs={{0,1},{1,0},{2,3},{3,2},{4,5},{5,4},{6,7},{7,6},{8,9},{9,8},{10,11... | collective-permute-start | bytes 3686408 | tf_op jit(solution)/shard_map/ppermute | solution.py:333
  166.4 8.6 %collective-permute-start.30 = (bf16[2,8,16,640]{3,2,1,0:T(8,128)(2,1)S(1)}, bf16[2,8,16,640]{3,2,1,0:T(8,128)(2,1)S(1)}, u32[]{:S(2)}, u32[]{:S(2)}) collective-permute-start(bf16[2,8,16,640]{3,2,1,0:T(8,128)(2,1)S(1)} %pad_maximum_fusion.2.refs_5_), channel_id=1, source_target_pairs={{0,2},{2,4},{4,6},{6,8},{8,10},{10,12},{12,14},{14,0},{1,3},{3,5},... | collective-permute-start | bytes 983048 | tf_op jit(solution)/shard_map/ppermute | solution.py:329
  169.0 9.0 %collective-permute-start.27 = (bf16[2,8,16,640]{3,2,1,0:T(8,128)(2,1)S(1)}, bf16[2,8,16,640]{3,2,1,0:T(8,128)(2,1)S(1)}, u32[]{:S(2)}, u32[]{:S(2)}) collective-permute-start(bf16[2,8,16,640]{3,2,1,0:T(8,128)(2,1)S(1)} %collective-permute-done.26.refs_6_), channel_id=1, source_target_pairs={{0,14},{2,0},{4,2},{6,4},{8,6},{10,8},{12,10},{14,12},{1,15},{3,1}... | collective-permute-start | bytes 983048 | tf_op jit(solution)/shard_map/ppermute | solution.py:329
  175.0 12.2 %collective-permute-start.31 = (bf16[2,8,16,640]{3,2,1,0:T(8,128)(2,1)S(1)}, bf16[2,8,16,640]{3,2,1,0:T(8,128)(2,1)S(1)}, u32[]{:S(2)}, u32[]{:S(2)}) collective-permute-start(bf16[2,8,16,640]{3,2,1,0:T(8,128)(2,1)S(1)} %collective-permute-done.30.refs_4_), channel_id=1, source_target_pairs={{0,2},{2,4},{4,6},{6,8},{8,10},{10,12},{12,14},{14,0},{1,3},{3,5},... | collective-permute-start | bytes 983048 | tf_op jit(solution)/shard_map/ppermute | solution.py:329
  177.9 9.7 %collective-permute-start.28 = (bf16[2,8,16,640]{3,2,1,0:T(8,128)(2,1)S(1)}, bf16[2,8,16,640]{3,2,1,0:T(8,128)(2,1)S(1)}, u32[]{:S(2)}, u32[]{:S(2)}) collective-permute-start(bf16[2,8,16,640]{3,2,1,0:T(8,128)(2,1)S(1)} %collective-permute-done.27.refs_7_), channel_id=1, source_target_pairs={{0,14},{2,0},{4,2},{6,4},{8,6},{10,8},{12,10},{14,12},{1,15},{3,1}... | collective-permute-start | bytes 983048 | tf_op jit(solution)/shard_map/ppermute | solution.py:329
  187.2 8.3 %collective-permute-start.32 = (bf16[2,8,16,640]{3,2,1,0:T(8,128)(2,1)S(1)}, bf16[2,8,16,640]{3,2,1,0:T(8,128)(2,1)S(1)}, u32[]{:S(2)}, u32[]{:S(2)}) collective-permute-start(bf16[2,8,16,640]{3,2,1,0:T(8,128)(2,1)S(1)} %collective-permute-done.31.refs_3_), channel_id=1, source_target_pairs={{0,2},{2,4},{4,6},{6,8},{8,10},{10,12},{12,14},{14,0},{1,3},{3,5},... | collective-permute-start | bytes 983048 | tf_op jit(solution)/shard_map/ppermute | solution.py:329
  187.7 7.8 %collective-permute-start.29 = (bf16[2,8,16,640]{3,2,1,0:T(8,128)(2,1)S(1)}, bf16[2,8,16,640]{3,2,1,0:T(8,128)(2,1)S(1)}, u32[]{:S(2)}, u32[]{:S(2)}) collective-permute-start(bf16[2,8,16,640]{3,2,1,0:T(8,128)(2,1)S(1)} %collective-permute-done.28.refs_0_), channel_id=1, source_target_pairs={{0,14},{2,0},{4,2},{6,4},{8,6},{10,8},{12,10},{14,12},{1,15},{3,1}... | collective-permute-start | bytes 983048 | tf_op jit(solution)/shard_map/ppermute | solution.py:329
  (18 other events, 320.1 us)

commit v4 on v3

--- a/solution.py
+++ b/solution.py
@@ -74,12 +74,16 @@
     return pl.BlockSpec(shape, lambda *_: (0,) * len(shape))
 
 
-CUTS = 5
+CUTS = 4
 CUT = LB // CUTS
+FLOWS = 2
+FLOW = LB // FLOWS
 
 
 def lift(slab, pick):
-    def body(which, src, dst, hold, came, went):
+    def body(which, src, *refs):
+        dsts, (hold, came, went) = refs[:FLOWS], refs[FLOWS:]
+
         def spot(i):
             return pl.ds(i * CUT, CUT)
 
@@ -90,7 +94,9 @@
             for i in range(CUTS)
         ]
         gives = [
-            pltpu.make_async_copy(hold.at[spot(i)], dst.at[spot(i)], went.at[i])
+            pltpu.make_async_copy(
+                hold.at[spot(i)], dsts[i * CUT // FLOW].at[pl.ds(i * CUT % FLOW, CUT)], went.at[i]
+            )
             for i in range(CUTS)
         ]
         for take in takes:
@@ -104,8 +110,8 @@
     return pl.pallas_call(
         body,
         in_specs=[pl.BlockSpec(memory_space=pltpu.SMEM), pl.BlockSpec(memory_space=pltpu.HBM)],
-        out_specs=pl.BlockSpec(memory_space=pltpu.HBM),
-        out_shape=jax.ShapeDtypeStruct((LB, YM, NB), BF),
+        out_specs=[pl.BlockSpec(memory_space=pltpu.HBM)] * FLOWS,
+        out_shape=[jax.ShapeDtypeStruct((FLOW, YM, NB), BF)] * FLOWS,
         scratch_shapes=[
             pltpu.VMEM((LB, YM, NB), BF),
             pltpu.SemaphoreType.DMA((CUTS,)),
@@ -120,8 +126,9 @@
 def y_parts(slab, swapped, k_mine, k_other, pick, first, tiles, lo, hi):
     rows = slice(lo * JB * TILE, hi * JB * TILE)
 
-    def body(_, here, came, km, ko, *outs):
-        part = dot(km[rows], fold(here[0])) + dot(ko[rows], fold(came[...]))
+    def body(_, here, *refs):
+        came, (km, ko), outs = refs[:FLOWS], refs[FLOWS : FLOWS + 2], refs[FLOWS + 2 :]
+        part = dot(km[rows], fold(here[0])) + dot(ko[rows], gathered([c[...] for c in came]))
         part = part.reshape(hi - lo, JB, TILE, NB)
         for k, out in enumerate(outs):
             out[...] = part[k].astype(BF)
@@ -131,22 +138,23 @@
         (tiles,),
         [
             pl.BlockSpec((1, LB, TILE, NB), lambda t, s: (s[0], 0, first + t, 0)),
-            pl.BlockSpec((LB, TILE, NB), lambda t, s: (0, t, 0)),
+            *[pl.BlockSpec((FLOW, TILE, NB), lambda t, s: (0, t, 0))] * FLOWS,
             whole((RW, CL)),
             whole((RW, CL)),
         ],
         [pl.BlockSpec((JB, TILE, NB), lambda t, s: (0, t, 0))] * (hi - lo),
         [jax.ShapeDtypeStruct((JB, tiles * TILE, NB), BF)] * (hi - lo),
-        (slab, swapped, k_mine, k_other),
+        (slab, *swapped, k_mine, k_other),
         pick,
         flops=4 * tiles * (hi - lo) * JB * TILE * CL * NB,
     )
 
 
-def z_parts(slab, k_mine, pick, first, tiles, lo, hi):
+def z_parts(slab, k_mine, pick, first, tiles, lo, hi, after=()):
     rows = slice(lo * JB * TILE, hi * JB * TILE)
 
-    def body(_, here, km, *outs):
+    def body(_, here, km, *refs):
+        outs = refs[len(after) :]
         part = dot(km[rows], fold(here[0])).reshape(hi - lo, JB, TILE, NB)
         for k, out in enumerate(outs):
             out[0] = part[k].astype(BF)
@@ -157,10 +165,11 @@
         [
             pl.BlockSpec((1, LB, TILE, NB), lambda o, t, s: (s[o], 0, first + t, 0)),
             whole((RW, CL)),
+            *[pl.BlockSpec(memory_space=pl.ANY)] * len(after),
         ],
         [pl.BlockSpec((1, JB, TILE, NB), lambda o, t, s: (o, 0, t, 0))] * (hi - lo),
         [jax.ShapeDtypeStruct((2, JB, tiles * TILE, NB), BF)] * (hi - lo),
-        (slab, k_mine),
+        (slab, k_mine, *after),
         pick,
         flops=4 * tiles * (hi - lo) * JB * TILE * CL * NB,
     )
@@ -176,17 +185,19 @@
 
 def y_send(slots, kt_other, tiles):
     def body(*refs):
-        slot_refs, (ko, send) = refs[: len(slots)], refs[len(slots) :]
+        slot_refs, (ko, *sends) = refs[: len(slots)], refs[len(slots) :]
         stack = gathered([s[...] for s in slot_refs])
-        send[...] = dot(ko[...], stack).reshape(LB, TILE, NB).astype(BF)
+        block = dot(ko[...], stack).reshape(LB, TILE, NB)
+        for i, send in enumerate(sends):
+            send[...] = block[i * FLOW : (i + 1) * FLOW].astype(BF)
 
     return call(
         body,
         (tiles,),
         [pl.BlockSpec((s.shape[0], TILE, NB), lambda t: (0, t, 0)) for s in slots]
         + [whole((CL, RW))],
-        pl.BlockSpec((LB, TILE, NB), lambda t: (0, t, 0)),
-        jax.ShapeDtypeStruct((LB, tiles * TILE, NB), BF),
+        [pl.BlockSpec((FLOW, TILE, NB), lambda t: (0, t, 0))] * FLOWS,
+        [jax.ShapeDtypeStruct((FLOW, tiles * TILE, NB), BF)] * FLOWS,
         (*slots, kt_other),
         flops=2 * tiles * RW * CL * NB,
     )
@@ -232,10 +243,11 @@
 
 
 def put(got, out, pick):
-    def body(which, src, _, dst, sem):
+    def body(which, *refs):
+        srcs, (_, dst, sem) = refs[:FLOWS], refs[FLOWS:]
         copies = [
             pltpu.make_async_copy(
-                src.at[pl.ds(i * CUT, CUT)],
+                srcs[i * CUT // FLOW].at[pl.ds(i * CUT % FLOW, CUT)],
                 dst.at[which[1], pl.ds(i * CUT, CUT), pl.ds(0, YM), :],
                 sem.at[i],
             )
@@ -250,17 +262,17 @@
         body,
         in_specs=[
             pl.BlockSpec(memory_space=pltpu.SMEM),
-            pl.BlockSpec(memory_space=pltpu.VMEM),
+            *[pl.BlockSpec(memory_space=pl.ANY)] * FLOWS,
             pl.BlockSpec(memory_space=pltpu.HBM),
         ],
         out_specs=pl.BlockSpec(memory_space=pltpu.HBM),
         out_shape=jax.ShapeDtypeStruct((2, LB, MB, NB), BF),
         scratch_shapes=[pltpu.SemaphoreType.DMA((CUTS,))],
-        input_output_aliases={2: 0},
+        input_output_aliases={1 + FLOWS: 0},
         name="put",
         cost_estimate=pl.CostEstimate(flops=0, bytes_accessed=4 * LB * YM * NB, transcendentals=0),
         compiler_params=pltpu.CompilerParams(vmem_limit_bytes=24 * 1024 * 1024),
-    )(pick, got, out)
+    )(pick, *got, out)
 
 
 def to_virtual(summed, v_halves):
@@ -400,11 +412,12 @@
     vt_halves = coef_t.reshape(2, HALF, NB)
 
     raised, coef_o = lax.optimization_barrier((lift(slab, pick), coef_occupied.T))
-    swapped = swap(raised)
+    swapped = [swap(r) for r in raised]
     k_mine = spread(coef_o, zi * 2 * LB + yi * LB, zi)
+    head = z_parts(slab, k_mine, pick, YT, ZT, 0, 2)
+    coef_o, _ = lax.optimization_barrier((coef_o, head[0]))
     k_other = spread(coef_o, zi * 2 * LB + (1 - yi) * LB, zi)
-    head = z_parts(slab, k_mine, pick, YT, ZT, 0, 2)
-    tail = z_parts(slab, k_mine, pick, YT, ZT, 2, NZ)
+    tail = z_parts(slab, k_mine, pick, YT, ZT, 2, NZ, (k_other,))
     both = chain_sum(unrolled([*head, *tail]))
     last = add(both[0], swap(both[1]))
     head = y_parts(slab, swapped, k_mine, k_other, pick, 0, YT, 0, 3)
@@ -420,7 +433,7 @@
 
     kt_mine, kt_other = k_mine.T, k_other.T
     slots = tree_gather(wide_y)
-    got = swap(y_send(slots, kt_other, YT))
+    got = [swap(b) for b in y_send(slots, kt_other, YT)]
     out = y_keep(slots, kt_mine, pick, 0, YT)
     both = jnp.stack([wide_z, swap(wide_z)])
     out = z_expand(chain_gather(both), kt_mine, out, pick, YT, ZT)

time: 202 us -> 187 us (0.926)
  waiting for transfers between devices: 69.8 us -> 59.4 us
  starting transfers between devices: 69.7 us -> 61.9 us
    ppermute x29, waiting for transfers between devices: 57.5 us -> 39.2 us  [move(): return lax.ppermute(x, 'z', [(i, (i + step) % NZ) for i in range(NZ)])]
    ppermute x29, starting transfers between devices: 57.3 us -> 47.6 us  [move(): return lax.ppermute(x, 'z', [(i, (i + step) % NZ) for i in range(NZ)])]
    ppermute x4 -> x6, waiting for transfers between devices: 7.47 us -> 15.3 us  [swap(): return lax.ppermute(x, 'ylo', SWAP)]
    ppermute x4 -> x6, starting transfers between devices: 4.83 us -> 6.68 us  [swap(): return lax.ppermute(x, 'ylo', SWAP)]
  transfers between devices with their start and end apart: 34 -> 36, of which waited for: 20 -> 18; matrix products, arithmetic and copies ran while one was open for 4% -> 9% of each run, Pallas kernels for 10% -> 13%
where the time goes in v4:
time: 187 us; the launch traced here: 186 us
  starting transfers between devices  61.9 us (33%)
  waiting for transfers between devices  59.4 us (32%)
  Pallas kernels  32.1 us (17%)
  blocking collectives  14.6 us (8%)
  other arithmetic  9.42 us (5%)
  local copies, waits for them, and re-layouts  4.4 us (2%)
  matrix products  3.65 us (2%)
    ppermute x29, starting transfers between devices, move(): return lax.ppermute(x, 'z', [(i, (i + step) % NZ) for i in range(NZ)])  47.6 us
    ppermute x29, waiting for transfers between devices, move(): return lax.ppermute(x, 'z', [(i, (i + step) % NZ) for i in range(NZ)])  39.2 us
    pallas_call x10, Pallas kernels, call(): pl.pallas_call(body, grid_spec=spec, out_shape=out_shape, input_output_al...  27.9 us
    ppermute x6, waiting for transfers between devices, swap(): return lax.ppermute(x, 'ylo', SWAP)  15.3 us
    all_to_all x1, blocking collectives, run(): lax.all_to_all(back_one.reshape(NROW, MB, HALF), 'row', 0, 0, tiled=True)  14.6 us
    all_to_all x1, starting transfers between devices, run(): second = lax.all_to_all(first, 'row', 0, 0, tiled=True).reshape(NB, HALF)  7.61 us
    ppermute x6, starting transfers between devices, swap(): return lax.ppermute(x, 'ylo', SWAP)  6.68 us
    all_to_all x1, waiting for transfers between devices, run(): second = lax.all_to_all(first, 'row', 0, 0, tiled=True).reshape(NB, HALF)  4.86 us
  transfers between devices with their start and end apart: 36, of which 18 were waited for; matrix products, arithmetic and copies ran while one was open for 9% of the time, Pallas kernels for 13%

profile of v4, /device:TPU:2, one launch (start us, length us, event | category | flops | bytes accessed | tf_op | source)
XLA Modules:
  0.0 186.0 jit_solution(10288971967533592962)
XLA Ops:
  0.1 2.6 %lift.1 = (bf16[20,24,640]{2,1,0:T(8,128)(2,1)}, bf16[20,24,640]{2,1,0:T(8,128)(2,1)}) custom-call(s32[2]{0:T(128)S(1)} %pad_add_fusion.which._, bf16[2,40,40,640]{3,2,1,0:T(8,128)(2,1)} %here.7), custom_call_target="tpu_custom_call" | custom-call | bytes 2457600 | tf_op jit(solution)/shard_map/lift/pallas_call | solution.py:110
  6.7 4.4 %shard_map.64 = (bf16[2,8,16,640]{3,2,1,0:T(8,128)(2,1)}, bf16[2,8,16,640]{3,2,1,0:T(8,128)(2,1)}) custom-call(s32[2]{0:T(128)S(1)} %pad_add_fusion.which._, bf16[2,40,40,640]{3,2,1,0:T(8,128)(2,1)} %here.7, bf16[512,320]{1,0:T(8,128)(2,1)S(1)} %select_convert_fusion.1.km.refs_2_), custom_call_target="tpu_custom_call" | custom-call | flops 209715200 | bytes 2211840 | tf_op jit(solution)/shard_map/pallas_call | solution.py:44
  11.2 5.9 %collective-permute-start.12 = (bf16[2,8,16,640]{3,2,1,0:T(8,128)(2,1)}, bf16[2,8,16,640]{3,2,1,0:T(8,128)(2,1)}, u32[]{:S(2)}, u32[]{:S(2)}) collective-permute-start(bf16[2,8,16,640]{3,2,1,0:T(8,128)(2,1)} %get-tuple-element.49), channel_id=1, source_target_pairs={{0,14},{2,0},{4,2},{6,4},{8,6},{10,8},{12,10},{14,12},{1,15},{3,1}... | collective-permute-start | bytes 983048 | tf_op jit(solution)/shard_map/ppermute | solution.py:341
  18.6 2.8 %fusion.8 = (bf16[320,512]{1,0:T(8,128)(2,1)}, bf16[320,512]{1,0:T(8,128)(2,1)}, bf16[512,320]{0,1:T(8,128)(2,1)}) fusion(bf16[512,320]{0,1:T(8,128)(2,1)} %copy-done.4, s32[320]{0:T(512)S(1)} %get-tuple-element.68, s32[320]{0:T(512)S(1)} %get-tuple-element.69, s32[512]{0:T(512)S(1)} %get-tuple-element.70, s32[512]{0:T(512)S(1)} %get-tuple-element.71, ...), kind=kOutput, calls=%fused_computation.13 | convolution fusion | flops 49819648 | bytes 1407624 | tf_op jit(solution)/shard_map/dot_general | solution.py:32
  26.0 4.1 %shard_map.67 = (bf16[2,8,16,640]{3,2,1,0:T(8,128)(2,1)S(1)}, bf16[2,8,16,640]{3,2,1,0:T(8,128)(2,1)S(1)}, bf16[2,8,16,640]{3,2,1,0:T(8,128)(2,1)S(1)}, bf16[2,8...) custom-call(s32[2]{0:T(128)S(1)} %pad_add_fusion.which._, ...), custom_call_target="tpu_custom_call" | custom-call | flops 629145600 | bytes 2375680 | tf_op jit(solution)/shard_map/pallas_call | solution.py:44
  32.4 3.3 %collective-permute-start.13 = (bf16[2,8,16,640]{3,2,1,0:T(8,128)(2,1)S(1)}, bf16[2,8,16,640]{3,2,1,0:T(8,128)(2,1)S(1)}, u32[]{:S(2)}, u32[]{:S(2)}) collective-permute-start(bf16[2,8,16,640]{3,2,1,0:T(8,128)(2,1)S(1)} %add_convert_fusion.3), channel_id=1, source_target_pairs={{0,14},{2,0},{4,2},{6,4},{8,6},{10,8},{12,10},{14,12},{1,15},{3,1}... | collective-permute-start | bytes 983048 | tf_op jit(solution)/shard_map/ppermute | solution.py:341
  35.7 3.6 %shard_map.66 = (bf16[8,24,640]{2,1,0:T(8,128)(2,1)S(1)}, bf16[8,24,640]{2,1,0:T(8,128)(2,1)S(1)}, bf16[8,24,640]{2,1,0:T(8,128)(2,1)S(1)}) custom-call(s32[2]{0:T(128)S(1)} %pad_add_fusion.which._, bf16[2,40,40,640]{3,2,1,0:T(8,128)(2,1)} %here.7, bf16[20,24,640]{2,1,0:T(8,128)(2,1)S(1)} %collective-permute-done.refs_0_, ...), custom_call_target="tpu_custom_call" | custom-call | flops 471859200 | bytes 2990080 | tf_op jit(solution)/shard_map/pallas_call | solution.py:44
  40.7 1.9 %collective-permute-start.6 = (bf16[8,24,640]{2,1,0:T(8,128)(2,1)S(1)}, bf16[8,24,640]{2,1,0:T(8,128)(2,1)S(1)}, u32[]{:S(2)}, u32[]{:S(2)}) collective-permute-start(bf16[8,24,640]{2,1,0:T(8,128)(2,1)S(1)} %get-tuple-element.43), channel_id=1, source_target_pairs={{0,14},{2,0},{4,2},{6,4},{8,6},{10,8},{12,10},{14,12},{1,15},{3,1}... | collective-permute-start | bytes 737288 | tf_op jit(solution)/shard_map/ppermute | solution.py:341
  42.6 3.9 %shard_map.65 = (bf16[8,24,640]{2,1,0:T(8,128)(2,1)S(1)}, bf16[8,24,640]{2,1,0:T(8,128)(2,1)S(1)}, bf16[8,24,640]{2,1,0:T(8,128)(2,1)S(1)}, bf16[8,24,640]{2,1,0:T(8,128)(2,1)S(1)}, bf16[8,24,640]{2,1,0:T(8,128)(2,1)S(1)}) custom-call(s32[2]{0:T(128)S(1)} %pad_add_fusion.which._, bf16[2,40,40,640]{3,2,1,0:T(8,128)(2,1)} %here.7, ...), custom_call_target="tpu_custom_call" | custom-call | flops 786432000 | bytes 2990080 | tf_op jit(solution)/shard_map/pallas_call | solution.py:44
  48.2 2.1 %collective-permute-start.14 = (bf16[2,8,16,640]{3,2,1,0:T(8,128)(2,1)S(1)}, bf16[2,8,16,640]{3,2,1,0:T(8,128)(2,1)S(1)}, u32[]{:S(2)}, u32[]{:S(2)}) collective-permute-start(bf16[2,8,16,640]{3,2,1,0:T(8,128)(2,1)S(1)} %add_convert_fusion.2), channel_id=1, source_target_pairs={{0,14},{2,0},{4,2},{6,4},{8,6},{10,8},{12,10},{14,12},{1,15},{3,1}... | collective-permute-start | bytes 983048 | tf_op jit(solution)/shard_map/ppermute | solution.py:341
  52.0 7.8 %collective-permute-done.3 = bf16[8,24,640]{2,1,0:T(8,128)(2,1)S(1)} collective-permute-done((bf16[8,24,640]{2,1,0:T(8,128)(2,1)S(1)}, bf16[8,24,640]{2,1,0:T(8,128)(2,1)S(1)}, u32[]{:S(2)}, u32[]{:S(2)}) %collective-permute-start.3) | collective-permute-done | bytes 245792 | tf_op jit(solution)/shard_map/ppermute | solution.py:341
  63.6 6.1 %collective-permute-done.4 = bf16[8,24,640]{2,1,0:T(8,128)(2,1)S(1)} collective-permute-done((bf16[8,24,640]{2,1,0:T(8,128)(2,1)S(1)}, bf16[8,24,640]{2,1,0:T(8,128)(2,1)S(1)}, u32[]{:S(2)}, u32[]{:S(2)}) %collective-permute-start.4) | collective-permute-done | bytes 245792 | tf_op jit(solution)/shard_map/ppermute | solution.py:341
  69.9 3.3 %collective-permute-start.8 = (bf16[8,24,640]{2,1,0:T(8,128)(2,1)S(1)}, bf16[8,24,640]{2,1,0:T(8,128)(2,1)S(1)}, u32[]{:S(2)}, u32[]{:S(2)}) collective-permute-start(bf16[8,24,640]{2,1,0:T(8,128)(2,1)S(1)} %add_convert_fusion.7), channel_id=1, source_target_pairs={{0,14},{2,0},{4,2},{6,4},{8,6},{10,8},{12,10},{14,12},{1,15},{3,1}... | collective-permute-start | bytes 737288 | tf_op jit(solution)/shard_map/ppermute | solution.py:341
  75.1 2.2 %collective-permute-done.5 = bf16[8,24,640]{2,1,0:T(8,128)(2,1)S(1)} collective-permute-done((bf16[8,24,640]{2,1,0:T(8,128)(2,1)S(1)}, bf16[8,24,640]{2,1,0:T(8,128)(2,1)S(1)}, u32[]{:S(2)}, u32[]{:S(2)}) %collective-permute-start.5) | collective-permute-done | bytes 245792 | tf_op jit(solution)/shard_map/ppermute | solution.py:341
  80.4 7.6 %all-to-all-start = ((bf16[16,40,288]{2,1,0:T(8,128)(2,1)}), bf16[16,40,288]{2,1,0:T(8,128)(2,1)S(1)}, u32[]{:S(2)}, u32[]{:S(2)}) async-start(bf16[16,40,288]{2,1,0:T(8,128)(2,1)} %shard_map.68), calls=%async_computation | async-start | bytes 983040 | tf_op jit(solution)/shard_map/all_to_all | solution.py:429
  91.6 4.9 %all-to-all-done = bf16[16,40,288]{2,1,0:T(8,128)(2,1)S(1)} async-done(((bf16[16,40,288]{2,1,0:T(8,128)(2,1)}), bf16[16,40,288]{2,1,0:T(8,128)(2,1)S(1)}, u32[]{:S(2)}, u32[]{:S(2)}) %all-to-all-start) | async-done | bytes 368672 | tf_op jit(solution)/shard_map/all_to_all | solution.py:429
  97.7 14.6 %all_to_all.10.x = bf16[16,40,288]{2,1,0:T(8,128)(2,1)S(1)} all-to-all(bf16[16,40,288]{2,1,0:T(8,128)(2,1)S(1)} %bitcast.36), channel_id=1, replica_groups=mesh['row'=16,'z'=8,'ylo'=2] {'row'}, dimensions={0} | all-to-all | bytes 737280 | tf_op jit(solution)/shard_map/all_to_all | solution.py:431
  113.7 3.2 %collective-permute-start.17 = (bf16[8,24,640]{2,1,0:T(8,128)(2,1)S(1)}, bf16[8,24,640]{2,1,0:T(8,128)(2,1)S(1)}, u32[]{:S(2)}, u32[]{:S(2)}) collective-permute-start(bf16[8,24,640]{2,1,0:T(8,128)(2,1)S(1)} %get-tuple-element.53.refs_6_), channel_id=1, source_target_pairs={{0,14},{2,0},{4,2},{6,4},{8,6},{10,8},{12,10},{14,12},{1,15},{3,1}... | collective-permute-start | bytes 737288 | tf_op jit(solution)/shard_map/ppermute | solution.py:341
  116.9 3.1 %collective-permute-done.27 = bf16[8,16,640]{2,1,0:T(8,128)(2,1)S(1)} collective-permute-done((bf16[8,16,640]{2,1,0:T(8,128)(2,1)S(1)}, bf16[8,16,640]{2,1,0:T(8,128)(2,1)S(1)}, u32[]{:S(2)}, u32[]{:S(2)}) %collective-permute-start.27) | collective-permute-done | bytes 163872 | tf_op jit(solution)/shard_map/ppermute | solution.py:345
  120.0 2.0 %collective-permute-start.28 = (bf16[2,8,16,640]{3,2,1,0:T(8,128)(2,1)S(1)}, bf16[2,8,16,640]{3,2,1,0:T(8,128)(2,1)S(1)}, u32[]{:S(2)}, u32[]{:S(2)}) collective-permute-start(bf16[2,8,16,640]{3,2,1,0:T(8,128)(2,1)S(1)} %pad_maximum_fusion.2.refs_5_), channel_id=1, source_target_pairs={{0,14},{2,0},{4,2},{6,4},{8,6},{10,8},{12,10},{14,12},{1,15},{3,1}... | collective-permute-start | bytes 983048 | tf_op jit(solution)/shard_map/ppermute | solution.py:341
  123.5 3.3 %collective-permute-start.18 = (bf16[8,24,640]{2,1,0:T(8,128)(2,1)S(1)}, bf16[8,24,640]{2,1,0:T(8,128)(2,1)S(1)}, u32[]{:S(2)}, u32[]{:S(2)}) collective-permute-start(bf16[8,24,640]{2,1,0:T(8,128)(2,1)S(1)} %collective-permute-done.17.refs_7_), channel_id=1, source_target_pairs={{0,14},{2,0},{4,2},{6,4},{8,6},{10,8},{12,10},{14,12},{1,15},{3,1}... | collective-permute-start | bytes 737288 | tf_op jit(solution)/shard_map/ppermute | solution.py:341
  126.8 3.9 %collective-permute-done.28.refs_6_ = bf16[2,8,16,640]{3,2,1,0:T(8,128)(2,1)S(1)} collective-permute-done((bf16[2,8,16,640]{3,2,1,0:T(8,128)(2,1)S(1)}, bf16[2,8,16,640]{3,2,1,0:T(8,128)(2,1)S(1)}, u32[]{:S(2)}, u32[]{:S(2)}) %collective-permute-start.28) | collective-permute-done | bytes 327712 | tf_op jit(solution)/shard_map/ppermute | solution.py:341
  130.7 3.2 %collective-permute-start.29 = (bf16[2,8,16,640]{3,2,1,0:T(8,128)(2,1)S(1)}, bf16[2,8,16,640]{3,2,1,0:T(8,128)(2,1)S(1)}, u32[]{:S(2)}, u32[]{:S(2)}) collective-permute-start(bf16[2,8,16,640]{3,2,1,0:T(8,128)(2,1)S(1)} %collective-permute-done.28.refs_6_), channel_id=1, source_target_pairs={{0,14},{2,0},{4,2},{6,4},{8,6},{10,8},{12,10},{14,12},{1,15},{3,1}... | collective-permute-start | bytes 983048 | tf_op jit(solution)/shard_map/ppermute | solution.py:341
  133.9 2.1 %collective-permute-done.18.refs_8_ = bf16[8,24,640]{2,1,0:T(8,128)(2,1)S(1)} collective-permute-done((bf16[8,24,640]{2,1,0:T(8,128)(2,1)S(1)}, bf16[8,24,640]{2,1,0:T(8,128)(2,1)S(1)}, u32[]{:S(2)}, u32[]{:S(2)}) %collective-permute-start.18) | collective-permute-done | bytes 245792 | tf_op jit(solution)/shard_map/ppermute | solution.py:341
  136.0 3.2 %collective-permute-start.19 = (bf16[8,24,640]{2,1,0:T(8,128)(2,1)S(1)}, bf16[8,24,640]{2,1,0:T(8,128)(2,1)S(1)}, u32[]{:S(2)}, u32[]{:S(2)}) collective-permute-start(bf16[8,24,640]{2,1,0:T(8,128)(2,1)S(1)} %collective-permute-done.18.refs_8_), channel_id=1, source_target_pairs={{0,14},{2,0},{4,2},{6,4},{8,6},{10,8},{12,10},{14,12},{1,15},{3,1}... | collective-permute-start | bytes 737288 | tf_op jit(solution)/shard_map/ppermute | solution.py:341
  140.5 3.0 %collective-permute-start.23 = (bf16[4,24,640]{2,1,0:T(8,128)(2,1)S(1)}, bf16[4,24,640]{2,1,0:T(8,128)(2,1)S(1)}, u32[]{:S(2)}, u32[]{:S(2)}) collective-permute-start(bf16[4,24,640]{2,1,0:T(8,128)(2,1)S(1)} %slice.37), channel_id=1, source_target_pairs={{0,12},{2,14},{4,0},{6,2},{8,4},{10,6},{12,8},{14,10},{1,13},{3,15... | collective-permute-start | bytes 368648 | tf_op jit(solution)/shard_map/ppermute | solution.py:341
  143.5 5.4 %collective-permute-done.22.refs_1_ = bf16[4,24,640]{2,1,0:T(8,128)(2,1)S(1)} collective-permute-done((bf16[4,24,640]{2,1,0:T(8,128)(2,1)S(1)}, bf16[4,24,640]{2,1,0:T(8,128)(2,1)S(1)}, u32[]{:S(2)}, u32[]{:S(2)}) %collective-permute-start.22) | collective-permute-done | bytes 122912 | tf_op jit(solution)/shard_map/ppermute | solution.py:341
  148.9 2.5 %collective-permute-start.33 = (bf16[2,8,16,640]{3,2,1,0:T(8,128)(2,1)S(1)}, bf16[2,8,16,640]{3,2,1,0:T(8,128)(2,1)S(1)}, u32[]{:S(2)}, u32[]{:S(2)}) collective-permute-start(bf16[2,8,16,640]{3,2,1,0:T(8,128)(2,1)S(1)} %collective-permute-done.32.refs_4_), channel_id=1, source_target_pairs={{0,2},{2,4},{4,6},{6,8},{8,10},{10,12},{12,14},{14,0},{1,3},{3,5},... | collective-permute-start | bytes 983048 | tf_op jit(solution)/shard_map/ppermute | solution.py:341
  160.2 3.1 %collective-permute-start.31 = (bf16[2,8,16,640]{3,2,1,0:T(8,128)(2,1)S(1)}, bf16[2,8,16,640]{3,2,1,0:T(8,128)(2,1)S(1)}, u32[]{:S(2)}, u32[]{:S(2)}) collective-permute-start(bf16[2,8,16,640]{3,2,1,0:T(8,128)(2,1)S(1)} %collective-permute-done.30.refs_0_), channel_id=1, source_target_pairs={{0,14},{2,0},{4,2},{6,4},{8,6},{10,8},{12,10},{14,12},{1,15},{3,1}... | collective-permute-start | bytes 983048 | tf_op jit(solution)/shard_map/ppermute | solution.py:341
  163.3 3.1 %shard_map.72.refs_9_ = bf16[2,40,40,640]{3,2,1,0:T(8,128)(2,1)} custom-call(s32[2]{0:T(128)S(1)} %pad_add_fusion.which._, bf16[8,24,640]{2,1,0:T(8,128)(2,1)S(1)} %collective-permute-done.19.refs_0_, bf16[4,24,640]{2,1,0:T(8,128)(2,1)S(1)} %collective-permute-done.22.refs_1_, bf16[4,24,640]{2,1,0:T(8,128)(2,1)S(1)} %collective-permute-done.23.refs_2_, ...), custom_call_target="tpu_custom_call" | custom-call | flops 629145600 | bytes 1146880 | tf_op jit(solution)/shard_map/pallas_call | solution.py:44
  169.8 3.7 %shard_map.73.refs_2_ = bf16[2,40,40,640]{3,2,1,0:T(8,128)(2,1)} custom-call(s32[2]{0:T(128)S(1)} %pad_add_fusion.which._, bf16[2,8,16,640]{3,2,1,0:T(8,128)(2,1)S(1)} %collective-permute-done.30.refs_0_, bf16[2,8,16,640]{3,2,1,0:T(8,128)(2,1)S(1)} %collective-permute-done.31.refs_1_, ...), custom_call_target="tpu_custom_call", output_to_operand_aliasing={{}: (10, {})} | custom-call | flops 838860800 | bytes 3522560 | tf_op jit(solution)/shard_map/pallas_call | solution.py:44
  173.5 10.7 %collective-permute-done.26.refs_1_ = bf16[20,24,640]{2,1,0:T(8,128)(2,1)S(1)} collective-permute-done((bf16[20,24,640]{2,1,0:T(8,128)(2,1)S(1)}, bf16[20,24,640]{2,1,0:T(8,128)(2,1)S(1)}, u32[]{:S(2)}, u32[]{:S(2)}) %collective-permute-start.26) | collective-permute-done | bytes 614432 | tf_op jit(solution)/shard_map/ppermute | solution.py:345
  (110 shorter events, 48.8 us)
Async XLA Ops:
  2.7 33.0 %collective-permute-start = (bf16[20,24,640]{2,1,0:T(8,128)(2,1)}, bf16[20,24,640]{2,1,0:T(8,128)(2,1)S(1)}, u32[]{:S(2)}, u32[]{:S(2)}) collective-permute-start(bf16[20,24,640]{2,1,0:T(8,128)(2,1)} %get-tuple-element.33), channel_id=1, source_target_pairs={{0,1},{1,0},{2,3},{3,2},{4,5},{5,4},{6,7},{7,6},{8,9},{9,8},{10,11... | collective-permute-start | bytes 1843208 | tf_op jit(solution)/shard_map/ppermute | solution.py:345
  4.4 31.4 %collective-permute-start.1 = (bf16[20,24,640]{2,1,0:T(8,128)(2,1)}, bf16[20,24,640]{2,1,0:T(8,128)(2,1)S(1)}, u32[]{:S(2)}, u32[]{:S(2)}) collective-permute-start(bf16[20,24,640]{2,1,0:T(8,128)(2,1)} %get-tuple-element.34), channel_id=1, source_target_pairs={{0,1},{1,0},{2,3},{3,2},{4,5},{5,4},{6,7},{7,6},{8,9},{9,8},{10,11... | collective-permute-start | bytes 1843208 | tf_op jit(solution)/shard_map/ppermute | solution.py:345
  11.2 20.1 %collective-permute-start.12 = (bf16[2,8,16,640]{3,2,1,0:T(8,128)(2,1)}, bf16[2,8,16,640]{3,2,1,0:T(8,128)(2,1)}, u32[]{:S(2)}, u32[]{:S(2)}) collective-permute-start(bf16[2,8,16,640]{3,2,1,0:T(8,128)(2,1)} %get-tuple-element.49), channel_id=1, source_target_pairs={{0,14},{2,0},{4,2},{6,4},{8,6},{10,8},{12,10},{14,12},{1,15},{3,1}... | collective-permute-start | bytes 983048 | tf_op jit(solution)/shard_map/ppermute | solution.py:341
  17.0 13.1 %collective-permute-start.9 = (bf16[2,8,16,640]{3,2,1,0:T(8,128)(2,1)}, bf16[2,8,16,640]{3,2,1,0:T(8,128)(2,1)}, u32[]{:S(2)}, u32[]{:S(2)}) collective-permute-start(bf16[2,8,16,640]{3,2,1,0:T(8,128)(2,1)} %get-tuple-element.36), channel_id=1, source_target_pairs={{0,2},{2,4},{4,6},{6,8},{8,10},{10,12},{12,14},{14,0},{1,3},{3,5},... | collective-permute-start | bytes 983048 | tf_op jit(solution)/shard_map/ppermute | solution.py:341
  31.2 15.3 %collective-permute-start.10 = (bf16[2,8,16,640]{3,2,1,0:T(8,128)(2,1)S(1)}, bf16[2,8,16,640]{3,2,1,0:T(8,128)(2,1)S(1)}, u32[]{:S(2)}, u32[]{:S(2)}) collective-permute-start(bf16[2,8,16,640]{3,2,1,0:T(8,128)(2,1)S(1)} %add_convert_fusion.5), channel_id=1, source_target_pairs={{0,2},{2,4},{4,6},{6,8},{8,10},{10,12},{12,14},{14,0},{1,3},{3,5},... | collective-permute-start | bytes 983048 | tf_op jit(solution)/shard_map/ppermute | solution.py:341
  32.4 15.7 %collective-permute-start.13 = (bf16[2,8,16,640]{3,2,1,0:T(8,128)(2,1)S(1)}, bf16[2,8,16,640]{3,2,1,0:T(8,128)(2,1)S(1)}, u32[]{:S(2)}, u32[]{:S(2)}) collective-permute-start(bf16[2,8,16,640]{3,2,1,0:T(8,128)(2,1)S(1)} %add_convert_fusion.3), channel_id=1, source_target_pairs={{0,14},{2,0},{4,2},{6,4},{8,6},{10,8},{12,10},{14,12},{1,15},{3,1}... | collective-permute-start | bytes 983048 | tf_op jit(solution)/shard_map/ppermute | solution.py:341
  39.3 12.7 %collective-permute-start.2 = (bf16[8,24,640]{2,1,0:T(8,128)(2,1)S(1)}, bf16[8,24,640]{2,1,0:T(8,128)(2,1)S(1)}, u32[]{:S(2)}, u32[]{:S(2)}) collective-permute-start(bf16[8,24,640]{2,1,0:T(8,128)(2,1)S(1)} %get-tuple-element.39), channel_id=1, source_target_pairs={{0,2},{2,4},{4,6},{6,8},{8,10},{10,12},{12,14},{14,0},{1,3},{3,5},... | collective-permute-start | bytes 737288 | tf_op jit(solution)/shard_map/ppermute | solution.py:341
  39.4 20.5 %collective-permute-start.3 = (bf16[8,24,640]{2,1,0:T(8,128)(2,1)S(1)}, bf16[8,24,640]{2,1,0:T(8,128)(2,1)S(1)}, u32[]{:S(2)}, u32[]{:S(2)}) collective-permute-start(bf16[8,24,640]{2,1,0:T(8,128)(2,1)S(1)} %get-tuple-element.41), channel_id=1, source_target_pairs={{0,4},{2,6},{4,8},{6,10},{8,12},{10,14},{12,0},{14,2},{1,5},{3,7},... | collective-permute-start | bytes 737288 | tf_op jit(solution)/shard_map/ppermute | solution.py:341
  40.7 20.9 %collective-permute-start.6 = (bf16[8,24,640]{2,1,0:T(8,128)(2,1)S(1)}, bf16[8,24,640]{2,1,0:T(8,128)(2,1)S(1)}, u32[]{:S(2)}, u32[]{:S(2)}) collective-permute-start(bf16[8,24,640]{2,1,0:T(8,128)(2,1)S(1)} %get-tuple-element.43), channel_id=1, source_target_pairs={{0,14},{2,0},{4,2},{6,4},{8,6},{10,8},{12,10},{14,12},{1,15},{3,1}... | collective-permute-start | bytes 737288 | tf_op jit(solution)/shard_map/ppermute | solution.py:341
  46.7 26.6 %collective-permute-start.11 = (bf16[2,8,16,640]{3,2,1,0:T(8,128)(2,1)S(1)}, bf16[2,8,16,640]{3,2,1,0:T(8,128)(2,1)S(1)}, u32[]{:S(2)}, u32[]{:S(2)}) collective-permute-start(bf16[2,8,16,640]{3,2,1,0:T(8,128)(2,1)S(1)} %add_convert_fusion.4), channel_id=1, source_target_pairs={{0,2},{2,4},{4,6},{6,8},{8,10},{10,12},{12,14},{14,0},{1,3},{3,5},... | collective-permute-start | bytes 983048 | tf_op jit(solution)/shard_map/ppermute | solution.py:341
  48.2 15.2 %collective-permute-start.14 = (bf16[2,8,16,640]{3,2,1,0:T(8,128)(2,1)S(1)}, bf16[2,8,16,640]{3,2,1,0:T(8,128)(2,1)S(1)}, u32[]{:S(2)}, u32[]{:S(2)}) collective-permute-start(bf16[2,8,16,640]{3,2,1,0:T(8,128)(2,1)S(1)} %add_convert_fusion.2), channel_id=1, source_target_pairs={{0,14},{2,0},{4,2},{6,4},{8,6},{10,8},{12,10},{14,12},{1,15},{3,1}... | collective-permute-start | bytes 983048 | tf_op jit(solution)/shard_map/ppermute | solution.py:341
  59.9 9.7 %collective-permute-start.4 = (bf16[8,24,640]{2,1,0:T(8,128)(2,1)S(1)}, bf16[8,24,640]{2,1,0:T(8,128)(2,1)S(1)}, u32[]{:S(2)}, u32[]{:S(2)}) collective-permute-start(bf16[8,24,640]{2,1,0:T(8,128)(2,1)S(1)} %add_convert_fusion.10), channel_id=1, source_target_pairs={{0,2},{2,4},{4,6},{6,8},{8,10},{10,12},{12,14},{14,0},{1,3},{3,5},... | collective-permute-start | bytes 737288 | tf_op jit(solution)/shard_map/ppermute | solution.py:341
  61.6 8.2 %collective-permute-start.7 = (bf16[8,24,640]{2,1,0:T(8,128)(2,1)S(1)}, bf16[8,24,640]{2,1,0:T(8,128)(2,1)S(1)}, u32[]{:S(2)}, u32[]{:S(2)}) collective-permute-start(bf16[8,24,640]{2,1,0:T(8,128)(2,1)S(1)} %add_convert_fusion.8), channel_id=1, source_target_pairs={{0,14},{2,0},{4,2},{6,4},{8,6},{10,8},{12,10},{14,12},{1,15},{3,1}... | collective-permute-start | bytes 737288 | tf_op jit(solution)/shard_map/ppermute | solution.py:341
  63.5 9.7 %collective-permute-start.15 = (bf16[2,8,16,640]{3,2,1,0:T(8,128)(2,1)S(1)}, bf16[2,8,16,640]{3,2,1,0:T(8,128)(2,1)S(1)}, u32[]{:S(2)}, u32[]{:S(2)}) collective-permute-start(bf16[2,8,16,640]{3,2,1,0:T(8,128)(2,1)S(1)} %add_convert_fusion.1), channel_id=1, source_target_pairs={{0,14},{2,0},{4,2},{6,4},{8,6},{10,8},{12,10},{14,12},{1,15},{3,1}... | collective-permute-start | bytes 983048 | tf_op jit(solution)/shard_map/ppermute | solution.py:341
  80.4 16.0 %all-to-all-start = ((bf16[16,40,288]{2,1,0:T(8,128)(2,1)}), bf16[16,40,288]{2,1,0:T(8,128)(2,1)S(1)}, u32[]{:S(2)}, u32[]{:S(2)}) async-start(bf16[16,40,288]{2,1,0:T(8,128)(2,1)} %shard_map.68), calls=%async_computation | async-start | bytes 983040 | tf_op jit(solution)/shard_map/all_to_all | solution.py:429
  113.6 9.8 %collective-permute-start.20 = (bf16[8,24,640]{2,1,0:T(8,128)(2,1)S(1)}, bf16[8,24,640]{2,1,0:T(8,128)(2,1)S(1)}, u32[]{:S(2)}, u32[]{:S(2)}) collective-permute-start(bf16[8,24,640]{2,1,0:T(8,128)(2,1)S(1)} %get-tuple-element.53.refs_6_), channel_id=1, source_target_pairs={{0,2},{2,4},{4,6},{6,8},{8,10},{10,12},{12,14},{14,0},{1,3},{3,5},... | collective-permute-start | bytes 737288 | tf_op jit(solution)/shard_map/ppermute | solution.py:341
  113.7 9.8 %collective-permute-start.17 = (bf16[8,24,640]{2,1,0:T(8,128)(2,1)S(1)}, bf16[8,24,640]{2,1,0:T(8,128)(2,1)S(1)}, u32[]{:S(2)}, u32[]{:S(2)}) collective-permute-start(bf16[8,24,640]{2,1,0:T(8,128)(2,1)S(1)} %get-tuple-element.53.refs_6_), channel_id=1, source_target_pairs={{0,14},{2,0},{4,2},{6,4},{8,6},{10,8},{12,10},{14,12},{1,15},{3,1}... | collective-permute-start | bytes 737288 | tf_op jit(solution)/shard_map/ppermute | solution.py:341
  120.0 10.7 %collective-permute-start.28 = (bf16[2,8,16,640]{3,2,1,0:T(8,128)(2,1)S(1)}, bf16[2,8,16,640]{3,2,1,0:T(8,128)(2,1)S(1)}, u32[]{:S(2)}, u32[]{:S(2)}) collective-permute-start(bf16[2,8,16,640]{3,2,1,0:T(8,128)(2,1)S(1)} %pad_maximum_fusion.2.refs_5_), channel_id=1, source_target_pairs={{0,14},{2,0},{4,2},{6,4},{8,6},{10,8},{12,10},{14,12},{1,15},{3,1}... | collective-permute-start | bytes 983048 | tf_op jit(solution)/shard_map/ppermute | solution.py:341
  123.5 10.4 %collective-permute-start.21 = (bf16[8,24,640]{2,1,0:T(8,128)(2,1)S(1)}, bf16[8,24,640]{2,1,0:T(8,128)(2,1)S(1)}, u32[]{:S(2)}, u32[]{:S(2)}) collective-permute-start(bf16[8,24,640]{2,1,0:T(8,128)(2,1)S(1)} %collective-permute-done.20.refs_5_), channel_id=1, source_target_pairs={{0,2},{2,4},{4,6},{6,8},{8,10},{10,12},{12,14},{14,0},{1,3},{3,5},... | collective-permute-start | bytes 737288 | tf_op jit(solution)/shard_map/ppermute | solution.py:341
  123.5 12.5 %collective-permute-start.18 = (bf16[8,24,640]{2,1,0:T(8,128)(2,1)S(1)}, bf16[8,24,640]{2,1,0:T(8,128)(2,1)S(1)}, u32[]{:S(2)}, u32[]{:S(2)}) collective-permute-start(bf16[8,24,640]{2,1,0:T(8,128)(2,1)S(1)} %collective-permute-done.17.refs_7_), channel_id=1, source_target_pairs={{0,14},{2,0},{4,2},{6,4},{8,6},{10,8},{12,10},{14,12},{1,15},{3,1}... | collective-permute-start | bytes 737288 | tf_op jit(solution)/shard_map/ppermute | solution.py:341
  126.8 13.7 %collective-permute-start.32 = (bf16[2,8,16,640]{3,2,1,0:T(8,128)(2,1)S(1)}, bf16[2,8,16,640]{3,2,1,0:T(8,128)(2,1)S(1)}, u32[]{:S(2)}, u32[]{:S(2)}) collective-permute-start(bf16[2,8,16,640]{3,2,1,0:T(8,128)(2,1)S(1)} %pad_maximum_fusion.2.refs_5_), channel_id=1, source_target_pairs={{0,2},{2,4},{4,6},{6,8},{8,10},{10,12},{12,14},{14,0},{1,3},{3,5},... | collective-permute-start | bytes 983048 | tf_op jit(solution)/shard_map/ppermute | solution.py:341
  130.7 20.7 %collective-permute-start.29 = (bf16[2,8,16,640]{3,2,1,0:T(8,128)(2,1)S(1)}, bf16[2,8,16,640]{3,2,1,0:T(8,128)(2,1)S(1)}, u32[]{:S(2)}, u32[]{:S(2)}) collective-permute-start(bf16[2,8,16,640]{3,2,1,0:T(8,128)(2,1)S(1)} %collective-permute-done.28.refs_6_), channel_id=1, source_target_pairs={{0,14},{2,0},{4,2},{6,4},{8,6},{10,8},{12,10},{14,12},{1,15},{3,1}... | collective-permute-start | bytes 983048 | tf_op jit(solution)/shard_map/ppermute | solution.py:341
  133.9 20.0 %collective-permute-start.24 = (bf16[8,24,640]{2,1,0:T(8,128)(2,1)S(1)}, bf16[8,24,640]{2,1,0:T(8,128)(2,1)S(1)}, u32[]{:S(2)}, u32[]{:S(2)}) collective-permute-start(bf16[8,24,640]{2,1,0:T(8,128)(2,1)S(1)} %collective-permute-done.21.refs_4_), channel_id=1, source_target_pairs={{0,2},{2,4},{4,6},{6,8},{8,10},{10,12},{12,14},{14,0},{1,3},{3,5},... | collective-permute-start | bytes 737288 | tf_op jit(solution)/shard_map/ppermute | solution.py:341
  136.0 18.0 %collective-permute-start.19 = (bf16[8,24,640]{2,1,0:T(8,128)(2,1)S(1)}, bf16[8,24,640]{2,1,0:T(8,128)(2,1)S(1)}, u32[]{:S(2)}, u32[]{:S(2)}) collective-permute-start(bf16[8,24,640]{2,1,0:T(8,128)(2,1)S(1)} %collective-permute-done.18.refs_8_), channel_id=1, source_target_pairs={{0,14},{2,0},{4,2},{6,4},{8,6},{10,8},{12,10},{14,12},{1,15},{3,1}... | collective-permute-start | bytes 737288 | tf_op jit(solution)/shard_map/ppermute | solution.py:341
  139.2 9.8 %collective-permute-start.22 = (bf16[4,24,640]{2,1,0:T(8,128)(2,1)S(1)}, bf16[4,24,640]{2,1,0:T(8,128)(2,1)S(1)}, u32[]{:S(2)}, u32[]{:S(2)}) collective-permute-start(bf16[4,24,640]{2,1,0:T(8,128)(2,1)S(1)} %slice.36), channel_id=1, source_target_pairs={{0,4},{2,6},{4,8},{6,10},{8,12},{10,14},{12,0},{14,2},{1,5},{3,7},... | collective-permute-start | bytes 368648 | tf_op jit(solution)/shard_map/ppermute | solution.py:341
  140.5 13.4 %collective-permute-start.23 = (bf16[4,24,640]{2,1,0:T(8,128)(2,1)S(1)}, bf16[4,24,640]{2,1,0:T(8,128)(2,1)S(1)}, u32[]{:S(2)}, u32[]{:S(2)}) collective-permute-start(bf16[4,24,640]{2,1,0:T(8,128)(2,1)S(1)} %slice.37), channel_id=1, source_target_pairs={{0,12},{2,14},{4,0},{6,2},{8,4},{10,6},{12,8},{14,10},{1,13},{3,15... | collective-permute-start | bytes 368648 | tf_op jit(solution)/shard_map/ppermute | solution.py:341
  148.9 10.0 %collective-permute-start.33 = (bf16[2,8,16,640]{3,2,1,0:T(8,128)(2,1)S(1)}, bf16[2,8,16,640]{3,2,1,0:T(8,128)(2,1)S(1)}, u32[]{:S(2)}, u32[]{:S(2)}) collective-permute-start(bf16[2,8,16,640]{3,2,1,0:T(8,128)(2,1)S(1)} %collective-permute-done.32.refs_4_), channel_id=1, source_target_pairs={{0,2},{2,4},{4,6},{6,8},{8,10},{10,12},{12,14},{14,0},{1,3},{3,5},... | collective-permute-start | bytes 983048 | tf_op jit(solution)/shard_map/ppermute | solution.py:341
  151.4 8.7 %collective-permute-start.30 = (bf16[2,8,16,640]{3,2,1,0:T(8,128)(2,1)S(1)}, bf16[2,8,16,640]{3,2,1,0:T(8,128)(2,1)S(1)}, u32[]{:S(2)}, u32[]{:S(2)}) collective-permute-start(bf16[2,8,16,640]{3,2,1,0:T(8,128)(2,1)S(1)} %collective-permute-done.29.refs_7_), channel_id=1, source_target_pairs={{0,14},{2,0},{4,2},{6,4},{8,6},{10,8},{12,10},{14,12},{1,15},{3,1}... | collective-permute-start | bytes 983048 | tf_op jit(solution)/shard_map/ppermute | solution.py:341
  155.6 17.9 %collective-permute-start.25 = (bf16[20,24,640]{2,1,0:T(8,128)(2,1)S(1)}, bf16[20,24,640]{2,1,0:T(8,128)(2,1)S(1)}, u32[]{:S(2)}, u32[]{:S(2)}) collective-permute-start(bf16[20,24,640]{2,1,0:T(8,128)(2,1)S(1)} %get-tuple-element.54), channel_id=1, source_target_pairs={{0,1},{1,0},{2,3},{3,2},{4,5},{5,4},{6,7},{7,6},{8,9},{9,8},{10,11... | collective-permute-start | bytes 1843208 | tf_op jit(solution)/shard_map/ppermute | solution.py:345
  157.1 27.2 %collective-permute-start.26 = (bf16[20,24,640]{2,1,0:T(8,128)(2,1)S(1)}, bf16[20,24,640]{2,1,0:T(8,128)(2,1)S(1)}, u32[]{:S(2)}, u32[]{:S(2)}) collective-permute-start(bf16[20,24,640]{2,1,0:T(8,128)(2,1)S(1)} %get-tuple-element.55), channel_id=1, source_target_pairs={{0,1},{1,0},{2,3},{3,2},{4,5},{5,4},{6,7},{7,6},{8,9},{9,8},{10,11... | collective-permute-start | bytes 1843208 | tf_op jit(solution)/shard_map/ppermute | solution.py:345
  159.0 9.2 %collective-permute-start.34 = (bf16[2,8,16,640]{3,2,1,0:T(8,128)(2,1)S(1)}, bf16[2,8,16,640]{3,2,1,0:T(8,128)(2,1)S(1)}, u32[]{:S(2)}, u32[]{:S(2)}) collective-permute-start(bf16[2,8,16,640]{3,2,1,0:T(8,128)(2,1)S(1)} %collective-permute-done.33.refs_3_), channel_id=1, source_target_pairs={{0,2},{2,4},{4,6},{6,8},{8,10},{10,12},{12,14},{14,0},{1,3},{3,5},... | collective-permute-start | bytes 983048 | tf_op jit(solution)/shard_map/ppermute | solution.py:341
  160.2 9.7 %collective-permute-start.31 = (bf16[2,8,16,640]{3,2,1,0:T(8,128)(2,1)S(1)}, bf16[2,8,16,640]{3,2,1,0:T(8,128)(2,1)S(1)}, u32[]{:S(2)}, u32[]{:S(2)}) collective-permute-start(bf16[2,8,16,640]{3,2,1,0:T(8,128)(2,1)S(1)} %collective-permute-done.30.refs_0_), channel_id=1, source_target_pairs={{0,14},{2,0},{4,2},{6,4},{8,6},{10,8},{12,10},{14,12},{1,15},{3,1}... | collective-permute-start | bytes 983048 | tf_op jit(solution)/shard_map/ppermute | solution.py:341
  (12 other events, 226.8 us)

commit v5 on v3

--- a/solution.py
+++ b/solution.py
@@ -25,7 +25,7 @@
 YM, ZM = YT * TILE, ZT * TILE
 LEAD = 3
 FAR = NZ // 2
-JH = JB // 2
+JH = 6
 
 
 def dot(a, b):
@@ -78,14 +78,16 @@
 CUT = LB // CUTS
 
 
-def lift(slab, pick):
-    def body(which, src, dst, hold, came, went):
+def lift(slab):
+    def body(src, dst, hold, came, went):
+        there = 1 - lax.axis_index("ylo")
+
         def spot(i):
             return pl.ds(i * CUT, CUT)
 
         takes = [
             pltpu.make_async_copy(
-                src.at[which[1], spot(i), pl.ds(0, YM), :], hold.at[spot(i)], came.at[i]
+                src.at[there, spot(i), pl.ds(0, YM), :], hold.at[spot(i)], came.at[i]
             )
             for i in range(CUTS)
         ]
@@ -103,7 +105,7 @@
 
     return pl.pallas_call(
         body,
-        in_specs=[pl.BlockSpec(memory_space=pltpu.SMEM), pl.BlockSpec(memory_space=pltpu.HBM)],
+        in_specs=[pl.BlockSpec(memory_space=pltpu.HBM)],
         out_specs=pl.BlockSpec(memory_space=pltpu.HBM),
         out_shape=jax.ShapeDtypeStruct((LB, YM, NB), BF),
         scratch_shapes=[
@@ -114,7 +116,7 @@
         name="lift",
         cost_estimate=pl.CostEstimate(flops=0, bytes_accessed=4 * LB * YM * NB, transcendentals=0),
         compiler_params=pltpu.CompilerParams(vmem_limit_bytes=24 * 1024 * 1024),
-    )(pick, slab)
+    )(slab)
 
 
 def y_parts(slab, swapped, k_mine, k_other, pick, first, tiles, lo, hi):
@@ -143,22 +145,31 @@
     )
 
 
+def beside(take, tiles):
+    return jnp.concatenate([take(slice(t * TILE, (t + 1) * TILE)) for t in range(tiles)], axis=1)
+
+
 def z_parts(slab, k_mine, pick, first, tiles, lo, hi):
     rows = slice(lo * JB * TILE, hi * JB * TILE)
 
     def body(_, here, km, *outs):
-        part = dot(km[rows], fold(here[0])).reshape(hi - lo, JB, TILE, NB)
-        for k, out in enumerate(outs):
-            out[0] = part[k].astype(BF)
-
-    return call(
-        body,
-        (2, tiles),
+        wide = dot(km[rows], beside(lambda spot: fold(here[0, :, spot]), tiles))
+        for t in range(tiles):
+            part = wide[:, t * NB : (t + 1) * NB].reshape(hi - lo, JB, TILE, NB)
+            for k, out in enumerate(outs):
+                out[0, :, t * TILE : (t + 1) * TILE] = part[k].astype(BF)
+
+    return call(
+        body,
+        (2,),
         [
-            pl.BlockSpec((1, LB, TILE, NB), lambda o, t, s: (s[o], 0, first + t, 0)),
+            pl.BlockSpec(
+                tuple(pl.Element(n) for n in (1, LB, tiles * TILE, NB)),
+                lambda o, s: (s[o], 0, first * TILE, 0),
+            ),
             whole((RW, CL)),
         ],
-        [pl.BlockSpec((1, JB, TILE, NB), lambda o, t, s: (o, 0, t, 0))] * (hi - lo),
+        [pl.BlockSpec((1, JB, tiles * TILE, NB), lambda o, s: (o, 0, 0, 0))] * (hi - lo),
         [jax.ShapeDtypeStruct((2, JB, tiles * TILE, NB), BF)] * (hi - lo),
         (slab, k_mine),
         pick,
@@ -214,15 +225,22 @@
 def z_expand(slots, kt_mine, out, pick, first, tiles):
     def body(_, *refs):
         slot_refs, km, kept = refs[:NZ], refs[NZ], refs[NZ + 2]
-        stack = gathered([s[0] for s in slot_refs])
-        kept[0] = dot(km[...], stack).reshape(LB, TILE, NB).astype(BF)
-
-    return call(
-        body,
-        (2, tiles),
-        [pl.BlockSpec((1, JB, TILE, NB), lambda o, t, s: (o, 0, t, 0))] * NZ
+        wide = dot(
+            km[...], beside(lambda spot: gathered([s[0, :, spot] for s in slot_refs]), tiles)
+        )
+        for t in range(tiles):
+            part = wide[:, t * NB : (t + 1) * NB].reshape(LB, TILE, NB)
+            kept[0, :, t * TILE : (t + 1) * TILE] = part.astype(BF)
+
+    return call(
+        body,
+        (2,),
+        [pl.BlockSpec((1, JB, tiles * TILE, NB), lambda o, s: (o, 0, 0, 0))] * NZ
         + [whole((CL, RW)), pl.BlockSpec(memory_space=pl.ANY)],
-        pl.BlockSpec((1, LB, TILE, NB), lambda o, t, s: (s[o], 0, first + t, 0)),
+        pl.BlockSpec(
+            tuple(pl.Element(n) for n in (1, LB, tiles * TILE, NB)),
+            lambda o, s: (s[o], 0, first * TILE, 0),
+        ),
         jax.ShapeDtypeStruct((2, LB, MB, NB), BF),
         (*slots, kt_mine, out),
         pick,
@@ -231,12 +249,13 @@
     )
 
 
-def put(got, out, pick):
-    def body(which, src, _, dst, sem):
+def put(got, out):
+    def body(src, _, dst, sem):
+        there = 1 - lax.axis_index("ylo")
         copies = [
             pltpu.make_async_copy(
                 src.at[pl.ds(i * CUT, CUT)],
-                dst.at[which[1], pl.ds(i * CUT, CUT), pl.ds(0, YM), :],
+                dst.at[there, pl.ds(i * CUT, CUT), pl.ds(0, YM), :],
                 sem.at[i],
             )
             for i in range(CUTS)
@@ -249,18 +268,17 @@
     return pl.pallas_call(
         body,
         in_specs=[
-            pl.BlockSpec(memory_space=pltpu.SMEM),
-            pl.BlockSpec(memory_space=pltpu.VMEM),
+            pl.BlockSpec(memory_space=pl.ANY),
             pl.BlockSpec(memory_space=pltpu.HBM),
         ],
         out_specs=pl.BlockSpec(memory_space=pltpu.HBM),
         out_shape=jax.ShapeDtypeStruct((2, LB, MB, NB), BF),
         scratch_shapes=[pltpu.SemaphoreType.DMA((CUTS,))],
-        input_output_aliases={2: 0},
+        input_output_aliases={1: 0},
         name="put",
         cost_estimate=pl.CostEstimate(flops=0, bytes_accessed=4 * LB * YM * NB, transcendentals=0),
         compiler_params=pltpu.CompilerParams(vmem_limit_bytes=24 * 1024 * 1024),
-    )(pick, got, out)
+    )(got, out)
 
 
 def to_virtual(summed, v_halves):
@@ -399,7 +417,7 @@
     v_halves = jnp.stack([coef_virtual[:, :HALF], coef_virtual[:, HALF:]])
     vt_halves = coef_t.reshape(2, HALF, NB)
 
-    raised, coef_o = lax.optimization_barrier((lift(slab, pick), coef_occupied.T))
+    raised, coef_o = lax.optimization_barrier((lift(slab), coef_occupied.T))
     swapped = swap(raised)
     k_mine = spread(coef_o, zi * 2 * LB + yi * LB, zi)
     k_other = spread(coef_o, zi * 2 * LB + (1 - yi) * LB, zi)
@@ -424,7 +442,7 @@
     out = y_keep(slots, kt_mine, pick, 0, YT)
     both = jnp.stack([wide_z, swap(wide_z)])
     out = z_expand(chain_gather(both), kt_mine, out, pick, YT, ZT)
-    return put(got, out, pick)
+    return put(got, out)
 
 
 def solution(mesh):

time: 202 us -> 199 us (0.985)
  waiting for transfers between devices: 69.8 us -> 74.6 us
  Pallas kernels: 32 us -> 27.6 us
  starting transfers between devices: 69.7 us -> 66.2 us
    ppermute x29, waiting for transfers between devices: 57.5 us -> 62.2 us  [move(): return lax.ppermute(x, 'z', [(i, (i + step) % NZ) for i in range(NZ)])]
    pallas_call x10, Pallas kernels: 27.7 us -> 24.4 us  [call(): pl.pallas_call(body, grid_spec=spec, out_shape=out_shape, input_output_al...]
    ppermute x29, starting transfers between devices: 57.3 us -> 54 us  [move(): return lax.ppermute(x, 'z', [(i, (i + step) % NZ) for i in range(NZ)])]
  transfers between devices with their start and end apart: 34 -> 34, of which waited for: 20 -> 19; matrix products, arithmetic and copies ran while one was open for 4% -> 4% of each run, Pallas kernels for 10% -> 9%
where the time goes in v5:
time: 199 us; the launch traced here: 198 us
  waiting for transfers between devices  74.6 us (37%)
  starting transfers between devices  66.2 us (33%)
  Pallas kernels  27.6 us (14%)
  blocking collectives  14.7 us (7%)
  other arithmetic  8.67 us (4%)
  local copies, waits for them, and re-layouts  2.7 us (1%)
  matrix products  2.63 us (1%)
    ppermute x29, waiting for transfers between devices, move(): return lax.ppermute(x, 'z', [(i, (i + step) % NZ) for i in range(NZ)])  62.2 us
    ppermute x29, starting transfers between devices, move(): return lax.ppermute(x, 'z', [(i, (i + step) % NZ) for i in range(NZ)])  54 us
    pallas_call x10, Pallas kernels, call(): pl.pallas_call(body, grid_spec=spec, out_shape=out_shape, input_output_al...  24.4 us
    all_to_all x1, blocking collectives, run(): lax.all_to_all(back_one.reshape(NROW, MB, HALF), 'row', 0, 0, tiled=True)  14.7 us
    all_to_all x1, starting transfers between devices, run(): second = lax.all_to_all(first, 'row', 0, 0, tiled=True).reshape(NB, HALF)  7.61 us
    ppermute x4, waiting for transfers between devices, swap(): return lax.ppermute(x, 'ylo', SWAP)  7.46 us
    all_to_all x1, waiting for transfers between devices, run(): second = lax.all_to_all(first, 'row', 0, 0, tiled=True).reshape(NB, HALF)  4.89 us
    ppermute x4, starting transfers between devices, swap(): return lax.ppermute(x, 'ylo', SWAP)  4.62 us
  transfers between devices with their start and end apart: 34, of which 19 were waited for; matrix products, arithmetic and copies ran while one was open for 4% of the time, Pallas kernels for 9%

profile of v5, /device:TPU:2, one launch (start us, length us, event | category | flops | bytes accessed | tf_op | source)
XLA Modules:
  0.0 197.7 jit_solution(9292598199989694134)
XLA Ops:
  6.5 3.0 %shard_map.67 = (bf16[2,8,16,640]{3,2,1,0:T(8,128)(2,1)}, bf16[2,8,16,640]{3,2,1,0:T(8,128)(2,1)S(1)}) custom-call(s32[2]{0:T(128)S(1)} %pad_add_fusion._, bf16[2,40,40,640]{3,2,1,0:T(8,128)(2,1)} %here.7, bf16[512,320]{1,0:T(8,128)(2,1)S(1)} %get-tuple-element.52.km), custom_call_target="tpu_custom_call" | custom-call | flops 209715200 | bytes 2211840 | tf_op jit(solution)/shard_map/pallas_call | solution.py:44
  9.5 5.9 %collective-permute-start.11 = (bf16[2,8,16,640]{3,2,1,0:T(8,128)(2,1)S(1)}, bf16[2,8,16,640]{3,2,1,0:T(8,128)(2,1)S(1)}, u32[]{:S(2)}, u32[]{:S(2)}) collective-permute-start(bf16[2,8,16,640]{3,2,1,0:T(8,128)(2,1)S(1)} %get-tuple-element.39), channel_id=1, source_target_pairs={{0,14},{2,0},{4,2},{6,4},{8,6},{10,8},{12,10},{14,12},{1,15},{3,1}... | collective-permute-start | bytes 983048 | tf_op jit(solution)/shard_map/ppermute | solution.py:347
  15.4 3.1 %shard_map.66 = (bf16[2,8,16,640]{3,2,1,0:T(8,128)(2,1)S(1)}, bf16[2,8,16,640]{3,2,1,0:T(8,128)(2,1)S(1)}, bf16[2,8,16,640]{3,2,1,0:T(8,128)(2,1)S(1)}, bf16[2,8...) custom-call(s32[2]{0:T(128)S(1)} %pad_add_fusion._, ...), custom_call_target="tpu_custom_call" | custom-call | flops 629145600 | bytes 2211840 | tf_op jit(solution)/shard_map/pallas_call | solution.py:44
  23.1 3.7 %collective-permute-start.12 = (bf16[2,8,16,640]{3,2,1,0:T(8,128)(2,1)}, bf16[2,8,16,640]{3,2,1,0:T(8,128)(2,1)}, u32[]{:S(2)}, u32[]{:S(2)}) collective-permute-start(bf16[2,8,16,640]{3,2,1,0:T(8,128)(2,1)} %add_convert_fusion.3), channel_id=1, source_target_pairs={{0,14},{2,0},{4,2},{6,4},{8,6},{10,8},{12,10},{14,12},{1,15},{3,1}... | collective-permute-start | bytes 983048 | tf_op jit(solution)/shard_map/ppermute | solution.py:347
  30.2 3.0 %collective-permute-done.12 = bf16[2,8,16,640]{3,2,1,0:T(8,128)(2,1)} collective-permute-done((bf16[2,8,16,640]{3,2,1,0:T(8,128)(2,1)}, bf16[2,8,16,640]{3,2,1,0:T(8,128)(2,1)}, u32[]{:S(2)}, u32[]{:S(2)}) %collective-permute-start.12) | collective-permute-done | bytes 327712 | tf_op jit(solution)/shard_map/ppermute | solution.py:347
  34.4 3.8 %collective-permute-start.13 = (bf16[2,8,16,640]{3,2,1,0:T(8,128)(2,1)S(1)}, bf16[2,8,16,640]{3,2,1,0:T(8,128)(2,1)S(1)}, u32[]{:S(2)}, u32[]{:S(2)}) collective-permute-start(bf16[2,8,16,640]{3,2,1,0:T(8,128)(2,1)S(1)} %add_convert_fusion.2), channel_id=1, source_target_pairs={{0,14},{2,0},{4,2},{6,4},{8,6},{10,8},{12,10},{14,12},{1,15},{3,1}... | collective-permute-start | bytes 983048 | tf_op jit(solution)/shard_map/ppermute | solution.py:347
  39.7 3.8 %collective-permute-done.13 = bf16[2,8,16,640]{3,2,1,0:T(8,128)(2,1)S(1)} collective-permute-done((bf16[2,8,16,640]{3,2,1,0:T(8,128)(2,1)S(1)}, bf16[2,8,16,640]{3,2,1,0:T(8,128)(2,1)S(1)}, u32[]{:S(2)}, u32[]{:S(2)}) %collective-permute-start.13) | collective-permute-done | bytes 327712 | tf_op jit(solution)/shard_map/ppermute | solution.py:347
  43.5 3.8 %collective-permute-start.14 = (bf16[2,8,16,640]{3,2,1,0:T(8,128)(2,1)S(1)}, bf16[2,8,16,640]{3,2,1,0:T(8,128)(2,1)S(1)}, u32[]{:S(2)}, u32[]{:S(2)}) collective-permute-start(bf16[2,8,16,640]{3,2,1,0:T(8,128)(2,1)S(1)} %add_convert_fusion.1), channel_id=1, source_target_pairs={{0,14},{2,0},{4,2},{6,4},{8,6},{10,8},{12,10},{14,12},{1,15},{3,1}... | collective-permute-start | bytes 983048 | tf_op jit(solution)/shard_map/ppermute | solution.py:347
  47.3 7.5 %collective-permute-done.came = bf16[40,24,640]{2,1,0:T(8,128)(2,1)S(1)} collective-permute-done((bf16[40,24,640]{2,1,0:T(8,128)(2,1)}, bf16[40,24,640]{2,1,0:T(8,128)(2,1)S(1)}, u32[]{:S(2)}, u32[]{:S(2)}) %collective-permute-start) | collective-permute-done | bytes 1228832 | tf_op jit(solution)/shard_map/ppermute | solution.py:351
  54.8 3.5 %shard_map.65 = (bf16[8,24,640]{2,1,0:T(8,128)(2,1)S(1)}, bf16[8,24,640]{2,1,0:T(8,128)(2,1)S(1)}, bf16[8,24,640]{2,1,0:T(8,128)(2,1)S(1)}) custom-call(s32[2]{0:T(128)S(1)} %pad_add_fusion._, bf16[2,40,40,640]{3,2,1,0:T(8,128)(2,1)} %here.7, bf16[40,24,640]{2,1,0:T(8,128)(2,1)S(1)} %collective-permute-done.came, bf16[512,320]{1,0:T(8,128)(2,1)S(1)} %get-tuple-element.52.km, ...), custom_call_target="tpu_custom_call" | custom-call | flops 471859200 | bytes 2990080 | tf_op jit(solution)/shard_map/pallas_call | solution.py:44
  58.7 3.0 %collective-permute-start.5 = (bf16[8,24,640]{2,1,0:T(8,128)(2,1)S(1)}, bf16[8,24,640]{2,1,0:T(8,128)(2,1)S(1)}, u32[]{:S(2)}, u32[]{:S(2)}) collective-permute-start(bf16[8,24,640]{2,1,0:T(8,128)(2,1)S(1)} %get-tuple-element.32), channel_id=1, source_target_pairs={{0,14},{2,0},{4,2},{6,4},{8,6},{10,8},{12,10},{14,12},{1,15},{3,1}... | collective-permute-start | bytes 737288 | tf_op jit(solution)/shard_map/ppermute | solution.py:347
  61.6 3.9 %shard_map.64 = (bf16[8,24,640]{2,1,0:T(8,128)(2,1)S(1)}, bf16[8,24,640]{2,1,0:T(8,128)(2,1)S(1)}, bf16[8,24,640]{2,1,0:T(8,128)(2,1)S(1)}, bf16[8,24,640]{2,1,0:T(8,128)(2,1)S(1)}, bf16[8,24,640]{2,1,0:T(8,128)(2,1)S(1)}) custom-call(s32[2]{0:T(128)S(1)} %pad_add_fusion._, bf16[2,40,40,640]{3,2,1,0:T(8,128)(2,1)} %here.7, ...), custom_call_target="tpu_custom_call" | custom-call | flops 786432000 | bytes 2990080 | tf_op jit(solution)/shard_map/pallas_call | solution.py:44
  65.7 7.1 %collective-permute-done.1 = bf16[8,24,640]{2,1,0:T(8,128)(2,1)S(1)} collective-permute-done((bf16[8,24,640]{2,1,0:T(8,128)(2,1)S(1)}, bf16[8,24,640]{2,1,0:T(8,128)(2,1)S(1)}, u32[]{:S(2)}, u32[]{:S(2)}) %collective-permute-start.1) | collective-permute-done | bytes 245792 | tf_op jit(solution)/shard_map/ppermute | solution.py:347
  73.0 6.3 %collective-permute-start.3 = (bf16[8,24,640]{2,1,0:T(8,128)(2,1)S(1)}, bf16[8,24,640]{2,1,0:T(8,128)(2,1)S(1)}, u32[]{:S(2)}, u32[]{:S(2)}) collective-permute-start(bf16[8,24,640]{2,1,0:T(8,128)(2,1)S(1)} %add_convert_fusion.10), channel_id=1, source_target_pairs={{0,2},{2,4},{4,6},{6,8},{8,10},{10,12},{12,14},{14,0},{1,3},{3,5},... | collective-permute-start | bytes 737288 | tf_op jit(solution)/shard_map/ppermute | solution.py:347
  80.9 3.8 %collective-permute-done.3 = bf16[8,24,640]{2,1,0:T(8,128)(2,1)S(1)} collective-permute-done((bf16[8,24,640]{2,1,0:T(8,128)(2,1)S(1)}, bf16[8,24,640]{2,1,0:T(8,128)(2,1)S(1)}, u32[]{:S(2)}, u32[]{:S(2)}) %collective-permute-start.3) | collective-permute-done | bytes 245792 | tf_op jit(solution)/shard_map/ppermute | solution.py:347
  88.5 3.8 %collective-permute-done.4 = bf16[8,24,640]{2,1,0:T(8,128)(2,1)S(1)} collective-permute-done((bf16[8,24,640]{2,1,0:T(8,128)(2,1)S(1)}, bf16[8,24,640]{2,1,0:T(8,128)(2,1)S(1)}, u32[]{:S(2)}, u32[]{:S(2)}) %collective-permute-start.4) | collective-permute-done | bytes 245792 | tf_op jit(solution)/shard_map/ppermute | solution.py:347
  95.6 7.6 %all-to-all-start = ((bf16[16,40,288]{2,1,0:T(8,128)(2,1)}), bf16[16,40,288]{2,1,0:T(8,128)(2,1)S(1)}, u32[]{:S(2)}, u32[]{:S(2)}) async-start(bf16[16,40,288]{2,1,0:T(8,128)(2,1)} %shard_map.68), calls=%async_computation | async-start | bytes 983040 | tf_op jit(solution)/shard_map/all_to_all | solution.py:434
  106.8 4.9 %all-to-all-done = bf16[16,40,288]{2,1,0:T(8,128)(2,1)S(1)} async-done(((bf16[16,40,288]{2,1,0:T(8,128)(2,1)}), bf16[16,40,288]{2,1,0:T(8,128)(2,1)S(1)}, u32[]{:S(2)}, u32[]{:S(2)}) %all-to-all-start) | async-done | bytes 368672 | tf_op jit(solution)/shard_map/all_to_all | solution.py:434
  112.9 14.7 %all_to_all.10.x = bf16[16,40,288]{2,1,0:T(8,128)(2,1)S(1)} all-to-all(bf16[16,40,288]{2,1,0:T(8,128)(2,1)S(1)} %bitcast.36), channel_id=1, replica_groups=mesh['row'=16,'z'=8,'ylo'=2] {'row'}, dimensions={0} | all-to-all | bytes 737280 | tf_op jit(solution)/shard_map/all_to_all | solution.py:436
  128.3 3.2 %collective-permute-start.16 = (bf16[8,24,640]{2,1,0:T(8,128)(2,1)S(1)}, bf16[8,24,640]{2,1,0:T(8,128)(2,1)S(1)}, u32[]{:S(2)}, u32[]{:S(2)}) collective-permute-start(bf16[8,24,640]{2,1,0:T(8,128)(2,1)S(1)} %get-tuple-element.43.refs_6_), channel_id=1, source_target_pairs={{0,14},{2,0},{4,2},{6,4},{8,6},{10,8},{12,10},{14,12},{1,15},{3,1}... | collective-permute-start | bytes 737288 | tf_op jit(solution)/shard_map/ppermute | solution.py:347
  131.5 6.8 %collective-permute-done.19.refs_5_ = bf16[8,24,640]{2,1,0:T(8,128)(2,1)S(1)} collective-permute-done((bf16[8,24,640]{2,1,0:T(8,128)(2,1)S(1)}, bf16[8,24,640]{2,1,0:T(8,128)(2,1)S(1)}, u32[]{:S(2)}, u32[]{:S(2)}) %collective-permute-start.19) | collective-permute-done | bytes 245792 | tf_op jit(solution)/shard_map/ppermute | solution.py:347
  138.3 3.2 %collective-permute-start.17 = (bf16[8,24,640]{2,1,0:T(8,128)(2,1)S(1)}, bf16[8,24,640]{2,1,0:T(8,128)(2,1)S(1)}, u32[]{:S(2)}, u32[]{:S(2)}) collective-permute-start(bf16[8,24,640]{2,1,0:T(8,128)(2,1)S(1)} %collective-permute-done.16.refs_7_), channel_id=1, source_target_pairs={{0,14},{2,0},{4,2},{6,4},{8,6},{10,8},{12,10},{14,12},{1,15},{3,1}... | collective-permute-start | bytes 737288 | tf_op jit(solution)/shard_map/ppermute | solution.py:347
  142.2 5.3 %collective-permute-done.20.refs_4_ = bf16[8,24,640]{2,1,0:T(8,128)(2,1)S(1)} collective-permute-done((bf16[8,24,640]{2,1,0:T(8,128)(2,1)S(1)}, bf16[8,24,640]{2,1,0:T(8,128)(2,1)S(1)}, u32[]{:S(2)}, u32[]{:S(2)}) %collective-permute-start.20) | collective-permute-done | bytes 245792 | tf_op jit(solution)/shard_map/ppermute | solution.py:347
  147.5 3.2 %collective-permute-start.18 = (bf16[8,24,640]{2,1,0:T(8,128)(2,1)S(1)}, bf16[8,24,640]{2,1,0:T(8,128)(2,1)S(1)}, u32[]{:S(2)}, u32[]{:S(2)}) collective-permute-start(bf16[8,24,640]{2,1,0:T(8,128)(2,1)S(1)} %collective-permute-done.17.refs_8_), channel_id=1, source_target_pairs={{0,14},{2,0},{4,2},{6,4},{8,6},{10,8},{12,10},{14,12},{1,15},{3,1}... | collective-permute-start | bytes 737288 | tf_op jit(solution)/shard_map/ppermute | solution.py:347
  152.4 2.8 %collective-permute-start.22 = (bf16[2,24,640]{2,1,0:T(8,128)(2,1)S(1)}, bf16[2,24,640]{2,1,0:T(8,128)(2,1)S(1)}, u32[]{:S(2)}, u32[]{:S(2)}) collective-permute-start(bf16[2,24,640]{2,1,0:T(8,128)(2,1)S(1)} %slice.37), channel_id=1, source_target_pairs={{0,12},{2,14},{4,0},{6,2},{8,4},{10,6},{12,8},{14,10},{1,13},{3,15... | collective-permute-start | bytes 184328 | tf_op jit(solution)/shard_map/ppermute | solution.py:347
  155.2 9.6 %collective-permute-done.22.refs_2_ = bf16[2,24,640]{2,1,0:T(8,128)(2,1)S(1)} collective-permute-done((bf16[2,24,640]{2,1,0:T(8,128)(2,1)S(1)}, bf16[2,24,640]{2,1,0:T(8,128)(2,1)S(1)}, u32[]{:S(2)}, u32[]{:S(2)}) %collective-permute-start.22) | collective-permute-done | bytes 61472 | tf_op jit(solution)/shard_map/ppermute | solution.py:347
  167.6 2.8 %collective-permute-start.27 = (bf16[2,8,16,640]{3,2,1,0:T(8,128)(2,1)S(1)}, bf16[2,8,16,640]{3,2,1,0:T(8,128)(2,1)S(1)}, u32[]{:S(2)}, u32[]{:S(2)}) collective-permute-start(bf16[2,8,16,640]{3,2,1,0:T(8,128)(2,1)S(1)} %collective-permute-done.26.refs_6_), channel_id=1, source_target_pairs={{0,14},{2,0},{4,2},{6,4},{8,6},{10,8},{12,10},{14,12},{1,15},{3,1}... | collective-permute-start | bytes 983048 | tf_op jit(solution)/shard_map/ppermute | solution.py:347
  170.4 5.3 %collective-permute-done.30.refs_4_ = bf16[2,8,16,640]{3,2,1,0:T(8,128)(2,1)S(1)} collective-permute-done((bf16[2,8,16,640]{3,2,1,0:T(8,128)(2,1)S(1)}, bf16[2,8,16,640]{3,2,1,0:T(8,128)(2,1)S(1)}, u32[]{:S(2)}, u32[]{:S(2)}) %collective-permute-start.30) | collective-permute-done | bytes 327712 | tf_op jit(solution)/shard_map/ppermute | solution.py:347
  176.4 2.8 %collective-permute-start.28 = (bf16[2,8,16,640]{3,2,1,0:T(8,128)(2,1)S(1)}, bf16[2,8,16,640]{3,2,1,0:T(8,128)(2,1)S(1)}, u32[]{:S(2)}, u32[]{:S(2)}) collective-permute-start(bf16[2,8,16,640]{3,2,1,0:T(8,128)(2,1)S(1)} %collective-permute-done.27.refs_7_), channel_id=1, source_target_pairs={{0,14},{2,0},{4,2},{6,4},{8,6},{10,8},{12,10},{14,12},{1,15},{3,1}... | collective-permute-start | bytes 983048 | tf_op jit(solution)/shard_map/ppermute | solution.py:347
  179.3 6.2 %collective-permute-done.31.refs_3_ = bf16[2,8,16,640]{3,2,1,0:T(8,128)(2,1)S(1)} collective-permute-done((bf16[2,8,16,640]{3,2,1,0:T(8,128)(2,1)S(1)}, bf16[2,8,16,640]{3,2,1,0:T(8,128)(2,1)S(1)}, u32[]{:S(2)}, u32[]{:S(2)}) %collective-permute-start.31) | collective-permute-done | bytes 327712 | tf_op jit(solution)/shard_map/ppermute | solution.py:347
  186.5 2.8 %collective-permute-start.29 = (bf16[2,8,16,640]{3,2,1,0:T(8,128)(2,1)S(1)}, bf16[2,8,16,640]{3,2,1,0:T(8,128)(2,1)S(1)}, u32[]{:S(2)}, u32[]{:S(2)}) collective-permute-start(bf16[2,8,16,640]{3,2,1,0:T(8,128)(2,1)S(1)} %collective-permute-done.28.refs_0_), channel_id=1, source_target_pairs={{0,14},{2,0},{4,2},{6,4},{8,6},{10,8},{12,10},{14,12},{1,15},{3,1}... | collective-permute-start | bytes 983048 | tf_op jit(solution)/shard_map/ppermute | solution.py:347
  189.2 3.1 %shard_map.72.refs_9_ = bf16[2,40,40,640]{3,2,1,0:T(8,128)(2,1)} custom-call(s32[2]{0:T(128)S(1)} %pad_add_fusion._, bf16[8,24,640]{2,1,0:T(8,128)(2,1)S(1)} %collective-permute-done.18.refs_0_, bf16[6,24,640]{2,1,0:T(8,128)(2,1)S(1)} %collective-permute-done.21.refs_1_, bf16[2,24,640]{2,1,0:T(8,128)(2,1)S(1)} %collective-permute-done.22.refs_2_, ...), custom_call_target="tpu_custom_call" | custom-call | flops 629145600 | bytes 1146880 | tf_op jit(solution)/shard_map/pallas_call | solution.py:44
  (119 shorter events, 44.0 us)
Async XLA Ops:
  9.5 12.8 %collective-permute-start.11 = (bf16[2,8,16,640]{3,2,1,0:T(8,128)(2,1)S(1)}, bf16[2,8,16,640]{3,2,1,0:T(8,128)(2,1)S(1)}, u32[]{:S(2)}, u32[]{:S(2)}) collective-permute-start(bf16[2,8,16,640]{3,2,1,0:T(8,128)(2,1)S(1)} %get-tuple-element.39), channel_id=1, source_target_pairs={{0,14},{2,0},{4,2},{6,4},{8,6},{10,8},{12,10},{14,12},{1,15},{3,1}... | collective-permute-start | bytes 983048 | tf_op jit(solution)/shard_map/ppermute | solution.py:347
  15.4 13.6 %collective-permute-start.8 = (bf16[2,8,16,640]{3,2,1,0:T(8,128)(2,1)}, bf16[2,8,16,640]{3,2,1,0:T(8,128)(2,1)}, u32[]{:S(2)}, u32[]{:S(2)}) collective-permute-start(bf16[2,8,16,640]{3,2,1,0:T(8,128)(2,1)} %get-tuple-element.36), channel_id=1, source_target_pairs={{0,2},{2,4},{4,6},{6,8},{8,10},{10,12},{12,14},{14,0},{1,3},{3,5},... | collective-permute-start | bytes 983048 | tf_op jit(solution)/shard_map/ppermute | solution.py:347
  23.1 10.1 %collective-permute-start.12 = (bf16[2,8,16,640]{3,2,1,0:T(8,128)(2,1)}, bf16[2,8,16,640]{3,2,1,0:T(8,128)(2,1)}, u32[]{:S(2)}, u32[]{:S(2)}) collective-permute-start(bf16[2,8,16,640]{3,2,1,0:T(8,128)(2,1)} %add_convert_fusion.3), channel_id=1, source_target_pairs={{0,14},{2,0},{4,2},{6,4},{8,6},{10,8},{12,10},{14,12},{1,15},{3,1}... | collective-permute-start | bytes 983048 | tf_op jit(solution)/shard_map/ppermute | solution.py:347
  26.8 27.9 %collective-permute-start = (bf16[40,24,640]{2,1,0:T(8,128)(2,1)}, bf16[40,24,640]{2,1,0:T(8,128)(2,1)S(1)}, u32[]{:S(2)}, u32[]{:S(2)}) collective-permute-start(bf16[40,24,640]{2,1,0:T(8,128)(2,1)} %lift.1), channel_id=1, source_target_pairs={{0,1},{1,0},{2,3},{3,2},{4,5},{5,4},{6,7},{7,6},{8,9},{9,8},{10,11... | collective-permute-start | bytes 3686408 | tf_op jit(solution)/shard_map/ppermute | solution.py:351
  30.2 9.3 %collective-permute-start.9 = (bf16[2,8,16,640]{3,2,1,0:T(8,128)(2,1)S(1)}, bf16[2,8,16,640]{3,2,1,0:T(8,128)(2,1)S(1)}, u32[]{:S(2)}, u32[]{:S(2)}) collective-permute-start(bf16[2,8,16,640]{3,2,1,0:T(8,128)(2,1)S(1)} %add_convert_fusion.5), channel_id=1, source_target_pairs={{0,2},{2,4},{4,6},{6,8},{8,10},{10,12},{12,14},{14,0},{1,3},{3,5},... | collective-permute-start | bytes 983048 | tf_op jit(solution)/shard_map/ppermute | solution.py:347
  34.4 9.0 %collective-permute-start.13 = (bf16[2,8,16,640]{3,2,1,0:T(8,128)(2,1)S(1)}, bf16[2,8,16,640]{3,2,1,0:T(8,128)(2,1)S(1)}, u32[]{:S(2)}, u32[]{:S(2)}) collective-permute-start(bf16[2,8,16,640]{3,2,1,0:T(8,128)(2,1)S(1)} %add_convert_fusion.2), channel_id=1, source_target_pairs={{0,14},{2,0},{4,2},{6,4},{8,6},{10,8},{12,10},{14,12},{1,15},{3,1}... | collective-permute-start | bytes 983048 | tf_op jit(solution)/shard_map/ppermute | solution.py:347
  39.6 26.0 %collective-permute-start.10 = (bf16[2,8,16,640]{3,2,1,0:T(8,128)(2,1)S(1)}, bf16[2,8,16,640]{3,2,1,0:T(8,128)(2,1)S(1)}, u32[]{:S(2)}, u32[]{:S(2)}) collective-permute-start(bf16[2,8,16,640]{3,2,1,0:T(8,128)(2,1)S(1)} %add_convert_fusion.4), channel_id=1, source_target_pairs={{0,2},{2,4},{4,6},{6,8},{8,10},{10,12},{12,14},{14,0},{1,3},{3,5},... | collective-permute-start | bytes 983048 | tf_op jit(solution)/shard_map/ppermute | solution.py:347
  43.5 22.1 %collective-permute-start.14 = (bf16[2,8,16,640]{3,2,1,0:T(8,128)(2,1)S(1)}, bf16[2,8,16,640]{3,2,1,0:T(8,128)(2,1)S(1)}, u32[]{:S(2)}, u32[]{:S(2)}) collective-permute-start(bf16[2,8,16,640]{3,2,1,0:T(8,128)(2,1)S(1)} %add_convert_fusion.1), channel_id=1, source_target_pairs={{0,14},{2,0},{4,2},{6,4},{8,6},{10,8},{12,10},{14,12},{1,15},{3,1}... | collective-permute-start | bytes 983048 | tf_op jit(solution)/shard_map/ppermute | solution.py:347
  58.3 14.5 %collective-permute-start.1 = (bf16[8,24,640]{2,1,0:T(8,128)(2,1)S(1)}, bf16[8,24,640]{2,1,0:T(8,128)(2,1)S(1)}, u32[]{:S(2)}, u32[]{:S(2)}) collective-permute-start(bf16[8,24,640]{2,1,0:T(8,128)(2,1)S(1)} %get-tuple-element.28), channel_id=1, source_target_pairs={{0,2},{2,4},{4,6},{6,8},{8,10},{10,12},{12,14},{14,0},{1,3},{3,5},... | collective-permute-start | bytes 737288 | tf_op jit(solution)/shard_map/ppermute | solution.py:347
  58.4 14.5 %collective-permute-start.2 = (bf16[8,24,640]{2,1,0:T(8,128)(2,1)S(1)}, bf16[8,24,640]{2,1,0:T(8,128)(2,1)S(1)}, u32[]{:S(2)}, u32[]{:S(2)}) collective-permute-start(bf16[8,24,640]{2,1,0:T(8,128)(2,1)S(1)} %get-tuple-element.30), channel_id=1, source_target_pairs={{0,4},{2,6},{4,8},{6,10},{8,12},{10,14},{12,0},{14,2},{1,5},{3,7},... | collective-permute-start | bytes 737288 | tf_op jit(solution)/shard_map/ppermute | solution.py:347
  58.7 20.5 %collective-permute-start.5 = (bf16[8,24,640]{2,1,0:T(8,128)(2,1)S(1)}, bf16[8,24,640]{2,1,0:T(8,128)(2,1)S(1)}, u32[]{:S(2)}, u32[]{:S(2)}) collective-permute-start(bf16[8,24,640]{2,1,0:T(8,128)(2,1)S(1)} %get-tuple-element.32), channel_id=1, source_target_pairs={{0,14},{2,0},{4,2},{6,4},{8,6},{10,8},{12,10},{14,12},{1,15},{3,1}... | collective-permute-start | bytes 737288 | tf_op jit(solution)/shard_map/ppermute | solution.py:347
  73.0 11.7 %collective-permute-start.3 = (bf16[8,24,640]{2,1,0:T(8,128)(2,1)S(1)}, bf16[8,24,640]{2,1,0:T(8,128)(2,1)S(1)}, u32[]{:S(2)}, u32[]{:S(2)}) collective-permute-start(bf16[8,24,640]{2,1,0:T(8,128)(2,1)S(1)} %add_convert_fusion.10), channel_id=1, source_target_pairs={{0,2},{2,4},{4,6},{6,8},{8,10},{10,12},{12,14},{14,0},{1,3},{3,5},... | collective-permute-start | bytes 737288 | tf_op jit(solution)/shard_map/ppermute | solution.py:347
  79.3 8.3 %collective-permute-start.6 = (bf16[8,24,640]{2,1,0:T(8,128)(2,1)S(1)}, bf16[8,24,640]{2,1,0:T(8,128)(2,1)S(1)}, u32[]{:S(2)}, u32[]{:S(2)}) collective-permute-start(bf16[8,24,640]{2,1,0:T(8,128)(2,1)S(1)} %add_convert_fusion.8), channel_id=1, source_target_pairs={{0,14},{2,0},{4,2},{6,4},{8,6},{10,8},{12,10},{14,12},{1,15},{3,1}... | collective-permute-start | bytes 737288 | tf_op jit(solution)/shard_map/ppermute | solution.py:347
  79.4 9.0 %collective-permute-start.15 = (bf16[8,16,640]{2,1,0:T(8,128)(2,1)S(1)}, bf16[8,16,640]{2,1,0:T(8,128)(2,1)S(1)}, u32[]{:S(2)}, u32[]{:S(2)}) collective-permute-start(bf16[8,16,640]{2,1,0:T(8,128)(2,1)S(1)} %slice_bitcast_fusion.2), channel_id=1, source_target_pairs={{0,1},{1,0},{2,3},{3,2},{4,5},{5,4},{6,7},{7,6},{8,9},{9,8},{10,11... | collective-permute-start | bytes 491528 | tf_op jit(solution)/shard_map/ppermute | solution.py:351
  84.8 7.5 %collective-permute-start.4 = (bf16[8,24,640]{2,1,0:T(8,128)(2,1)S(1)}, bf16[8,24,640]{2,1,0:T(8,128)(2,1)S(1)}, u32[]{:S(2)}, u32[]{:S(2)}) collective-permute-start(bf16[8,24,640]{2,1,0:T(8,128)(2,1)S(1)} %add_convert_fusion.9), channel_id=1, source_target_pairs={{0,2},{2,4},{4,6},{6,8},{8,10},{10,12},{12,14},{14,0},{1,3},{3,5},... | collective-permute-start | bytes 737288 | tf_op jit(solution)/shard_map/ppermute | solution.py:347
  95.6 16.0 %all-to-all-start = ((bf16[16,40,288]{2,1,0:T(8,128)(2,1)}), bf16[16,40,288]{2,1,0:T(8,128)(2,1)S(1)}, u32[]{:S(2)}, u32[]{:S(2)}) async-start(bf16[16,40,288]{2,1,0:T(8,128)(2,1)} %shard_map.68), calls=%async_computation | async-start | bytes 983040 | tf_op jit(solution)/shard_map/all_to_all | solution.py:434
  128.2 10.1 %collective-permute-start.19 = (bf16[8,24,640]{2,1,0:T(8,128)(2,1)S(1)}, bf16[8,24,640]{2,1,0:T(8,128)(2,1)S(1)}, u32[]{:S(2)}, u32[]{:S(2)}) collective-permute-start(bf16[8,24,640]{2,1,0:T(8,128)(2,1)S(1)} %get-tuple-element.43.refs_6_), channel_id=1, source_target_pairs={{0,2},{2,4},{4,6},{6,8},{8,10},{10,12},{12,14},{14,0},{1,3},{3,5},... | collective-permute-start | bytes 737288 | tf_op jit(solution)/shard_map/ppermute | solution.py:347
  128.3 10.0 %collective-permute-start.16 = (bf16[8,24,640]{2,1,0:T(8,128)(2,1)S(1)}, bf16[8,24,640]{2,1,0:T(8,128)(2,1)S(1)}, u32[]{:S(2)}, u32[]{:S(2)}) collective-permute-start(bf16[8,24,640]{2,1,0:T(8,128)(2,1)S(1)} %get-tuple-element.43.refs_6_), channel_id=1, source_target_pairs={{0,14},{2,0},{4,2},{6,4},{8,6},{10,8},{12,10},{14,12},{1,15},{3,1}... | collective-permute-start | bytes 737288 | tf_op jit(solution)/shard_map/ppermute | solution.py:347
  138.3 9.2 %collective-permute-start.20 = (bf16[8,24,640]{2,1,0:T(8,128)(2,1)S(1)}, bf16[8,24,640]{2,1,0:T(8,128)(2,1)S(1)}, u32[]{:S(2)}, u32[]{:S(2)}) collective-permute-start(bf16[8,24,640]{2,1,0:T(8,128)(2,1)S(1)} %collective-permute-done.19.refs_5_), channel_id=1, source_target_pairs={{0,2},{2,4},{4,6},{6,8},{8,10},{10,12},{12,14},{14,0},{1,3},{3,5},... | collective-permute-start | bytes 737288 | tf_op jit(solution)/shard_map/ppermute | solution.py:347
  138.3 9.2 %collective-permute-start.17 = (bf16[8,24,640]{2,1,0:T(8,128)(2,1)S(1)}, bf16[8,24,640]{2,1,0:T(8,128)(2,1)S(1)}, u32[]{:S(2)}, u32[]{:S(2)}) collective-permute-start(bf16[8,24,640]{2,1,0:T(8,128)(2,1)S(1)} %collective-permute-done.16.refs_7_), channel_id=1, source_target_pairs={{0,14},{2,0},{4,2},{6,4},{8,6},{10,8},{12,10},{14,12},{1,15},{3,1}... | collective-permute-start | bytes 737288 | tf_op jit(solution)/shard_map/ppermute | solution.py:347
  141.5 9.3 %collective-permute-start.25 = (bf16[8,16,640]{2,1,0:T(8,128)(2,1)S(1)}, bf16[8,16,640]{2,1,0:T(8,128)(2,1)S(1)}, u32[]{:S(2)}, u32[]{:S(2)}) collective-permute-start(bf16[8,16,640]{2,1,0:T(8,128)(2,1)S(1)} %get-tuple-element.44), channel_id=1, source_target_pairs={{0,1},{1,0},{2,3},{3,2},{4,5},{5,4},{6,7},{7,6},{8,9},{9,8},{10,11... | collective-permute-start | bytes 491528 | tf_op jit(solution)/shard_map/ppermute | solution.py:351
  147.5 17.3 %collective-permute-start.23 = (bf16[8,24,640]{2,1,0:T(8,128)(2,1)S(1)}, bf16[8,24,640]{2,1,0:T(8,128)(2,1)S(1)}, u32[]{:S(2)}, u32[]{:S(2)}) collective-permute-start(bf16[8,24,640]{2,1,0:T(8,128)(2,1)S(1)} %collective-permute-done.20.refs_4_), channel_id=1, source_target_pairs={{0,2},{2,4},{4,6},{6,8},{8,10},{10,12},{12,14},{14,0},{1,3},{3,5},... | collective-permute-start | bytes 737288 | tf_op jit(solution)/shard_map/ppermute | solution.py:347
  147.5 17.3 %collective-permute-start.18 = (bf16[8,24,640]{2,1,0:T(8,128)(2,1)S(1)}, bf16[8,24,640]{2,1,0:T(8,128)(2,1)S(1)}, u32[]{:S(2)}, u32[]{:S(2)}) collective-permute-start(bf16[8,24,640]{2,1,0:T(8,128)(2,1)S(1)} %collective-permute-done.17.refs_8_), channel_id=1, source_target_pairs={{0,14},{2,0},{4,2},{6,4},{8,6},{10,8},{12,10},{14,12},{1,15},{3,1}... | collective-permute-start | bytes 737288 | tf_op jit(solution)/shard_map/ppermute | solution.py:347
  150.7 14.0 %collective-permute-start.21 = (bf16[6,24,640]{2,1,0:T(8,128)(2,1)S(1)}, bf16[6,24,640]{2,1,0:T(8,128)(2,1)S(1)}, u32[]{:S(2)}, u32[]{:S(2)}) collective-permute-start(bf16[6,24,640]{2,1,0:T(8,128)(2,1)S(1)} %slice.36), channel_id=1, source_target_pairs={{0,4},{2,6},{4,8},{6,10},{8,12},{10,14},{12,0},{14,2},{1,5},{3,7},... | collective-permute-start | bytes 552968 | tf_op jit(solution)/shard_map/ppermute | solution.py:347
  150.9 16.7 %collective-permute-start.26 = (bf16[2,8,16,640]{3,2,1,0:T(8,128)(2,1)S(1)}, bf16[2,8,16,640]{3,2,1,0:T(8,128)(2,1)S(1)}, u32[]{:S(2)}, u32[]{:S(2)}) collective-permute-start(bf16[2,8,16,640]{3,2,1,0:T(8,128)(2,1)S(1)} %pad_maximum_fusion.2.refs_5_), channel_id=1, source_target_pairs={{0,14},{2,0},{4,2},{6,4},{8,6},{10,8},{12,10},{14,12},{1,15},{3,1}... | collective-permute-start | bytes 983048 | tf_op jit(solution)/shard_map/ppermute | solution.py:347
  152.4 12.3 %collective-permute-start.22 = (bf16[2,24,640]{2,1,0:T(8,128)(2,1)S(1)}, bf16[2,24,640]{2,1,0:T(8,128)(2,1)S(1)}, u32[]{:S(2)}, u32[]{:S(2)}) collective-permute-start(bf16[2,24,640]{2,1,0:T(8,128)(2,1)S(1)} %slice.37), channel_id=1, source_target_pairs={{0,12},{2,14},{4,0},{6,2},{8,4},{10,6},{12,8},{14,10},{1,13},{3,15... | collective-permute-start | bytes 184328 | tf_op jit(solution)/shard_map/ppermute | solution.py:347
  166.4 30.1 %collective-permute-start.24 = (bf16[40,24,640]{2,1,0:T(8,128)(2,1)S(1)}, bf16[40,24,640]{2,1,0:T(8,128)(2,1)S(1)}, u32[]{:S(2)}, u32[]{:S(2)}) collective-permute-start(bf16[40,24,640]{2,1,0:T(8,128)(2,1)S(1)} %shard_map.71), channel_id=1, source_target_pairs={{0,1},{1,0},{2,3},{3,2},{4,5},{5,4},{6,7},{7,6},{8,9},{9,8},{10,11... | collective-permute-start | bytes 3686408 | tf_op jit(solution)/shard_map/ppermute | solution.py:351
  167.2 8.5 %collective-permute-start.30 = (bf16[2,8,16,640]{3,2,1,0:T(8,128)(2,1)S(1)}, bf16[2,8,16,640]{3,2,1,0:T(8,128)(2,1)S(1)}, u32[]{:S(2)}, u32[]{:S(2)}) collective-permute-start(bf16[2,8,16,640]{3,2,1,0:T(8,128)(2,1)S(1)} %pad_maximum_fusion.2.refs_5_), channel_id=1, source_target_pairs={{0,2},{2,4},{4,6},{6,8},{8,10},{10,12},{12,14},{14,0},{1,3},{3,5},... | collective-permute-start | bytes 983048 | tf_op jit(solution)/shard_map/ppermute | solution.py:347
  167.6 8.8 %collective-permute-start.27 = (bf16[2,8,16,640]{3,2,1,0:T(8,128)(2,1)S(1)}, bf16[2,8,16,640]{3,2,1,0:T(8,128)(2,1)S(1)}, u32[]{:S(2)}, u32[]{:S(2)}) collective-permute-start(bf16[2,8,16,640]{3,2,1,0:T(8,128)(2,1)S(1)} %collective-permute-done.26.refs_6_), channel_id=1, source_target_pairs={{0,14},{2,0},{4,2},{6,4},{8,6},{10,8},{12,10},{14,12},{1,15},{3,1}... | collective-permute-start | bytes 983048 | tf_op jit(solution)/shard_map/ppermute | solution.py:347
  175.7 9.7 %collective-permute-start.31 = (bf16[2,8,16,640]{3,2,1,0:T(8,128)(2,1)S(1)}, bf16[2,8,16,640]{3,2,1,0:T(8,128)(2,1)S(1)}, u32[]{:S(2)}, u32[]{:S(2)}) collective-permute-start(bf16[2,8,16,640]{3,2,1,0:T(8,128)(2,1)S(1)} %collective-permute-done.30.refs_4_), channel_id=1, source_target_pairs={{0,2},{2,4},{4,6},{6,8},{8,10},{10,12},{12,14},{14,0},{1,3},{3,5},... | collective-permute-start | bytes 983048 | tf_op jit(solution)/shard_map/ppermute | solution.py:347
  176.4 10.0 %collective-permute-start.28 = (bf16[2,8,16,640]{3,2,1,0:T(8,128)(2,1)S(1)}, bf16[2,8,16,640]{3,2,1,0:T(8,128)(2,1)S(1)}, u32[]{:S(2)}, u32[]{:S(2)}) collective-permute-start(bf16[2,8,16,640]{3,2,1,0:T(8,128)(2,1)S(1)} %collective-permute-done.27.refs_7_), channel_id=1, source_target_pairs={{0,14},{2,0},{4,2},{6,4},{8,6},{10,8},{12,10},{14,12},{1,15},{3,1}... | collective-permute-start | bytes 983048 | tf_op jit(solution)/shard_map/ppermute | solution.py:347
  185.4 8.3 %collective-permute-start.32 = (bf16[2,8,16,640]{3,2,1,0:T(8,128)(2,1)S(1)}, bf16[2,8,16,640]{3,2,1,0:T(8,128)(2,1)S(1)}, u32[]{:S(2)}, u32[]{:S(2)}) collective-permute-start(bf16[2,8,16,640]{3,2,1,0:T(8,128)(2,1)S(1)} %collective-permute-done.31.refs_3_), channel_id=1, source_target_pairs={{0,2},{2,4},{4,6},{6,8},{8,10},{10,12},{12,14},{14,0},{1,3},{3,5},... | collective-permute-start | bytes 983048 | tf_op jit(solution)/shard_map/ppermute | solution.py:347
  (18 other events, 324.0 us)

commit v6 on v5

--- a/solution.py
+++ b/solution.py
@@ -25,7 +25,7 @@
 YM, ZM = YT * TILE, ZT * TILE
 LEAD = 3
 FAR = NZ // 2
-JH = 6
+JH = JB // 2
 
 
 def dot(a, b):
@@ -281,18 +281,19 @@
     )(got, out)
 
 
-def to_virtual(summed, v_halves):
+def to_virtual(summed, vt_halves):
     def body(s, v, out):
         flat = s[...].astype(F32).reshape(JB * MB, NB).astype(BF)
-        out[...] = dot(flat, v[0]).reshape(JB, MB, HALF).astype(BF)
+        wide = lax.dot_general(flat, v[0], (((1,), (1,)), ((), ())), preferred_element_type=F32)
+        out[...] = wide.reshape(JB, MB, HALF).astype(BF)
 
     return call(
         body,
         (2,),
-        [whole((JB, MB, NB)), pl.BlockSpec((1, NB, HALF), lambda h: (h, 0, 0))],
+        [whole((JB, MB, NB)), pl.BlockSpec((1, HALF, NB), lambda h: (h, 0, 0))],
         pl.BlockSpec((JB, MB, HALF), lambda h: (h, 0, 0)),
         jax.ShapeDtypeStruct((NROW, MB, HALF), BF),
-        (summed, v_halves),
+        (summed, vt_halves),
         flops=2 * JB * MB * NB * NV,
     )
 
@@ -414,7 +415,6 @@
     row = (jnp.where(ri // JB == 0, ev[:HALF], ev[HALF:]) - energy_i - energy_j)[None, :]
     column = ev[:, None]
     coef_t = coef_virtual.T
-    v_halves = jnp.stack([coef_virtual[:, :HALF], coef_virtual[:, HALF:]])
     vt_halves = coef_t.reshape(2, HALF, NB)
 
     raised, coef_o = lax.optimization_barrier((lift(slab), coef_occupied.T))
@@ -430,9 +430,10 @@
     lead = tree_sum(unrolled([*head, *tail]))
     summed = jnp.concatenate([lead, last], axis=1)
 
-    first = to_virtual(summed, v_halves)
+    first = to_virtual(summed, vt_halves)
+    first, coef_late = lax.optimization_barrier((first, coef_virtual))
     second = lax.all_to_all(first, "row", 0, 0, tiled=True).reshape(NB, HALF)
-    back_one = divide(second, coef_virtual, coef_t, column, row)
+    back_one = divide(second, coef_late, coef_t, column, row)
     back = lax.all_to_all(back_one.reshape(NROW, MB, HALF), "row", 0, 0, tiled=True)
     wide_y, wide_z = to_basis(back, vt_halves, (YM, ZM))
 

time: 199 us -> 196 us (0.985)
  other arithmetic: 8.67 us -> 4.71 us
  starting transfers between devices: 66.2 us -> 68.8 us
    convert_element_type x12, other arithmetic: 3.88 us -> 0.96 us  [add(): return total.astype(BF)]
    ppermute x29, starting transfers between devices: 54 us -> 56.7 us  [move(): return lax.ppermute(x, 'z', [(i, (i + step) % NZ) for i in range(NZ)])]
  transfers between devices with their start and end apart: 34 -> 34, of which waited for: 19 -> 20; matrix products, arithmetic and copies ran while one was open for 4% -> 2% of each run, Pallas kernels for 9% -> 9%
where the time goes in v6:
time: 196 us; the launch traced here: 195 us
  waiting for transfers between devices  76 us (39%)
  starting transfers between devices  68.8 us (35%)
  Pallas kernels  27.3 us (14%)
  blocking collectives  14.6 us (7%)
  other arithmetic  4.71 us (2%)
    ppermute x29, waiting for transfers between devices, move(): return lax.ppermute(x, 'z', [(i, (i + step) % NZ) for i in range(NZ)])  62.8 us
    ppermute x29, starting transfers between devices, move(): return lax.ppermute(x, 'z', [(i, (i + step) % NZ) for i in range(NZ)])  56.7 us
    pallas_call x10, Pallas kernels, call(): pl.pallas_call(body, grid_spec=spec, out_shape=out_shape, input_output_al...  23.7 us
    all_to_all x1, blocking collectives, run(): lax.all_to_all(back_one.reshape(NROW, MB, HALF), 'row', 0, 0, tiled=True)  14.6 us
    ppermute x4, waiting for transfers between devices, swap(): return lax.ppermute(x, 'ylo', SWAP)  8.56 us
    all_to_all x1, starting transfers between devices, run(): second = lax.all_to_all(first, 'row', 0, 0, tiled=True).reshape(NB, HALF)  7.47 us
    ppermute x4, starting transfers between devices, swap(): return lax.ppermute(x, 'ylo', SWAP)  4.68 us
    all_to_all x1, waiting for transfers between devices, run(): second = lax.all_to_all(first, 'row', 0, 0, tiled=True).reshape(NB, HALF)  4.58 us
  transfers between devices with their start and end apart: 34, of which 20 were waited for; matrix products, arithmetic and copies ran while one was open for 2% of the time, Pallas kernels for 9%

profile of v6, /device:TPU:2, one launch (start us, length us, event | category | flops | bytes accessed | tf_op | source)
XLA Modules:
  0.0 194.8 jit_solution(2012076693403818785)
XLA Ops:
  7.6 5.9 %collective-permute-start.11 = (bf16[2,8,16,640]{3,2,1,0:T(8,128)(2,1)S(1)}, bf16[2,8,16,640]{3,2,1,0:T(8,128)(2,1)S(1)}, u32[]{:S(2)}, u32[]{:S(2)}) collective-permute-start(bf16[2,8,16,640]{3,2,1,0:T(8,128)(2,1)S(1)} %get-tuple-element.41), channel_id=1, source_target_pairs={{0,14},{2,0},{4,2},{6,4},{8,6},{10,8},{12,10},{14,12},{1,15},{3,1}... | collective-permute-start | bytes 983048 | tf_op jit(solution)/shard_map/ppermute | solution.py:348
  13.6 3.1 %shard_map.66 = (bf16[2,8,16,640]{3,2,1,0:T(8,128)(2,1)S(1)}, bf16[2,8,16,640]{3,2,1,0:T(8,128)(2,1)S(1)}, bf16[2,8,16,640]{3,2,1,0:T(8,128)(2,1)S(1)}, bf16[2,8...) custom-call(s32[2]{0:T(128)S(1)} %pad_add_fusion._, ...), custom_call_target="tpu_custom_call" | custom-call | flops 629145600 | bytes 2211840 | tf_op jit(solution)/shard_map/pallas_call | solution.py:44
  16.7 3.9 %collective-permute-done.11 = bf16[2,8,16,640]{3,2,1,0:T(8,128)(2,1)S(1)} collective-permute-done((bf16[2,8,16,640]{3,2,1,0:T(8,128)(2,1)S(1)}, bf16[2,8,16,640]{3,2,1,0:T(8,128)(2,1)S(1)}, u32[]{:S(2)}, u32[]{:S(2)}) %collective-permute-start.11) | collective-permute-done | bytes 327712 | tf_op jit(solution)/shard_map/ppermute | solution.py:348
  20.6 3.8 %collective-permute-start.12 = (bf16[2,8,16,640]{3,2,1,0:T(8,128)(2,1)S(1)}, bf16[2,8,16,640]{3,2,1,0:T(8,128)(2,1)S(1)}, u32[]{:S(2)}, u32[]{:S(2)}) collective-permute-start(bf16[2,8,16,640]{3,2,1,0:T(8,128)(2,1)S(1)} %add_convert_fusion.3), channel_id=1, source_target_pairs={{0,14},{2,0},{4,2},{6,4},{8,6},{10,8},{12,10},{14,12},{1,15},{3,1}... | collective-permute-start | bytes 983048 | tf_op jit(solution)/shard_map/ppermute | solution.py:348
  26.2 4.4 %collective-permute-done.12 = bf16[2,8,16,640]{3,2,1,0:T(8,128)(2,1)S(1)} collective-permute-done((bf16[2,8,16,640]{3,2,1,0:T(8,128)(2,1)S(1)}, bf16[2,8,16,640]{3,2,1,0:T(8,128)(2,1)S(1)}, u32[]{:S(2)}, u32[]{:S(2)}) %collective-permute-start.12) | collective-permute-done | bytes 327712 | tf_op jit(solution)/shard_map/ppermute | solution.py:348
  30.6 3.8 %collective-permute-start.13 = (bf16[2,8,16,640]{3,2,1,0:T(8,128)(2,1)S(1)}, bf16[2,8,16,640]{3,2,1,0:T(8,128)(2,1)S(1)}, u32[]{:S(2)}, u32[]{:S(2)}) collective-permute-start(bf16[2,8,16,640]{3,2,1,0:T(8,128)(2,1)S(1)} %add_convert_fusion.2), channel_id=1, source_target_pairs={{0,14},{2,0},{4,2},{6,4},{8,6},{10,8},{12,10},{14,12},{1,15},{3,1}... | collective-permute-start | bytes 983048 | tf_op jit(solution)/shard_map/ppermute | solution.py:348
  35.6 4.0 %collective-permute-done.13 = bf16[2,8,16,640]{3,2,1,0:T(8,128)(2,1)S(1)} collective-permute-done((bf16[2,8,16,640]{3,2,1,0:T(8,128)(2,1)S(1)}, bf16[2,8,16,640]{3,2,1,0:T(8,128)(2,1)S(1)}, u32[]{:S(2)}, u32[]{:S(2)}) %collective-permute-start.13) | collective-permute-done | bytes 327712 | tf_op jit(solution)/shard_map/ppermute | solution.py:348
  39.7 3.8 %collective-permute-start.14 = (bf16[2,8,16,640]{3,2,1,0:T(8,128)(2,1)S(1)}, bf16[2,8,16,640]{3,2,1,0:T(8,128)(2,1)S(1)}, u32[]{:S(2)}, u32[]{:S(2)}) collective-permute-start(bf16[2,8,16,640]{3,2,1,0:T(8,128)(2,1)S(1)} %add_convert_fusion.1), channel_id=1, source_target_pairs={{0,14},{2,0},{4,2},{6,4},{8,6},{10,8},{12,10},{14,12},{1,15},{3,1}... | collective-permute-start | bytes 983048 | tf_op jit(solution)/shard_map/ppermute | solution.py:348
  43.5 8.5 %collective-permute-done.came = bf16[40,24,640]{2,1,0:T(8,128)(2,1)S(1)} collective-permute-done((bf16[40,24,640]{2,1,0:T(8,128)(2,1)S(1)}, bf16[40,24,640]{2,1,0:T(8,128)(2,1)S(1)}, u32[]{:S(2)}, u32[]{:S(2)}) %collective-permute-start) | collective-permute-done | bytes 1228832 | tf_op jit(solution)/shard_map/ppermute | solution.py:352
  52.0 3.5 %shard_map.65 = (bf16[8,24,640]{2,1,0:T(8,128)(2,1)S(1)}, bf16[8,24,640]{2,1,0:T(8,128)(2,1)S(1)}, bf16[8,24,640]{2,1,0:T(8,128)(2,1)S(1)}) custom-call(s32[2]{0:T(128)S(1)} %pad_add_fusion._, bf16[2,40,40,640]{3,2,1,0:T(8,128)(2,1)} %here.7, bf16[40,24,640]{2,1,0:T(8,128)(2,1)S(1)} %collective-permute-done.came, bf16[512,320]{1,0:T(8,128)(2,1)S(1)} %get-tuple-element.54.km, ...), custom_call_target="tpu_custom_call" | custom-call | flops 471859200 | bytes 2990080 | tf_op jit(solution)/shard_map/pallas_call | solution.py:44
  55.8 3.1 %collective-permute-start.5 = (bf16[8,24,640]{2,1,0:T(8,128)(2,1)S(1)}, bf16[8,24,640]{2,1,0:T(8,128)(2,1)S(1)}, u32[]{:S(2)}, u32[]{:S(2)}) collective-permute-start(bf16[8,24,640]{2,1,0:T(8,128)(2,1)S(1)} %get-tuple-element.34), channel_id=1, source_target_pairs={{0,14},{2,0},{4,2},{6,4},{8,6},{10,8},{12,10},{14,12},{1,15},{3,1}... | collective-permute-start | bytes 737288 | tf_op jit(solution)/shard_map/ppermute | solution.py:348
  58.9 3.9 %shard_map.64 = (bf16[8,24,640]{2,1,0:T(8,128)(2,1)S(1)}, bf16[8,24,640]{2,1,0:T(8,128)(2,1)S(1)}, bf16[8,24,640]{2,1,0:T(8,128)(2,1)S(1)}, bf16[8,24,640]{2,1,0:T(8,128)(2,1)S(1)}, bf16[8,24,640]{2,1,0:T(8,128)(2,1)S(1)}) custom-call(s32[2]{0:T(128)S(1)} %pad_add_fusion._, bf16[2,40,40,640]{3,2,1,0:T(8,128)(2,1)} %here.7, ...), custom_call_target="tpu_custom_call" | custom-call | flops 786432000 | bytes 2990080 | tf_op jit(solution)/shard_map/pallas_call | solution.py:44
  63.0 7.2 %collective-permute-done.1 = bf16[8,24,640]{2,1,0:T(8,128)(2,1)S(1)} collective-permute-done((bf16[8,24,640]{2,1,0:T(8,128)(2,1)S(1)}, bf16[8,24,640]{2,1,0:T(8,128)(2,1)S(1)}, u32[]{:S(2)}, u32[]{:S(2)}) %collective-permute-start.1) | collective-permute-done | bytes 245792 | tf_op jit(solution)/shard_map/ppermute | solution.py:348
  70.3 6.2 %collective-permute-start.3 = (bf16[8,24,640]{2,1,0:T(8,128)(2,1)S(1)}, bf16[8,24,640]{2,1,0:T(8,128)(2,1)S(1)}, u32[]{:S(2)}, u32[]{:S(2)}) collective-permute-start(bf16[8,24,640]{2,1,0:T(8,128)(2,1)S(1)} %add_convert_fusion.10), channel_id=1, source_target_pairs={{0,2},{2,4},{4,6},{6,8},{8,10},{10,12},{12,14},{14,0},{1,3},{3,5},... | collective-permute-start | bytes 737288 | tf_op jit(solution)/shard_map/ppermute | solution.py:348
  78.4 3.7 %collective-permute-done.3 = bf16[8,24,640]{2,1,0:T(8,128)(2,1)S(1)} collective-permute-done((bf16[8,24,640]{2,1,0:T(8,128)(2,1)S(1)}, bf16[8,24,640]{2,1,0:T(8,128)(2,1)S(1)}, u32[]{:S(2)}, u32[]{:S(2)}) %collective-permute-start.3) | collective-permute-done | bytes 245792 | tf_op jit(solution)/shard_map/ppermute | solution.py:348
  85.6 4.0 %collective-permute-done.4 = bf16[8,24,640]{2,1,0:T(8,128)(2,1)S(1)} collective-permute-done((bf16[8,24,640]{2,1,0:T(8,128)(2,1)S(1)}, bf16[8,24,640]{2,1,0:T(8,128)(2,1)S(1)}, u32[]{:S(2)}, u32[]{:S(2)}) %collective-permute-start.4) | collective-permute-done | bytes 245792 | tf_op jit(solution)/shard_map/ppermute | solution.py:348
  93.0 7.5 %all-to-all-start = ((bf16[16,40,288]{2,1,0:T(8,128)(2,1)}), bf16[16,40,288]{2,1,0:T(8,128)(2,1)S(1)}, u32[]{:S(2)}, u32[]{:S(2)}) async-start(bf16[16,40,288]{2,1,0:T(8,128)(2,1)} %shard_map.68), calls=%async_computation | async-start | bytes 983040 | tf_op jit(solution)/shard_map/all_to_all | solution.py:435
  104.3 4.6 %all-to-all-done = bf16[16,40,288]{2,1,0:T(8,128)(2,1)S(1)} async-done(((bf16[16,40,288]{2,1,0:T(8,128)(2,1)}), bf16[16,40,288]{2,1,0:T(8,128)(2,1)S(1)}, u32[]{:S(2)}, u32[]{:S(2)}) %all-to-all-start) | async-done | bytes 368672 | tf_op jit(solution)/shard_map/all_to_all | solution.py:435
  110.0 14.6 %all_to_all.10.x = bf16[16,40,288]{2,1,0:T(8,128)(2,1)S(1)} all-to-all(bf16[16,40,288]{2,1,0:T(8,128)(2,1)S(1)} %bitcast.33), channel_id=1, replica_groups=mesh['row'=16,'z'=8,'ylo'=2] {'row'}, dimensions={0} | all-to-all | bytes 737280 | tf_op jit(solution)/shard_map/all_to_all | solution.py:437
  125.4 3.2 %collective-permute-start.16 = (bf16[8,24,640]{2,1,0:T(8,128)(2,1)S(1)}, bf16[8,24,640]{2,1,0:T(8,128)(2,1)S(1)}, u32[]{:S(2)}, u32[]{:S(2)}) collective-permute-start(bf16[8,24,640]{2,1,0:T(8,128)(2,1)S(1)} %get-tuple-element.47.refs_6_), channel_id=1, source_target_pairs={{0,14},{2,0},{4,2},{6,4},{8,6},{10,8},{12,10},{14,12},{1,15},{3,1}... | collective-permute-start | bytes 737288 | tf_op jit(solution)/shard_map/ppermute | solution.py:348
  128.6 6.8 %collective-permute-done.19.refs_5_ = bf16[8,24,640]{2,1,0:T(8,128)(2,1)S(1)} collective-permute-done((bf16[8,24,640]{2,1,0:T(8,128)(2,1)S(1)}, bf16[8,24,640]{2,1,0:T(8,128)(2,1)S(1)}, u32[]{:S(2)}, u32[]{:S(2)}) %collective-permute-start.19) | collective-permute-done | bytes 245792 | tf_op jit(solution)/shard_map/ppermute | solution.py:348
  135.3 3.2 %collective-permute-start.17 = (bf16[8,24,640]{2,1,0:T(8,128)(2,1)S(1)}, bf16[8,24,640]{2,1,0:T(8,128)(2,1)S(1)}, u32[]{:S(2)}, u32[]{:S(2)}) collective-permute-start(bf16[8,24,640]{2,1,0:T(8,128)(2,1)S(1)} %collective-permute-done.16.refs_7_), channel_id=1, source_target_pairs={{0,14},{2,0},{4,2},{6,4},{8,6},{10,8},{12,10},{14,12},{1,15},{3,1}... | collective-permute-start | bytes 737288 | tf_op jit(solution)/shard_map/ppermute | solution.py:348
  139.3 5.3 %collective-permute-done.20.refs_4_ = bf16[8,24,640]{2,1,0:T(8,128)(2,1)S(1)} collective-permute-done((bf16[8,24,640]{2,1,0:T(8,128)(2,1)S(1)}, bf16[8,24,640]{2,1,0:T(8,128)(2,1)S(1)}, u32[]{:S(2)}, u32[]{:S(2)}) %collective-permute-start.20) | collective-permute-done | bytes 245792 | tf_op jit(solution)/shard_map/ppermute | solution.py:348
  144.5 3.2 %collective-permute-start.18 = (bf16[8,24,640]{2,1,0:T(8,128)(2,1)S(1)}, bf16[8,24,640]{2,1,0:T(8,128)(2,1)S(1)}, u32[]{:S(2)}, u32[]{:S(2)}) collective-permute-start(bf16[8,24,640]{2,1,0:T(8,128)(2,1)S(1)} %collective-permute-done.17.refs_8_), channel_id=1, source_target_pairs={{0,14},{2,0},{4,2},{6,4},{8,6},{10,8},{12,10},{14,12},{1,15},{3,1}... | collective-permute-start | bytes 737288 | tf_op jit(solution)/shard_map/ppermute | solution.py:348
  147.9 4.2 %collective-permute-start.22 = (bf16[4,24,640]{2,1,0:T(8,128)(2,1)S(1)}, bf16[4,24,640]{2,1,0:T(8,128)(2,1)S(1)}, u32[]{:S(2)}, u32[]{:S(2)}) collective-permute-start(bf16[4,24,640]{2,1,0:T(8,128)(2,1)S(1)} %slice.27), channel_id=1, source_target_pairs={{0,12},{2,14},{4,0},{6,2},{8,4},{10,6},{12,8},{14,10},{1,13},{3,15... | collective-permute-start | bytes 368648 | tf_op jit(solution)/shard_map/ppermute | solution.py:348
  152.2 3.7 %collective-permute-done.21.refs_1_ = bf16[4,24,640]{2,1,0:T(8,128)(2,1)S(1)} collective-permute-done((bf16[4,24,640]{2,1,0:T(8,128)(2,1)S(1)}, bf16[4,24,640]{2,1,0:T(8,128)(2,1)S(1)}, u32[]{:S(2)}, u32[]{:S(2)}) %collective-permute-start.21) | collective-permute-done | bytes 122912 | tf_op jit(solution)/shard_map/ppermute | solution.py:348
  155.9 3.5 %collective-permute-done.22.refs_2_ = bf16[4,24,640]{2,1,0:T(8,128)(2,1)S(1)} collective-permute-done((bf16[4,24,640]{2,1,0:T(8,128)(2,1)S(1)}, bf16[4,24,640]{2,1,0:T(8,128)(2,1)S(1)}, u32[]{:S(2)}, u32[]{:S(2)}) %collective-permute-start.22) | collective-permute-done | bytes 122912 | tf_op jit(solution)/shard_map/ppermute | solution.py:348
  164.4 3.7 %collective-permute-start.27 = (bf16[2,8,16,640]{3,2,1,0:T(8,128)(2,1)S(1)}, bf16[2,8,16,640]{3,2,1,0:T(8,128)(2,1)S(1)}, u32[]{:S(2)}, u32[]{:S(2)}) collective-permute-start(bf16[2,8,16,640]{3,2,1,0:T(8,128)(2,1)S(1)} %collective-permute-done.26.refs_6_), channel_id=1, source_target_pairs={{0,14},{2,0},{4,2},{6,4},{8,6},{10,8},{12,10},{14,12},{1,15},{3,1}... | collective-permute-start | bytes 983048 | tf_op jit(solution)/shard_map/ppermute | solution.py:348
  173.4 3.7 %collective-permute-start.28 = (bf16[2,8,16,640]{3,2,1,0:T(8,128)(2,1)S(1)}, bf16[2,8,16,640]{3,2,1,0:T(8,128)(2,1)S(1)}, u32[]{:S(2)}, u32[]{:S(2)}) collective-permute-start(bf16[2,8,16,640]{3,2,1,0:T(8,128)(2,1)S(1)} %collective-permute-done.27.refs_7_), channel_id=1, source_target_pairs={{0,14},{2,0},{4,2},{6,4},{8,6},{10,8},{12,10},{14,12},{1,15},{3,1}... | collective-permute-start | bytes 983048 | tf_op jit(solution)/shard_map/ppermute | solution.py:348
  177.1 5.5 %collective-permute-done.31.refs_3_ = bf16[2,8,16,640]{3,2,1,0:T(8,128)(2,1)S(1)} collective-permute-done((bf16[2,8,16,640]{3,2,1,0:T(8,128)(2,1)S(1)}, bf16[2,8,16,640]{3,2,1,0:T(8,128)(2,1)S(1)}, u32[]{:S(2)}, u32[]{:S(2)}) %collective-permute-start.31) | collective-permute-done | bytes 327712 | tf_op jit(solution)/shard_map/ppermute | solution.py:348
  182.6 3.2 %collective-permute-start.29 = (bf16[2,8,16,640]{3,2,1,0:T(8,128)(2,1)S(1)}, bf16[2,8,16,640]{3,2,1,0:T(8,128)(2,1)S(1)}, u32[]{:S(2)}, u32[]{:S(2)}) collective-permute-start(bf16[2,8,16,640]{3,2,1,0:T(8,128)(2,1)S(1)} %collective-permute-done.28.refs_0_), channel_id=1, source_target_pairs={{0,14},{2,0},{4,2},{6,4},{8,6},{10,8},{12,10},{14,12},{1,15},{3,1}... | collective-permute-start | bytes 983048 | tf_op jit(solution)/shard_map/ppermute | solution.py:348
  185.8 3.1 %shard_map.72.refs_9_ = bf16[2,40,40,640]{3,2,1,0:T(8,128)(2,1)} custom-call(s32[2]{0:T(128)S(1)} %pad_add_fusion._, bf16[8,24,640]{2,1,0:T(8,128)(2,1)S(1)} %collective-permute-done.18.refs_0_, bf16[4,24,640]{2,1,0:T(8,128)(2,1)S(1)} %collective-permute-done.21.refs_1_, bf16[4,24,640]{2,1,0:T(8,128)(2,1)S(1)} %collective-permute-done.22.refs_2_, ...), custom_call_target="tpu_custom_call" | custom-call | flops 629145600 | bytes 1146880 | tf_op jit(solution)/shard_map/pallas_call | solution.py:44
  (95 shorter events, 42.5 us)
Async XLA Ops:
  7.6 12.9 %collective-permute-start.11 = (bf16[2,8,16,640]{3,2,1,0:T(8,128)(2,1)S(1)}, bf16[2,8,16,640]{3,2,1,0:T(8,128)(2,1)S(1)}, u32[]{:S(2)}, u32[]{:S(2)}) collective-permute-start(bf16[2,8,16,640]{3,2,1,0:T(8,128)(2,1)S(1)} %get-tuple-element.41), channel_id=1, source_target_pairs={{0,14},{2,0},{4,2},{6,4},{8,6},{10,8},{12,10},{14,12},{1,15},{3,1}... | collective-permute-start | bytes 983048 | tf_op jit(solution)/shard_map/ppermute | solution.py:348
  13.6 12.4 %collective-permute-start.8 = (bf16[2,8,16,640]{3,2,1,0:T(8,128)(2,1)S(1)}, bf16[2,8,16,640]{3,2,1,0:T(8,128)(2,1)S(1)}, u32[]{:S(2)}, u32[]{:S(2)}) collective-permute-start(bf16[2,8,16,640]{3,2,1,0:T(8,128)(2,1)S(1)} %get-tuple-element.38), channel_id=1, source_target_pairs={{0,2},{2,4},{4,6},{6,8},{8,10},{10,12},{12,14},{14,0},{1,3},{3,5},... | collective-permute-start | bytes 983048 | tf_op jit(solution)/shard_map/ppermute | solution.py:348
  20.6 9.9 %collective-permute-start.12 = (bf16[2,8,16,640]{3,2,1,0:T(8,128)(2,1)S(1)}, bf16[2,8,16,640]{3,2,1,0:T(8,128)(2,1)S(1)}, u32[]{:S(2)}, u32[]{:S(2)}) collective-permute-start(bf16[2,8,16,640]{3,2,1,0:T(8,128)(2,1)S(1)} %add_convert_fusion.3), channel_id=1, source_target_pairs={{0,14},{2,0},{4,2},{6,4},{8,6},{10,8},{12,10},{14,12},{1,15},{3,1}... | collective-permute-start | bytes 983048 | tf_op jit(solution)/shard_map/ppermute | solution.py:348
  24.4 27.6 %collective-permute-start = (bf16[40,24,640]{2,1,0:T(8,128)(2,1)S(1)}, bf16[40,24,640]{2,1,0:T(8,128)(2,1)S(1)}, u32[]{:S(2)}, u32[]{:S(2)}) collective-permute-start(bf16[40,24,640]{2,1,0:T(8,128)(2,1)S(1)} %lift.1), channel_id=1, source_target_pairs={{0,1},{1,0},{2,3},{3,2},{4,5},{5,4},{6,7},{7,6},{8,9},{9,8},{10,11... | collective-permute-start | bytes 3686408 | tf_op jit(solution)/shard_map/ppermute | solution.py:352
  26.1 9.3 %collective-permute-start.9 = (bf16[2,8,16,640]{3,2,1,0:T(8,128)(2,1)S(1)}, bf16[2,8,16,640]{3,2,1,0:T(8,128)(2,1)S(1)}, u32[]{:S(2)}, u32[]{:S(2)}) collective-permute-start(bf16[2,8,16,640]{3,2,1,0:T(8,128)(2,1)S(1)} %add_convert_fusion.5), channel_id=1, source_target_pairs={{0,2},{2,4},{4,6},{6,8},{8,10},{10,12},{12,14},{14,0},{1,3},{3,5},... | collective-permute-start | bytes 983048 | tf_op jit(solution)/shard_map/ppermute | solution.py:348
  30.6 9.0 %collective-permute-start.13 = (bf16[2,8,16,640]{3,2,1,0:T(8,128)(2,1)S(1)}, bf16[2,8,16,640]{3,2,1,0:T(8,128)(2,1)S(1)}, u32[]{:S(2)}, u32[]{:S(2)}) collective-permute-start(bf16[2,8,16,640]{3,2,1,0:T(8,128)(2,1)S(1)} %add_convert_fusion.2), channel_id=1, source_target_pairs={{0,14},{2,0},{4,2},{6,4},{8,6},{10,8},{12,10},{14,12},{1,15},{3,1}... | collective-permute-start | bytes 983048 | tf_op jit(solution)/shard_map/ppermute | solution.py:348
  35.5 27.4 %collective-permute-start.10 = (bf16[2,8,16,640]{3,2,1,0:T(8,128)(2,1)S(1)}, bf16[2,8,16,640]{3,2,1,0:T(8,128)(2,1)S(1)}, u32[]{:S(2)}, u32[]{:S(2)}) collective-permute-start(bf16[2,8,16,640]{3,2,1,0:T(8,128)(2,1)S(1)} %add_convert_fusion.4), channel_id=1, source_target_pairs={{0,2},{2,4},{4,6},{6,8},{8,10},{10,12},{12,14},{14,0},{1,3},{3,5},... | collective-permute-start | bytes 983048 | tf_op jit(solution)/shard_map/ppermute | solution.py:348
  39.7 23.1 %collective-permute-start.14 = (bf16[2,8,16,640]{3,2,1,0:T(8,128)(2,1)S(1)}, bf16[2,8,16,640]{3,2,1,0:T(8,128)(2,1)S(1)}, u32[]{:S(2)}, u32[]{:S(2)}) collective-permute-start(bf16[2,8,16,640]{3,2,1,0:T(8,128)(2,1)S(1)} %add_convert_fusion.1), channel_id=1, source_target_pairs={{0,14},{2,0},{4,2},{6,4},{8,6},{10,8},{12,10},{14,12},{1,15},{3,1}... | collective-permute-start | bytes 983048 | tf_op jit(solution)/shard_map/ppermute | solution.py:348
  55.6 14.6 %collective-permute-start.1 = (bf16[8,24,640]{2,1,0:T(8,128)(2,1)S(1)}, bf16[8,24,640]{2,1,0:T(8,128)(2,1)S(1)}, u32[]{:S(2)}, u32[]{:S(2)}) collective-permute-start(bf16[8,24,640]{2,1,0:T(8,128)(2,1)S(1)} %get-tuple-element.30), channel_id=1, source_target_pairs={{0,2},{2,4},{4,6},{6,8},{8,10},{10,12},{12,14},{14,0},{1,3},{3,5},... | collective-permute-start | bytes 737288 | tf_op jit(solution)/shard_map/ppermute | solution.py:348
  55.6 14.5 %collective-permute-start.2 = (bf16[8,24,640]{2,1,0:T(8,128)(2,1)S(1)}, bf16[8,24,640]{2,1,0:T(8,128)(2,1)S(1)}, u32[]{:S(2)}, u32[]{:S(2)}) collective-permute-start(bf16[8,24,640]{2,1,0:T(8,128)(2,1)S(1)} %get-tuple-element.32), channel_id=1, source_target_pairs={{0,4},{2,6},{4,8},{6,10},{8,12},{10,14},{12,0},{14,2},{1,5},{3,7},... | collective-permute-start | bytes 737288 | tf_op jit(solution)/shard_map/ppermute | solution.py:348
  55.8 20.8 %collective-permute-start.5 = (bf16[8,24,640]{2,1,0:T(8,128)(2,1)S(1)}, bf16[8,24,640]{2,1,0:T(8,128)(2,1)S(1)}, u32[]{:S(2)}, u32[]{:S(2)}) collective-permute-start(bf16[8,24,640]{2,1,0:T(8,128)(2,1)S(1)} %get-tuple-element.34), channel_id=1, source_target_pairs={{0,14},{2,0},{4,2},{6,4},{8,6},{10,8},{12,10},{14,12},{1,15},{3,1}... | collective-permute-start | bytes 737288 | tf_op jit(solution)/shard_map/ppermute | solution.py:348
  70.3 11.7 %collective-permute-start.3 = (bf16[8,24,640]{2,1,0:T(8,128)(2,1)S(1)}, bf16[8,24,640]{2,1,0:T(8,128)(2,1)S(1)}, u32[]{:S(2)}, u32[]{:S(2)}) collective-permute-start(bf16[8,24,640]{2,1,0:T(8,128)(2,1)S(1)} %add_convert_fusion.10), channel_id=1, source_target_pairs={{0,2},{2,4},{4,6},{6,8},{8,10},{10,12},{12,14},{14,0},{1,3},{3,5},... | collective-permute-start | bytes 737288 | tf_op jit(solution)/shard_map/ppermute | solution.py:348
  76.6 8.3 %collective-permute-start.6 = (bf16[8,24,640]{2,1,0:T(8,128)(2,1)S(1)}, bf16[8,24,640]{2,1,0:T(8,128)(2,1)S(1)}, u32[]{:S(2)}, u32[]{:S(2)}) collective-permute-start(bf16[8,24,640]{2,1,0:T(8,128)(2,1)S(1)} %add_convert_fusion.8), channel_id=1, source_target_pairs={{0,14},{2,0},{4,2},{6,4},{8,6},{10,8},{12,10},{14,12},{1,15},{3,1}... | collective-permute-start | bytes 737288 | tf_op jit(solution)/shard_map/ppermute | solution.py:348
  76.7 8.9 %collective-permute-start.15 = (bf16[8,16,640]{2,1,0:T(8,128)(2,1)S(1)}, bf16[8,16,640]{2,1,0:T(8,128)(2,1)S(1)}, u32[]{:S(2)}, u32[]{:S(2)}) collective-permute-start(bf16[8,16,640]{2,1,0:T(8,128)(2,1)S(1)} %slice_bitcast_fusion), channel_id=1, source_target_pairs={{0,1},{1,0},{2,3},{3,2},{4,5},{5,4},{6,7},{7,6},{8,9},{9,8},{10,11... | collective-permute-start | bytes 491528 | tf_op jit(solution)/shard_map/ppermute | solution.py:352
  93.0 15.9 %all-to-all-start = ((bf16[16,40,288]{2,1,0:T(8,128)(2,1)}), bf16[16,40,288]{2,1,0:T(8,128)(2,1)S(1)}, u32[]{:S(2)}, u32[]{:S(2)}) async-start(bf16[16,40,288]{2,1,0:T(8,128)(2,1)} %shard_map.68), calls=%async_computation | async-start | bytes 983040 | tf_op jit(solution)/shard_map/all_to_all | solution.py:435
  125.3 10.1 %collective-permute-start.19 = (bf16[8,24,640]{2,1,0:T(8,128)(2,1)S(1)}, bf16[8,24,640]{2,1,0:T(8,128)(2,1)S(1)}, u32[]{:S(2)}, u32[]{:S(2)}) collective-permute-start(bf16[8,24,640]{2,1,0:T(8,128)(2,1)S(1)} %get-tuple-element.47.refs_6_), channel_id=1, source_target_pairs={{0,2},{2,4},{4,6},{6,8},{8,10},{10,12},{12,14},{14,0},{1,3},{3,5},... | collective-permute-start | bytes 737288 | tf_op jit(solution)/shard_map/ppermute | solution.py:348
  125.4 10.0 %collective-permute-start.16 = (bf16[8,24,640]{2,1,0:T(8,128)(2,1)S(1)}, bf16[8,24,640]{2,1,0:T(8,128)(2,1)S(1)}, u32[]{:S(2)}, u32[]{:S(2)}) collective-permute-start(bf16[8,24,640]{2,1,0:T(8,128)(2,1)S(1)} %get-tuple-element.47.refs_6_), channel_id=1, source_target_pairs={{0,14},{2,0},{4,2},{6,4},{8,6},{10,8},{12,10},{14,12},{1,15},{3,1}... | collective-permute-start | bytes 737288 | tf_op jit(solution)/shard_map/ppermute | solution.py:348
  135.3 9.2 %collective-permute-start.20 = (bf16[8,24,640]{2,1,0:T(8,128)(2,1)S(1)}, bf16[8,24,640]{2,1,0:T(8,128)(2,1)S(1)}, u32[]{:S(2)}, u32[]{:S(2)}) collective-permute-start(bf16[8,24,640]{2,1,0:T(8,128)(2,1)S(1)} %collective-permute-done.19.refs_5_), channel_id=1, source_target_pairs={{0,2},{2,4},{4,6},{6,8},{8,10},{10,12},{12,14},{14,0},{1,3},{3,5},... | collective-permute-start | bytes 737288 | tf_op jit(solution)/shard_map/ppermute | solution.py:348
  135.3 9.2 %collective-permute-start.17 = (bf16[8,24,640]{2,1,0:T(8,128)(2,1)S(1)}, bf16[8,24,640]{2,1,0:T(8,128)(2,1)S(1)}, u32[]{:S(2)}, u32[]{:S(2)}) collective-permute-start(bf16[8,24,640]{2,1,0:T(8,128)(2,1)S(1)} %collective-permute-done.16.refs_7_), channel_id=1, source_target_pairs={{0,14},{2,0},{4,2},{6,4},{8,6},{10,8},{12,10},{14,12},{1,15},{3,1}... | collective-permute-start | bytes 737288 | tf_op jit(solution)/shard_map/ppermute | solution.py:348
  138.6 13.5 %collective-permute-start.25 = (bf16[8,16,640]{2,1,0:T(8,128)(2,1)S(1)}, bf16[8,16,640]{2,1,0:T(8,128)(2,1)S(1)}, u32[]{:S(2)}, u32[]{:S(2)}) collective-permute-start(bf16[8,16,640]{2,1,0:T(8,128)(2,1)S(1)} %get-tuple-element.48), channel_id=1, source_target_pairs={{0,1},{1,0},{2,3},{3,2},{4,5},{5,4},{6,7},{7,6},{8,9},{9,8},{10,11... | collective-permute-start | bytes 491528 | tf_op jit(solution)/shard_map/ppermute | solution.py:352
  144.5 14.9 %collective-permute-start.23 = (bf16[8,24,640]{2,1,0:T(8,128)(2,1)S(1)}, bf16[8,24,640]{2,1,0:T(8,128)(2,1)S(1)}, u32[]{:S(2)}, u32[]{:S(2)}) collective-permute-start(bf16[8,24,640]{2,1,0:T(8,128)(2,1)S(1)} %collective-permute-done.20.refs_4_), channel_id=1, source_target_pairs={{0,2},{2,4},{4,6},{6,8},{8,10},{10,12},{12,14},{14,0},{1,3},{3,5},... | collective-permute-start | bytes 737288 | tf_op jit(solution)/shard_map/ppermute | solution.py:348
  144.5 14.9 %collective-permute-start.18 = (bf16[8,24,640]{2,1,0:T(8,128)(2,1)S(1)}, bf16[8,24,640]{2,1,0:T(8,128)(2,1)S(1)}, u32[]{:S(2)}, u32[]{:S(2)}) collective-permute-start(bf16[8,24,640]{2,1,0:T(8,128)(2,1)S(1)} %collective-permute-done.17.refs_8_), channel_id=1, source_target_pairs={{0,14},{2,0},{4,2},{6,4},{8,6},{10,8},{12,10},{14,12},{1,15},{3,1}... | collective-permute-start | bytes 737288 | tf_op jit(solution)/shard_map/ppermute | solution.py:348
  147.8 8.1 %collective-permute-start.21 = (bf16[4,24,640]{2,1,0:T(8,128)(2,1)S(1)}, bf16[4,24,640]{2,1,0:T(8,128)(2,1)S(1)}, u32[]{:S(2)}, u32[]{:S(2)}) collective-permute-start(bf16[4,24,640]{2,1,0:T(8,128)(2,1)S(1)} %slice.26), channel_id=1, source_target_pairs={{0,4},{2,6},{4,8},{6,10},{8,12},{10,14},{12,0},{14,2},{1,5},{3,7},... | collective-permute-start | bytes 368648 | tf_op jit(solution)/shard_map/ppermute | solution.py:348
  147.9 11.5 %collective-permute-start.22 = (bf16[4,24,640]{2,1,0:T(8,128)(2,1)S(1)}, bf16[4,24,640]{2,1,0:T(8,128)(2,1)S(1)}, u32[]{:S(2)}, u32[]{:S(2)}) collective-permute-start(bf16[4,24,640]{2,1,0:T(8,128)(2,1)S(1)} %slice.27), channel_id=1, source_target_pairs={{0,12},{2,14},{4,0},{6,2},{8,4},{10,6},{12,8},{14,10},{1,13},{3,15... | collective-permute-start | bytes 368648 | tf_op jit(solution)/shard_map/ppermute | solution.py:348
  152.1 12.3 %collective-permute-start.26 = (bf16[2,8,16,640]{3,2,1,0:T(8,128)(2,1)S(1)}, bf16[2,8,16,640]{3,2,1,0:T(8,128)(2,1)S(1)}, u32[]{:S(2)}, u32[]{:S(2)}) collective-permute-start(bf16[2,8,16,640]{3,2,1,0:T(8,128)(2,1)S(1)} %pad_maximum_fusion.1.refs_5_), channel_id=1, source_target_pairs={{0,14},{2,0},{4,2},{6,4},{8,6},{10,8},{12,10},{14,12},{1,15},{3,1}... | collective-permute-start | bytes 983048 | tf_op jit(solution)/shard_map/ppermute | solution.py:348
  161.0 32.5 %collective-permute-start.24 = (bf16[40,24,640]{2,1,0:T(8,128)(2,1)S(1)}, bf16[40,24,640]{2,1,0:T(8,128)(2,1)S(1)}, u32[]{:S(2)}, u32[]{:S(2)}) collective-permute-start(bf16[40,24,640]{2,1,0:T(8,128)(2,1)S(1)} %shard_map.71), channel_id=1, source_target_pairs={{0,1},{1,0},{2,3},{3,2},{4,5},{5,4},{6,7},{7,6},{8,9},{9,8},{10,11... | collective-permute-start | bytes 3686408 | tf_op jit(solution)/shard_map/ppermute | solution.py:352
  161.8 8.6 %collective-permute-start.30 = (bf16[2,8,16,640]{3,2,1,0:T(8,128)(2,1)S(1)}, bf16[2,8,16,640]{3,2,1,0:T(8,128)(2,1)S(1)}, u32[]{:S(2)}, u32[]{:S(2)}) collective-permute-start(bf16[2,8,16,640]{3,2,1,0:T(8,128)(2,1)S(1)} %pad_maximum_fusion.1.refs_5_), channel_id=1, source_target_pairs={{0,2},{2,4},{4,6},{6,8},{8,10},{10,12},{12,14},{14,0},{1,3},{3,5},... | collective-permute-start | bytes 983048 | tf_op jit(solution)/shard_map/ppermute | solution.py:348
  164.4 8.9 %collective-permute-start.27 = (bf16[2,8,16,640]{3,2,1,0:T(8,128)(2,1)S(1)}, bf16[2,8,16,640]{3,2,1,0:T(8,128)(2,1)S(1)}, u32[]{:S(2)}, u32[]{:S(2)}) collective-permute-start(bf16[2,8,16,640]{3,2,1,0:T(8,128)(2,1)S(1)} %collective-permute-done.26.refs_6_), channel_id=1, source_target_pairs={{0,14},{2,0},{4,2},{6,4},{8,6},{10,8},{12,10},{14,12},{1,15},{3,1}... | collective-permute-start | bytes 983048 | tf_op jit(solution)/shard_map/ppermute | solution.py:348
  170.4 12.2 %collective-permute-start.31 = (bf16[2,8,16,640]{3,2,1,0:T(8,128)(2,1)S(1)}, bf16[2,8,16,640]{3,2,1,0:T(8,128)(2,1)S(1)}, u32[]{:S(2)}, u32[]{:S(2)}) collective-permute-start(bf16[2,8,16,640]{3,2,1,0:T(8,128)(2,1)S(1)} %collective-permute-done.30.refs_4_), channel_id=1, source_target_pairs={{0,2},{2,4},{4,6},{6,8},{8,10},{10,12},{12,14},{14,0},{1,3},{3,5},... | collective-permute-start | bytes 983048 | tf_op jit(solution)/shard_map/ppermute | solution.py:348
  173.4 9.2 %collective-permute-start.28 = (bf16[2,8,16,640]{3,2,1,0:T(8,128)(2,1)S(1)}, bf16[2,8,16,640]{3,2,1,0:T(8,128)(2,1)S(1)}, u32[]{:S(2)}, u32[]{:S(2)}) collective-permute-start(bf16[2,8,16,640]{3,2,1,0:T(8,128)(2,1)S(1)} %collective-permute-done.27.refs_7_), channel_id=1, source_target_pairs={{0,14},{2,0},{4,2},{6,4},{8,6},{10,8},{12,10},{14,12},{1,15},{3,1}... | collective-permute-start | bytes 983048 | tf_op jit(solution)/shard_map/ppermute | solution.py:348
  182.6 8.3 %collective-permute-start.32 = (bf16[2,8,16,640]{3,2,1,0:T(8,128)(2,1)S(1)}, bf16[2,8,16,640]{3,2,1,0:T(8,128)(2,1)S(1)}, u32[]{:S(2)}, u32[]{:S(2)}) collective-permute-start(bf16[2,8,16,640]{3,2,1,0:T(8,128)(2,1)S(1)} %collective-permute-done.31.refs_3_), channel_id=1, source_target_pairs={{0,2},{2,4},{4,6},{6,8},{8,10},{10,12},{12,14},{14,0},{1,3},{3,5},... | collective-permute-start | bytes 983048 | tf_op jit(solution)/shard_map/ppermute | solution.py:348
  182.6 8.3 %collective-permute-start.29 = (bf16[2,8,16,640]{3,2,1,0:T(8,128)(2,1)S(1)}, bf16[2,8,16,640]{3,2,1,0:T(8,128)(2,1)S(1)}, u32[]{:S(2)}, u32[]{:S(2)}) collective-permute-start(bf16[2,8,16,640]{3,2,1,0:T(8,128)(2,1)S(1)} %collective-permute-done.28.refs_0_), channel_id=1, source_target_pairs={{0,14},{2,0},{4,2},{6,4},{8,6},{10,8},{12,10},{14,12},{1,15},{3,1}... | collective-permute-start | bytes 983048 | tf_op jit(solution)/shard_map/ppermute | solution.py:348
  (7 other events, 136.2 us)
